TPU v7x, 32 devices: a whole 2x2x4 slice. The times are simulated.
32 devices in a mesh: row: 16 (over z, x, core), col: 2 (over y).
Axes of the slice: x: 2, y: 2, z: 4, core: 2. Of those that a mesh axis runs over, the one named last changes fastest.
Arguments:
- matrix_panel: bfloat16 [128, 131072], P('col', 'row'), may hold values from -6 to 6
- row_signs: int32 [131072], P('row'), may hold values from -1 to 1, as said below
- sample_rows: int32 [2048], replicated, may hold values from 0 to 131071, as said below
Outputs:
- sketch: float32 [128, 2048], P('col', 'row')
- gram: float32 [128, 128], P('col')
Inputs may be any that keep to these rules, and one draw needn't show every extreme that they name: `row_signs`: each entry is -1 or +1. `sample_rows`: strictly increasing, so all distinct.
All inputs are finite; a program needn't handle non-finite values.
Results may differ from a plain program's by a relative error of at most 0.0003.
Values sent between devices are 32-bit elements; how exact they have to be, the bound alone decides.
No kernel may reach another device: no remote copies, remote signals or barrier semaphores. Data moves between devices by JAX's collectives and lax.ppermute only.
A program may use at most 64 MiB of HBM per device.

v0:
```python
import jax
import jax.numpy as jnp
from jax import lax
from jax.sharding import PartitionSpec as P


def parity_sign(left, right, bit_count):
    common = jnp.bitwise_and(left, right)
    total = jnp.zeros_like(common)
    for bit_index in range(bit_count):
        total = total + jnp.bitwise_and(jnp.right_shift(common, bit_index), 1)
    return (1 - 2 * jnp.bitwise_and(total, 1)).astype(jnp.float32)


def hadamard(order_size):
    bit_count = order_size.bit_length() - 1
    row_index = jnp.arange(order_size, dtype=jnp.int32)
    return parity_sign(row_index[:, None], row_index[None, :], bit_count)


def local_mix(block, signs):
    columns, length = block.shape
    first_size = min(length, 256)
    second_size = length // first_size
    values = block.astype(jnp.float32) * signs.astype(jnp.float32)[None, :]
    values = values.reshape(columns, first_size, second_size)
    values = jnp.einsum(
        "cab,ad->cdb", values, hadamard(first_size), precision=lax.Precision.HIGHEST
    )
    values = jnp.einsum(
        "cdb,be->cde", values, hadamard(second_size), precision=lax.Precision.HIGHEST
    )
    return values.reshape(columns, length) / jnp.sqrt(jnp.float32(length))


def body(matrix_panel, row_signs, sample_rows):
    devices = lax.axis_size("row")
    position = lax.axis_index("row")
    bit_count = devices.bit_length() - 1
    columns, length = matrix_panel.shape
    everything = sample_rows.shape[0]
    per_device = everything // devices
    mixed = local_mix(matrix_panel, row_signs)
    owner = sample_rows // length
    offset = sample_rows - owner * length
    chosen = jnp.take(mixed, offset, axis=1)
    pieces = chosen.reshape(columns, devices, per_device)
    received = lax.all_to_all(pieces, "row", split_axis=1, concat_axis=1, tiled=True)
    mine = lax.dynamic_slice_in_dim(owner, position * per_device, per_device, 0)
    sources = jnp.arange(devices, dtype=jnp.int32)
    table = parity_sign(sources[:, None], mine[None, :], bit_count)
    summed = jnp.sum(received * table[None, :, :], axis=1)
    sketch = summed / jnp.sqrt(jnp.float32(devices))
    gathered = lax.all_gather(sketch, "col", axis=0, tiled=True)
    partial_gram = jnp.dot(gathered, gathered.T, precision=lax.Precision.HIGHEST)
    totals = lax.psum(partial_gram, "row")
    own_rows = lax.dynamic_slice_in_dim(totals, lax.axis_index("col") * columns, columns, 0)
    gram = own_rows / everything
    return (sketch, gram)


def solution(mesh):
    return jax.shard_map(
        body,
        mesh=mesh,
        in_specs=(P("col", "row"), P("row"), P()),
        out_specs=(P("col", "row"), P("col", None)),
        check_vma=False,
    )
```

profile of v0, /device:TPU:0, one launch (start us, length us, event | category | flops | bytes accessed | tf_op | source)
XLA Modules:
  0.0 156.9 jit_solution(18320951381184153002)
XLA Ops:
  7.2 0.7 add_select_fusion
  7.9 0.7 and_bitcast_fusion
  8.6 0.8 convert_element_type.21
  9.4 1.4 convert_multiply_fusion
  10.8 2.7 %copy.13 = f32[64,8192]{0,1:T(8,128)} copy(f32[64,8192]{1,0:T(8,128)S(1)} %convert_multiply_fusion) | data formatting | bytes 4194304 | tf_op jit(solution)/shard_map/mul | solution.py:25
  13.5 4.5 %copy.14 = f32[64,256,32]{1,2,0:T(8,128)S(1)} copy(f32[64,256,32]{0,2,1:T(8,128)} %bitcast.21) | data formatting | bytes 4194304 | tf_op jit(solution)/shard_map/reshape | solution.py:26
  17.9 2.2 %fusion = f32[256,2048]{0,1:S(1)} fusion(f32[256,2048]{0,1:T(8,128)S(1)} %bitcast.22), kind=kOutput, calls=%fused_computation.5 | convolution fusion | flops 1612447744 | bytes 4194304
  20.1 1.9 %convolution_multiply_fusion = f32[64,256,32]{1,2,0:T(8,128)S(1)} fusion(f32[64,256,32]{1,2,0:T(8,128)S(1)} %bitcast.23), kind=kOutput, calls=%fused_computation.2 | convolution fusion | flops 201870336 | bytes 4194304 | tf_op jit(solution)/shard_map/cdb,be->cde/dot_general | solution.py:30
  22.0 4.5 %copy.15 = f32[64,256,32]{0,2,1:T(8,128)} copy(f32[64,256,32]{1,2,0:T(8,128)S(1)} %convolution_multiply_fusion) | data formatting | bytes 4194304 | tf_op jit(solution)/shard_map/div | solution.py:33
  26.5 7.6 %gather_fusion = f32[2048,64]{1,0:T(8,128)S(1)} fusion(f32[64,8192]{0,1:T(8,128)} %bitcast.20, s32[2048]{0:T(1024)S(1)} %get-tuple-element.7), kind=kCustom, calls=%fused_computation | custom fusion | bytes 1056768 | tf_op jit(solution)/shard_map/jit(_take)/gather | solution.py:46
  34.2 0.3 copy.16
  34.5 0.8 broadcast_select_fusion
  35.3 7.4 %all-to-all-start = ((f32[64,16,128]{2,0,1:T(8,128)}), f32[64,16,128]{2,0,1:T(8,128)S(1)}, u32[]{:S(2)}, u32[]{:S(2)}) async-start(f32[64,16,128]{2,0,1:T(8,128)} %broadcast_select_fusion), calls=%async_computation | async-start | bytes 1048576 | tf_op jit(solution)/shard_map/all_to_all | solution.py:48
  42.7 0.0 all-reduce.2.cloned.1.call-start
  42.8 0.1 dynamic_slice.6
  42.9 14.1 %all-to-all-done = f32[64,16,128]{2,0,1:T(8,128)S(1)} async-done(((f32[64,16,128]{2,0,1:T(8,128)}), f32[64,16,128]{2,0,1:T(8,128)S(1)}, u32[]{:S(2)}, u32[]{:S(2)}) %all-to-all-start) | async-done | bytes 524320 | tf_op jit(solution)/shard_map/all_to_all | solution.py:48
  57.0 0.1 copy.20
  57.2 0.1 copy.19
  57.2 0.0 copy-start
  57.2 4.6 %all_gather.3 = f32[128,128]{1,0:T(8,128)S(1)} all-gather(f32[64,128]{1,0:T(8,128)S(1)} %copy.19), channel_id=1, replica_groups=mesh['row'=16,'col'=2] {'col'}, dimensions={0}, use_global_device_ids=true | all-gather | bytes 98304 | tf_op jit(solution)/shard_map/all_gather | solution.py:54
  61.8 0.9 fusion.81
  62.7 0.0 all-reduce.2.cloned.1.call-update
  62.7 86.0 %all-reduce.2.cloned.1.call-done = f32[128,128]{1,0:T(8,128)} async-done(((f32[128,128]{1,0:T(8,128)}), f32[128,128]{1,0:T(8,128)}) %all-reduce.2.cloned.1.call-update) | async-done | bytes 65552 | tf_op jit(solution)/shard_map/psum | solution.py:56
  148.7 1.4 dynamic-slice_multiply_fusion
  150.1 0.0 copy-done
  (3 shorter events, 0.1 us)
Async XLA Ops:
  35.3 21.7 %all-to-all-start = ((f32[64,16,128]{2,0,1:T(8,128)}), f32[64,16,128]{2,0,1:T(8,128)S(1)}, u32[]{:S(2)}, u32[]{:S(2)}) async-start(f32[64,16,128]{2,0,1:T(8,128)} %broadcast_select_fusion), calls=%async_computation | async-start | bytes 1048576 | tf_op jit(solution)/shard_map/all_to_all | solution.py:48
  42.7 106.0 %all-reduce.2.cloned.1.call-start = ((), (), s32[]{:S(2)}) async-start(), calls=%async_computation.1 | async-start | bytes 131072 | tf_op jit(solution)/shard_map/psum | solution.py:56
  57.2 92.9 %copy-start = (f32[64,128]{1,0:T(8,128)}, f32[64,128]{1,0:T(8,128)S(1)}, u32[]{:S(2)}) copy-start(f32[64,128]{1,0:T(8,128)S(1)} %copy.19) | copy-start | bytes 98308
Sparse Core Ops, SparseCore 0:
  62.9 85.8 all-reduce.1
where the time goes:
time: 158 us; the launch traced here: 157 us
  waiting for transfers between devices  100 us (63%)
  local copies, waits for them, and re-layouts  19.9 us (13%)
  between operations  14.1 us (9%)
  starting transfers between devices  7.42 us (5%)
  other arithmetic  5.87 us (4%)
  matrix products  4.98 us (3%)
  blocking collectives  4.58 us (3%)
    psum x1, waiting for transfers between devices, body(): totals = lax.psum(partial_gram, 'row')  86 us
    all_to_all x1, waiting for transfers between devices, body(): lax.all_to_all(pieces, 'row', split_axis=1, concat_axis=1, tiled=True)  14.1 us
    gather x2, local copies, waits for them, and re-layouts, body(): chosen = jnp.take(mixed, offset, axis=1)  7.96 us
    all_to_all x1, starting transfers between devices, body(): lax.all_to_all(pieces, 'row', split_axis=1, concat_axis=1, tiled=True)  7.38 us
    all_gather x1, blocking collectives, body(): gathered = lax.all_gather(sketch, 'col', axis=0, tiled=True)  4.58 us
    div x1, local copies, waits for them, and re-layouts, local_mix(): return values.reshape(columns, length) / jnp.sqrt(jnp.float32(length))  4.48 us
    reshape x1, local copies, waits for them, and re-layouts, local_mix(): values = values.reshape(columns, first_size, second_size)  4.46 us
  transfers between devices with their start and end apart: 2, of which 2 were waited for; matrix products, arithmetic and copies ran while one was open for 0% of the time, Pallas kernels for 0%

commit v1 on v0

v1 whole, which is shorter than its diff:
```python
import jax
import jax.numpy as jnp
import numpy as np
from jax import lax
from jax.experimental import pallas as pl
from jax.experimental.pallas import tpu as pltpu
from jax.sharding import PartitionSpec as P

WIDE = 256
LANES = 128


def parity(value, bits):
    total = jnp.zeros_like(value)
    for k in range(bits):
        total = total ^ (value >> k)
    return total & 1


def mix_kernel(devices, scale, x_hbm, s_ref, rows_smem, rows_ref, keep_ref, send_ref,
               x_ref, t_ref, g_ref, sems):
    columns, length = x_ref.shape
    blocks = length // WIDE
    slabs = blocks // 2
    per = rows_ref.shape[1]
    bits = devices.bit_length() - 1
    groups = slabs // 2
    span = 2 * WIDE
    half = length // 2
    copies = []
    for g in range(groups):
        for h in range(2):
            window = pl.ds(h * half + g * span, span)
            copies.append(pltpu.make_async_copy(x_hbm.at[:, window], x_ref.at[:, window], sems.at[g, h]))
            copies[-1].start()
    left = lax.broadcasted_iota(jnp.int32, (WIDE, WIDE), 0)
    right = lax.broadcasted_iota(jnp.int32, (WIDE, WIDE), 1)
    mat = (1 - 2 * parity(left & right, WIDE.bit_length() - 1)).astype(jnp.float32).astype(jnp.bfloat16)
    for g in range(groups):
        copies[2 * g].wait()
        copies[2 * g + 1].wait()
        parts = []
        for q in range(2):
            for h in range(2):
                block = h * slabs + 2 * g + q
                signs = jnp.concatenate([s_ref[2 * block:2 * block + 1, :], s_ref[2 * block + 1:2 * block + 2, :]], axis=1)
                parts.append(x_ref[:, block * WIDE:(block + 1) * WIDE] * signs.astype(jnp.float32).astype(jnp.bfloat16))
        stacked = jnp.concatenate(parts, axis=0)
        out = lax.dot_general(mat, stacked, (((1,), (1,)), ((), ())), preferred_element_type=jnp.float32)
        one, two = out[:, :LANES], out[:, LANES:]
        t_ref[(2 * g) * WIDE:(2 * g + 1) * WIDE, :] = one + two
        t_ref[(2 * g + 1) * WIDE:(2 * g + 2) * WIDE, :] = one - two

    def butterfly(i, _):
        for q in range(2):
            at = [pl.ds(pl.multiple_of((2 * g + q) * WIDE + i * 8, 8), 8) for g in range(groups)]
            v = [t_ref[a, :] for a in at]
            step = 1
            while step < groups:
                for j in range(groups):
                    if not j & step:
                        v[j], v[j + step] = v[j] + v[j + step], v[j] - v[j + step]
                step *= 2
            for a, value in zip(at, v):
                t_ref[a, :] = value
        return 0

    lax.fori_loop(0, WIDE // 8, butterfly, 0, unroll=4)

    me = lax.axis_index("row")
    top = length.bit_length() - 2
    for out_ref, base in ((send_ref, devices // 2), (keep_ref, 0)):
        def gather(i, _, out_ref=out_ref, base=base):
            p = base + i
            dest = me
            for k in range(bits):
                dest = dest ^ (((p >> k) & 1) << (bits - 1 - k))
            for t in range(per):
                row = rows_smem[dest * per + t] & (half - 1)
                g_ref[t:t + 1, :] = t_ref[pl.ds(row, 1), :]
            turned = g_ref[...].T
            samples = rows_ref[pl.ds(dest, 1), :]
            flip = parity((samples >> (top + 1)) & me, bits)
            first = jnp.where(flip == 1, -scale, scale)
            second = jnp.where((flip ^ ((samples >> top) & 1)) == 1, -scale, scale)
            out_ref[i] = turned[:columns, :] * first + turned[columns:, :] * second
            return 0
        lax.fori_loop(0, devices // 2, gather, 0)


def mix(matrix_panel, row_signs, sample_rows, devices):
    columns, length = matrix_panel.shape
    per = sample_rows.shape[0] // devices
    scale = float(1.0 / np.sqrt(float(length) * devices))
    vmem = pl.BlockSpec(memory_space=pltpu.VMEM)
    smem = pl.BlockSpec(memory_space=pltpu.SMEM)
    piece = jax.ShapeDtypeStruct((devices // 2, columns, per), jnp.float32)
    return pl.pallas_call(
        lambda *refs: mix_kernel(devices, scale, *refs),
        out_shape=(piece, piece),
        in_specs=[pl.BlockSpec(memory_space=pl.ANY), vmem, smem, vmem],
        out_specs=(vmem, vmem),
        scratch_shapes=[
            pltpu.VMEM((columns, length), jnp.bfloat16),
            pltpu.VMEM((length // 2, LANES), jnp.float32),
            pltpu.VMEM((per, LANES), jnp.float32),
            pltpu.SemaphoreType.DMA((length // WIDE // 4, 2)),
        ],
    )(matrix_panel, row_signs.reshape(length // LANES, LANES), sample_rows, sample_rows.reshape(devices, per))


def flip(value, axis, bit):
    size = lax.axis_size(axis)
    return lax.ppermute(value, axis, [(i, i ^ bit) for i in range(size)])


def body(matrix_panel, row_signs, sample_rows):
    devices = lax.axis_size("row")
    columns, length = matrix_panel.shape
    everything = sample_rows.shape[0]
    per = everything // devices
    bits = devices.bit_length() - 1
    keep, send = mix(matrix_panel, row_signs, sample_rows, devices)
    for k in range(bits):
        total = keep + flip(send, "row", 1 << k)
        if k < bits - 1:
            half = total.shape[0] // 2
            keep, send = total[:half], total[half:]
    sketch = total[0]
    other = flip(sketch, "col", 1)
    own = jnp.dot(sketch, sketch.T, precision=lax.Precision.HIGHEST)
    cross = jnp.dot(sketch, other.T, precision=lax.Precision.HIGHEST)
    first = lax.axis_index("col") == 0
    gram = jnp.concatenate([jnp.where(first, own, cross), jnp.where(first, cross, own)], axis=1)
    gram = gram / everything
    for k in range(bits):
        gram = gram + flip(gram, "row", 1 << k)
    return (sketch, gram)


def solution(mesh):
    return jax.shard_map(
        body,
        mesh=mesh,
        in_specs=(P("col", "row"), P("row"), P()),
        out_specs=(P("col", "row"), P("col", None)),
        check_vma=False,
    )
```

time: 158 us -> 47.5 us (0.30)
  waiting for transfers between devices: 100 us -> 19.1 us
  local copies, waits for them, and re-layouts: 19.9 us -> 0.02 us
  between operations: 14.1 us -> 0.71 us
  starting transfers between devices: 7.42 us -> 16.5 us
  Pallas kernels: 0 us -> 8.59 us
  matrix products: 4.98 us -> 0.36 us
  blocking collectives: 4.58 us -> 0 us
  other arithmetic: 5.87 us -> 1.81 us
    psum x1 -> x0, waiting for transfers between devices: 86 us -> none  [body(): totals = lax.psum(partial_gram, 'row')]
    ppermute x0 -> x9, waiting for transfers between devices: none -> 19.1 us  [flip(): return lax.ppermute(value, axis, [(i, i ^ bit) for i in range(size)])]
    ppermute x0 -> x9, starting transfers between devices: none -> 16.5 us  [flip(): return lax.ppermute(value, axis, [(i, i ^ bit) for i in range(size)])]
    all_to_all x1 -> x0, waiting for transfers between devices: 14.1 us -> none  [body(): lax.all_to_all(pieces, 'row', split_axis=1, concat_axis=1, tiled=True)]
    pallas_call x0 -> x1, Pallas kernels: none -> 8.59 us  [mix(): pl.pallas_call(lambda *refs: mix_kernel(devices, scale, *refs), out_shape...]
    gather x2 -> x0, local copies, waits for them, and re-layouts: 7.96 us -> none  [body(): chosen = jnp.take(mixed, offset, axis=1)]
    all_to_all x1 -> x0, starting transfers between devices: 7.38 us -> none  [body(): lax.all_to_all(pieces, 'row', split_axis=1, concat_axis=1, tiled=True)]
    all_gather x1 -> x0, blocking collectives: 4.58 us -> none  [body(): gathered = lax.all_gather(sketch, 'col', axis=0, tiled=True)]
  transfers between devices with their start and end apart: 2 -> 9, of which waited for: 2 -> 9; matrix products, arithmetic and copies ran while one was open for 0% -> 0% of each run, Pallas kernels for 0% -> 0%
where the time goes in v1:
time: 47.5 us; the launch traced here: 47.2 us
  waiting for transfers between devices  19.1 us (40%)
  starting transfers between devices  16.5 us (35%)
  Pallas kernels  8.59 us (18%)
  other arithmetic  1.81 us (4%)
  between operations  0.71 us (1%)
    ppermute x9, waiting for transfers between devices, flip(): return lax.ppermute(value, axis, [(i, i ^ bit) for i in range(size)])  19.1 us
    ppermute x9, starting transfers between devices, flip(): return lax.ppermute(value, axis, [(i, i ^ bit) for i in range(size)])  16.5 us
    pallas_call x1, Pallas kernels, mix(): pl.pallas_call(lambda *refs: mix_kernel(devices, scale, *refs), out_shape...  8.59 us
    add x3, other arithmetic, body(): total = keep + flip(send, 'row', 1 << k)  1.02 us
  transfers between devices with their start and end apart: 9, of which 9 were waited for; matrix products, arithmetic and copies ran while one was open for 0% of the time, Pallas kernels for 0%

profile of v1, /device:TPU:0, one launch (start us, length us, event | category | flops | bytes accessed | tf_op | source)
XLA Modules:
  0.0 47.2 jit_solution(127149743070740608)
XLA Ops:
  0.6 8.6 %shard_map.50 = (f32[8,64,128]{2,1,0:T(8,128)}, f32[8,64,128]{2,1,0:T(8,128)}) custom-call(bf16[64,8192]{1,0:T(8,128)(2,1)} %refs_0_.1, s32[64,128]{1,0:T(8,128)} %bitcast.9, s32[2048]{0:T(1024)} %refs_2_.1, s32[16,128]{1,0:T(8,128)} %bitcast.8), custom_call_target="tpu_custom_call" | custom-call | tf_op jit(solution)/shard_map/pallas_call | solution.py:98
  9.2 0.6 %collective-permute-start = (f32[8,64,128]{2,1,0:T(8,128)}, f32[8,64,128]{2,1,0:T(8,128)S(1)}, u32[]{:S(2)}, u32[]{:S(2)}) collective-permute-start(f32[8,64,128]{2,1,0:T(8,128)} %get-tuple-element.5), channel_id=1, source_target_pairs={{0,2},{2,0},{4,6},{6,4},{8,10},{10,8},{12,14},{14,12},{16,18},{18,... | collective-permute-start | bytes 786440 | tf_op jit(solution)/shard_map/ppermute | solution.py:114
  9.8 1.4 %collective-permute-done = f32[8,64,128]{2,1,0:T(8,128)S(1)} collective-permute-done((f32[8,64,128]{2,1,0:T(8,128)}, f32[8,64,128]{2,1,0:T(8,128)S(1)}, u32[]{:S(2)}, u32[]{:S(2)}) %collective-permute-start) | collective-permute-done | bytes 262176 | tf_op jit(solution)/shard_map/ppermute | solution.py:114
  11.2 1.0 %add.24 = f32[8,64,128]{2,1,0:T(8,128)S(1)} add(f32[8,64,128]{2,1,0:T(8,128)} %get-tuple-element.4, f32[8,64,128]{2,1,0:T(8,128)S(1)} %collective-permute-done) | non-fusion elementwise | flops 65536 | bytes 786432 | tf_op jit(solution)/shard_map/add | solution.py:125
  12.2 2.9 %collective-permute-start.1 = (f32[4,64,128]{2,1,0:T(8,128)S(1)}, f32[4,64,128]{2,1,0:T(8,128)S(1)}, u32[]{:S(2)}, u32[]{:S(2)}) collective-permute-start(f32[4,64,128]{2,1,0:T(8,128)S(1)} %slice.25), channel_id=1, source_target_pairs={{0,4},{2,6},{4,0},{6,2},{8,12},{10,14},{12,8},{14,10},{16,20},{18,... | collective-permute-start | bytes 393224 | tf_op jit(solution)/shard_map/ppermute | solution.py:114
  15.1 3.8 %collective-permute-done.1 = f32[4,64,128]{2,1,0:T(8,128)S(1)} collective-permute-done((f32[4,64,128]{2,1,0:T(8,128)S(1)}, f32[4,64,128]{2,1,0:T(8,128)S(1)}, u32[]{:S(2)}, u32[]{:S(2)}) %collective-permute-start.1) | collective-permute-done | bytes 131104 | tf_op jit(solution)/shard_map/ppermute | solution.py:114
  18.9 1.9 %collective-permute-start.2 = (f32[2,64,128]{2,1,0:T(8,128)S(1)}, f32[2,64,128]{2,1,0:T(8,128)S(1)}, u32[]{:S(2)}, u32[]{:S(2)}) collective-permute-start(f32[2,64,128]{2,1,0:T(8,128)S(1)} %slice.27), channel_id=1, source_target_pairs={{0,8},{2,10},{4,12},{6,14},{8,0},{10,2},{12,4},{14,6},{16,24},{18,... | collective-permute-start | bytes 196616 | tf_op jit(solution)/shard_map/ppermute | solution.py:114
  20.8 2.4 %collective-permute-done.2 = f32[2,64,128]{2,1,0:T(8,128)S(1)} collective-permute-done((f32[2,64,128]{2,1,0:T(8,128)S(1)}, f32[2,64,128]{2,1,0:T(8,128)S(1)}, u32[]{:S(2)}, u32[]{:S(2)}) %collective-permute-start.2) | collective-permute-done | bytes 65568 | tf_op jit(solution)/shard_map/ppermute | solution.py:114
  23.3 2.9 %collective-permute-start.3 = (f32[1,64,128]{2,1,0:T(8,128)S(1)}, f32[1,64,128]{2,1,0:T(8,128)S(1)}, u32[]{:S(2)}, u32[]{:S(2)}) collective-permute-start(f32[1,64,128]{2,1,0:T(8,128)S(1)} %slice.29), channel_id=1, source_target_pairs={{0,16},{2,18},{4,20},{6,22},{8,24},{10,26},{12,28},{14,30},{16,0},... | collective-permute-start | bytes 98312 | tf_op jit(solution)/shard_map/ppermute | solution.py:114
  26.2 2.0 %collective-permute-done.3 = f32[1,64,128]{2,1,0:T(8,128)S(1)} collective-permute-done((f32[1,64,128]{2,1,0:T(8,128)S(1)}, f32[1,64,128]{2,1,0:T(8,128)S(1)}, u32[]{:S(2)}, u32[]{:S(2)}) %collective-permute-start.3) | collective-permute-done | bytes 32800 | tf_op jit(solution)/shard_map/ppermute | solution.py:114
  28.2 0.0 copy-start
  28.2 1.8 %collective-permute-start.4 = (f32[64,128]{1,0:T(8,128)S(1)}, f32[64,128]{1,0:T(8,128)S(1)}, u32[]{:S(2)}, u32[]{:S(2)}) collective-permute-start(f32[64,128]{1,0:T(8,128)S(1)} %fusion), channel_id=1, source_target_pairs={{0,1},{1,0},{2,3},{3,2},{4,5},{5,4},{6,7},{7,6},{8,9},{9,8},{10,11... | collective-permute-start | bytes 98312 | tf_op jit(solution)/shard_map/ppermute | solution.py:114
  30.0 2.1 %collective-permute-done.4 = f32[64,128]{1,0:T(8,128)S(1)} collective-permute-done((f32[64,128]{1,0:T(8,128)S(1)}, f32[64,128]{1,0:T(8,128)S(1)}, u32[]{:S(2)}, u32[]{:S(2)}) %collective-permute-start.4) | collective-permute-done | bytes 32800 | tf_op jit(solution)/shard_map/ppermute | solution.py:114
  32.1 0.2 fusion.1
  32.3 0.0 copy-done
  32.3 0.2 broadcast_select_fusion.1
  32.5 0.1 maximum_multiply_fusion
  32.6 0.0 collective-permute-start.5
  32.6 1.2 %collective-permute-done.5 = f32[64,128]{1,0:T(8,128)S(1)} collective-permute-done((f32[64,128]{1,0:T(8,128)S(1)}, f32[64,128]{1,0:T(8,128)S(1)}, u32[]{:S(2)}, u32[]{:S(2)}) %collective-permute-start.5) | collective-permute-done | bytes 32800 | tf_op jit(solution)/shard_map/ppermute | solution.py:114
  33.8 0.1 fusion.6
  33.9 1.7 %collective-permute-start.6 = (f32[64,128]{1,0:T(8,128)S(1)}, f32[64,128]{1,0:T(8,128)S(1)}, u32[]{:S(2)}, u32[]{:S(2)}) collective-permute-start(f32[64,128]{1,0:T(8,128)S(1)} %fusion.6), channel_id=1, source_target_pairs={{0,4},{2,6},{4,0},{6,2},{8,12},{10,14},{12,8},{14,10},{16,20},{18,... | collective-permute-start | bytes 98312 | tf_op jit(solution)/shard_map/ppermute | solution.py:114
  35.7 2.2 %collective-permute-done.6 = f32[64,128]{1,0:T(8,128)S(1)} collective-permute-done((f32[64,128]{1,0:T(8,128)S(1)}, f32[64,128]{1,0:T(8,128)S(1)}, u32[]{:S(2)}, u32[]{:S(2)}) %collective-permute-start.6) | collective-permute-done | bytes 32800 | tf_op jit(solution)/shard_map/ppermute | solution.py:114
  37.8 1.8 %collective-permute-start.7 = (f32[64,128]{1,0:T(8,128)S(1)}, f32[64,128]{1,0:T(8,128)S(1)}, u32[]{:S(2)}, u32[]{:S(2)}) collective-permute-start(f32[64,128]{1,0:T(8,128)S(1)} %add.29), channel_id=1, source_target_pairs={{0,8},{2,10},{4,12},{6,14},{8,0},{10,2},{12,4},{14,6},{16,24},{18,... | collective-permute-start | bytes 98312 | tf_op jit(solution)/shard_map/ppermute | solution.py:114
  39.7 2.1 %collective-permute-done.7 = f32[64,128]{1,0:T(8,128)S(1)} collective-permute-done((f32[64,128]{1,0:T(8,128)S(1)}, f32[64,128]{1,0:T(8,128)S(1)}, u32[]{:S(2)}, u32[]{:S(2)}) %collective-permute-start.7) | collective-permute-done | bytes 32800 | tf_op jit(solution)/shard_map/ppermute | solution.py:114
  41.8 2.9 %collective-permute-start.8 = (f32[64,128]{1,0:T(8,128)S(1)}, f32[64,128]{1,0:T(8,128)S(1)}, u32[]{:S(2)}, u32[]{:S(2)}) collective-permute-start(f32[64,128]{1,0:T(8,128)S(1)} %add.30), channel_id=1, source_target_pairs={{0,16},{2,18},{4,20},{6,22},{8,24},{10,26},{12,28},{14,30},{16,0},... | collective-permute-start | bytes 98312 | tf_op jit(solution)/shard_map/ppermute | solution.py:114
  44.6 2.0 %collective-permute-done.8 = f32[64,128]{1,0:T(8,128)S(1)} collective-permute-done((f32[64,128]{1,0:T(8,128)S(1)}, f32[64,128]{1,0:T(8,128)S(1)}, u32[]{:S(2)}, u32[]{:S(2)}) %collective-permute-start.8) | collective-permute-done | bytes 32800 | tf_op jit(solution)/shard_map/ppermute | solution.py:114
  46.6 0.6 %add.31 = f32[64,128]{1,0:T(8,128)} add(f32[64,128]{1,0:T(8,128)S(1)} %add.30, f32[64,128]{1,0:T(8,128)S(1)} %collective-permute-done.8) | non-fusion elementwise | flops 8192 | bytes 98304 | tf_op jit(solution)/shard_map/add | solution.py:137
  (8 shorter events, 0.1 us)
Async XLA Ops:
  9.2 1.9 %collective-permute-start = (f32[8,64,128]{2,1,0:T(8,128)}, f32[8,64,128]{2,1,0:T(8,128)S(1)}, u32[]{:S(2)}, u32[]{:S(2)}) collective-permute-start(f32[8,64,128]{2,1,0:T(8,128)} %get-tuple-element.5), channel_id=1, source_target_pairs={{0,2},{2,0},{4,6},{6,4},{8,10},{10,8},{12,14},{14,12},{16,18},{18,... | collective-permute-start | bytes 786440 | tf_op jit(solution)/shard_map/ppermute | solution.py:114
  12.2 6.7 %collective-permute-start.1 = (f32[4,64,128]{2,1,0:T(8,128)S(1)}, f32[4,64,128]{2,1,0:T(8,128)S(1)}, u32[]{:S(2)}, u32[]{:S(2)}) collective-permute-start(f32[4,64,128]{2,1,0:T(8,128)S(1)} %slice.25), channel_id=1, source_target_pairs={{0,4},{2,6},{4,0},{6,2},{8,12},{10,14},{12,8},{14,10},{16,20},{18,... | collective-permute-start | bytes 393224 | tf_op jit(solution)/shard_map/ppermute | solution.py:114
  18.9 4.3 %collective-permute-start.2 = (f32[2,64,128]{2,1,0:T(8,128)S(1)}, f32[2,64,128]{2,1,0:T(8,128)S(1)}, u32[]{:S(2)}, u32[]{:S(2)}) collective-permute-start(f32[2,64,128]{2,1,0:T(8,128)S(1)} %slice.27), channel_id=1, source_target_pairs={{0,8},{2,10},{4,12},{6,14},{8,0},{10,2},{12,4},{14,6},{16,24},{18,... | collective-permute-start | bytes 196616 | tf_op jit(solution)/shard_map/ppermute | solution.py:114
  23.3 4.9 %collective-permute-start.3 = (f32[1,64,128]{2,1,0:T(8,128)S(1)}, f32[1,64,128]{2,1,0:T(8,128)S(1)}, u32[]{:S(2)}, u32[]{:S(2)}) collective-permute-start(f32[1,64,128]{2,1,0:T(8,128)S(1)} %slice.29), channel_id=1, source_target_pairs={{0,16},{2,18},{4,20},{6,22},{8,24},{10,26},{12,28},{14,30},{16,0},... | collective-permute-start | bytes 98312 | tf_op jit(solution)/shard_map/ppermute | solution.py:114
  28.2 4.2 %copy-start = (f32[64,128]{1,0:T(8,128)}, f32[64,128]{1,0:T(8,128)S(1)}, u32[]{:S(2)}) copy-start(f32[64,128]{1,0:T(8,128)S(1)} %fusion) | copy-start | bytes 98308
  28.2 4.0 %collective-permute-start.4 = (f32[64,128]{1,0:T(8,128)S(1)}, f32[64,128]{1,0:T(8,128)S(1)}, u32[]{:S(2)}, u32[]{:S(2)}) collective-permute-start(f32[64,128]{1,0:T(8,128)S(1)} %fusion), channel_id=1, source_target_pairs={{0,1},{1,0},{2,3},{3,2},{4,5},{5,4},{6,7},{7,6},{8,9},{9,8},{10,11... | collective-permute-start | bytes 98312 | tf_op jit(solution)/shard_map/ppermute | solution.py:114
  32.6 1.2 %collective-permute-start.5 = (f32[64,128]{1,0:T(8,128)S(1)}, f32[64,128]{1,0:T(8,128)S(1)}, u32[]{:S(2)}, u32[]{:S(2)}) collective-permute-start(f32[64,128]{1,0:T(8,128)S(1)} %maximum_multiply_fusion), channel_id=1, source_target_pairs={{0,2},{2,0},{4,6},{6,4},{8,10},{10,8},{12,14},{14,12},{16,18},{18,... | collective-permute-start | bytes 98312 | tf_op jit(solution)/shard_map/ppermute | solution.py:114
  33.9 3.9 %collective-permute-start.6 = (f32[64,128]{1,0:T(8,128)S(1)}, f32[64,128]{1,0:T(8,128)S(1)}, u32[]{:S(2)}, u32[]{:S(2)}) collective-permute-start(f32[64,128]{1,0:T(8,128)S(1)} %fusion.6), channel_id=1, source_target_pairs={{0,4},{2,6},{4,0},{6,2},{8,12},{10,14},{12,8},{14,10},{16,20},{18,... | collective-permute-start | bytes 98312 | tf_op jit(solution)/shard_map/ppermute | solution.py:114
  37.8 3.9 %collective-permute-start.7 = (f32[64,128]{1,0:T(8,128)S(1)}, f32[64,128]{1,0:T(8,128)S(1)}, u32[]{:S(2)}, u32[]{:S(2)}) collective-permute-start(f32[64,128]{1,0:T(8,128)S(1)} %add.29), channel_id=1, source_target_pairs={{0,8},{2,10},{4,12},{6,14},{8,0},{10,2},{12,4},{14,6},{16,24},{18,... | collective-permute-start | bytes 98312 | tf_op jit(solution)/shard_map/ppermute | solution.py:114
  41.8 4.8 %collective-permute-start.8 = (f32[64,128]{1,0:T(8,128)S(1)}, f32[64,128]{1,0:T(8,128)S(1)}, u32[]{:S(2)}, u32[]{:S(2)}) collective-permute-start(f32[64,128]{1,0:T(8,128)S(1)} %add.30), channel_id=1, source_target_pairs={{0,16},{2,18},{4,20},{6,22},{8,24},{10,26},{12,28},{14,30},{16,0},... | collective-permute-start | bytes 98312 | tf_op jit(solution)/shard_map/ppermute | solution.py:114

commit v2 on v1

v2 whole, which is shorter than its diff:
```python
import jax
import jax.numpy as jnp
import numpy as np
from jax import lax
from jax.experimental import pallas as pl
from jax.experimental.pallas import tpu as pltpu
from jax.sharding import PartitionSpec as P

WIDE = 256
LANES = 128
VMEM_GRANT = 16 << 20


def in_hbm(value):
    return pltpu.with_memory_space_constraint(value, pltpu.HBM)


def parity(value, bits):
    total = jnp.zeros_like(value)
    for k in range(bits):
        total = total ^ (value >> k)
    return total & 1


def mix_blocks(x_hbm, s_ref, s_copy, x_ref, t_ref, sems):
    columns, length = x_ref.shape
    slabs = length // WIDE // 2
    groups = slabs // 2
    span = 2 * WIDE
    half = length // 2
    copies = []
    for g in range(groups):
        for h in range(2):
            window = pl.ds(h * half + g * span, span)
            copies.append(pltpu.make_async_copy(x_hbm.at[:, window], x_ref.at[:, window], sems.at[g, h]))
            copies[-1].start()
    left = lax.broadcasted_iota(jnp.int32, (WIDE, WIDE), 0)
    right = lax.broadcasted_iota(jnp.int32, (WIDE, WIDE), 1)
    mat = (1 - 2 * parity(left & right, WIDE.bit_length() - 1)).astype(jnp.float32).astype(jnp.bfloat16)
    s_copy.wait()
    for g in range(groups):
        copies[2 * g].wait()
        copies[2 * g + 1].wait()
        parts = []
        for q in range(2):
            for h in range(2):
                block = h * slabs + 2 * g + q
                signs = jnp.concatenate([s_ref[2 * block:2 * block + 1, :], s_ref[2 * block + 1:2 * block + 2, :]], axis=1)
                parts.append(x_ref[:, block * WIDE:(block + 1) * WIDE] * signs.astype(jnp.float32).astype(jnp.bfloat16))
        stacked = jnp.concatenate(parts, axis=0)
        out = lax.dot_general(mat, stacked, (((1,), (1,)), ((), ())), preferred_element_type=jnp.float32)
        one, two = out[:, :LANES], out[:, LANES:]
        t_ref[(2 * g) * WIDE:(2 * g + 1) * WIDE, :] = one + two
        t_ref[(2 * g + 1) * WIDE:(2 * g + 2) * WIDE, :] = one - two

    def butterfly(i, _):
        for q in range(2):
            at = [pl.ds(pl.multiple_of((2 * g + q) * WIDE + i * 8, 8), 8) for g in range(groups)]
            v = [t_ref[a, :] for a in at]
            step = 1
            while step < groups:
                for j in range(groups):
                    if not j & step:
                        v[j], v[j + step] = v[j] + v[j + step], v[j] - v[j + step]
                step *= 2
            for a, value in zip(at, v):
                t_ref[a, :] = value
        return 0

    lax.fori_loop(0, WIDE // 8, butterfly, 0, unroll=4)


def gather_blocks(devices, length, columns, base, rows_smem, rows_ref, t_ref, g_ref, out_ref):
    per = rows_ref.shape[1]
    half = length // 2
    bits = devices.bit_length() - 1
    top = length.bit_length() - 2
    scale = float(1.0 / np.sqrt(float(length) * devices))
    me = lax.axis_index("row")

    def gather(i, _):
        p = base + i
        dest = (me & -2) ^ (p & 1)
        for k in range(1, bits):
            dest = dest ^ (((p >> k) & 1) << (bits - k))
        for t in range(per):
            row = rows_smem[dest * per + t] & (half - 1)
            g_ref[t:t + 1, :] = t_ref[pl.ds(row, 1), :]
        turned = g_ref[...].T
        samples = rows_ref[pl.ds(dest, 1), :]
        flip = parity((samples >> (top + 1)) & me, bits)
        first = jnp.where(flip == 1, -scale, scale)
        second = jnp.where((flip ^ ((samples >> top) & 1)) == 1, -scale, scale)
        out_ref[i] = turned[:columns, :] * first + turned[columns:, :] * second
        return 0

    lax.fori_loop(0, out_ref.shape[0], gather, 0)


def mix(matrix_panel, row_signs, sample_rows, devices):
    columns, length = matrix_panel.shape
    per = sample_rows.shape[0] // devices
    half = devices // 2
    anywhere = pl.BlockSpec(memory_space=pltpu.HBM)

    def kernel(x_hbm, s_hbm, flat_hbm, rows_hbm, t_ref, out_ref, x_ref, s_ref, flat_ref, rows_ref, g_ref, sems, more):
        fetch = [pltpu.make_async_copy(a, b, more.at[k]) for k, (a, b) in enumerate(((s_hbm, s_ref), (flat_hbm, flat_ref), (rows_hbm, rows_ref)))]
        for copy in fetch:
            copy.start()
        mix_blocks(x_hbm, s_ref, fetch[0], x_ref, t_ref, sems)
        fetch[1].wait()
        fetch[2].wait()
        gather_blocks(devices, length, columns, half, flat_ref, rows_ref, t_ref, g_ref, out_ref)

    return pl.pallas_call(
        kernel,
        out_shape=(pltpu.VMEM((length // 2, LANES), jnp.float32), pltpu.VMEM((half, columns, per), jnp.float32)),
        in_specs=[anywhere] * 4,
        scratch_shapes=[
            pltpu.VMEM((columns, length), jnp.bfloat16),
            pltpu.VMEM((length // LANES, LANES), jnp.int32),
            pltpu.SMEM(sample_rows.shape, jnp.int32),
            pltpu.VMEM((devices, per), jnp.int32),
            pltpu.VMEM((per, LANES), jnp.float32),
            pltpu.SemaphoreType.DMA((length // WIDE // 4, 2)),
            pltpu.SemaphoreType.DMA((3,)),
        ],
        compiler_params=pltpu.CompilerParams(vmem_limit_bytes=VMEM_GRANT),
    )(*(in_hbm(a) for a in (matrix_panel, row_signs.reshape(length // LANES, LANES), sample_rows, sample_rows.reshape(devices, per))))


def pick(table, sample_rows, columns, length, devices):
    per = sample_rows.shape[0] // devices
    half = devices // 2
    anywhere = pl.BlockSpec(memory_space=pltpu.HBM)

    def kernel(t_ref, flat_hbm, rows_hbm, out_ref, flat_ref, rows_ref, g_ref, more):
        fetch = [pltpu.make_async_copy(a, b, more.at[k]) for k, (a, b) in enumerate(((flat_hbm, flat_ref), (rows_hbm, rows_ref)))]
        for copy in fetch:
            copy.start()
        for copy in fetch:
            copy.wait()
        gather_blocks(devices, length, columns, 0, flat_ref, rows_ref, t_ref, g_ref, out_ref)

    return pl.pallas_call(
        kernel,
        out_shape=pltpu.VMEM((half, columns, per), jnp.float32),
        in_specs=[pl.BlockSpec(memory_space=pltpu.VMEM), anywhere, anywhere],
        scratch_shapes=[
            pltpu.SMEM(sample_rows.shape, jnp.int32),
            pltpu.VMEM((devices, per), jnp.int32),
            pltpu.VMEM((per, LANES), jnp.float32),
            pltpu.SemaphoreType.DMA((2,)),
        ],
        compiler_params=pltpu.CompilerParams(vmem_limit_bytes=VMEM_GRANT),
    )(pltpu.with_memory_space_constraint(table, pltpu.VMEM), in_hbm(sample_rows), in_hbm(sample_rows.reshape(devices, per)))


def chips(value, bit):
    size = lax.axis_size("row")
    return lax.ppermute(value, "row", [(i, i ^ bit) for i in range(1, size, 2)])


def up(value):
    return lax.ppermute(value, "row", [(i, i + 1) for i in range(0, lax.axis_size("row"), 2)])


def down(value):
    return lax.ppermute(value, "row", [(i + 1, i) for i in range(0, lax.axis_size("row"), 2)])


def body(matrix_panel, row_signs, sample_rows):
    devices = lax.axis_size("row")
    columns, length = matrix_panel.shape
    everything = sample_rows.shape[0]
    bits = devices.bit_length() - 1
    odd = (lax.axis_index("row") & 1) == 1
    table, send = mix(matrix_panel, row_signs, sample_rows, devices)
    send = send + up(send)
    table, send = lax.optimization_barrier((table, send))
    moved = chips(send, 2)
    keep = pick(table, sample_rows, columns, length, devices)
    total = (keep + up(keep)) + moved
    for k in range(2, bits - 1):
        half = total.shape[0] // 2
        total = total[:half] + chips(total[half:], 1 << k)
    moved = chips(total, 1 << (bits - 1))
    mine = total[:2] + moved[2:]
    theirs = total[2:] + moved[:2]
    full = jnp.concatenate([mine, theirs], axis=0)
    pairs = [((2 * i + 1) * 2 + c, (2 * i + 1) * 2 + 1 - c) for i in range(devices // 2) for c in range(2)]
    other = lax.ppermute(full, ("row", "col"), pairs)
    sketch = jnp.where(odd, mine[1], down(mine[0]))
    own = jnp.einsum("bcs,bds->cd", full, full, precision=lax.Precision.HIGHEST)
    cross = jnp.einsum("bcs,bds->cd", full, other, precision=lax.Precision.HIGHEST)
    first = lax.axis_index("col") == 0
    gram = jnp.concatenate([jnp.where(first, own, cross), jnp.where(first, cross, own)], axis=1)
    gram = gram / everything
    for k in range(1, bits - 1):
        gram = gram + chips(gram, 1 << k)
    gram = jnp.where(odd, gram, down(gram))
    return (sketch, gram)


def solution(mesh):
    return jax.shard_map(
        body,
        mesh=mesh,
        in_specs=(P("col", "row"), P("row"), P()),
        out_specs=(P("col", "row"), P("col", None)),
        check_vma=False,
    )
```

time: 47.5 us -> 52.6 us (1.11)
  waiting for transfers between devices: 19.1 us -> 26.7 us
  starting transfers between devices: 16.5 us -> 14.5 us
    ppermute x9 -> x10, waiting for transfers between devices: 19.1 us -> 26.7 us  [the longest x2 24.4 us: down(): lax.ppermute(value, 'row', [(i + 1, i) for i in range(0, lax.axis_size('r...]
    ppermute x9 -> x10, starting transfers between devices: 16.5 us -> 14.5 us  [the longest x2 7.97 us: up(): lax.ppermute(value, 'row', [(i, i + 1) for i in range(0, lax.axis_size('r...]
    add x7 -> x6, other arithmetic: 1.72 us -> 0.22 us  [the longest x2 0.09 us: body(): gram = gram + chips(gram, 1 << k)]
    select_n x0 -> x2, other arithmetic: none -> 1.24 us  [the longest x1 0.62 us: body(): sketch = jnp.where(odd, mine[1], down(mine[0]))]
    pallas_call x1 -> x2, Pallas kernels: 8.59 us -> 8.07 us  [the longest x1 5.48 us: mix(): pl.pallas_call(kernel, out_shape=(pltpu.VMEM((length // 2, LANES), jnp.fl...]
  transfers between devices with their start and end apart: 9 -> 10, of which waited for: 9 -> 4; matrix products, arithmetic and copies ran while one was open for 0% -> 1% of each run, Pallas kernels for 0% -> 5%
where the time goes in v2:
time: 52.6 us; the launch traced here: 52.2 us
  waiting for transfers between devices  26.7 us (51%)
  starting transfers between devices  14.5 us (28%)
  Pallas kernels  8.07 us (15%)
  other arithmetic  1.55 us (3%)
  between operations  0.85 us (2%)
    ppermute x2, waiting for transfers between devices, down(): lax.ppermute(value, 'row', [(i + 1, i) for i in range(0, lax.axis_size('r...  24.4 us
    ppermute x2, starting transfers between devices, up(): lax.ppermute(value, 'row', [(i, i + 1) for i in range(0, lax.axis_size('r...  7.97 us
    pallas_call x1, Pallas kernels, mix(): pl.pallas_call(kernel, out_shape=(pltpu.VMEM((length // 2, LANES), jnp.fl...  5.48 us
    ppermute x5, starting transfers between devices, chips(): return lax.ppermute(value, 'row', [(i, i ^ bit) for i in range(1, size, 2)])  3.32 us
    pallas_call x1, Pallas kernels, pick(): pl.pallas_call(kernel, out_shape=pltpu.VMEM((half, columns, per), jnp.flo...  2.59 us
    ppermute x2, starting transfers between devices, down(): lax.ppermute(value, 'row', [(i + 1, i) for i in range(0, lax.axis_size('r...  2.58 us
    ppermute x2, waiting for transfers between devices, up(): lax.ppermute(value, 'row', [(i, i + 1) for i in range(0, lax.axis_size('r...  2.25 us
  transfers between devices with their start and end apart: 10, of which 4 were waited for; matrix products, arithmetic and copies ran while one was open for 1% of the time, Pallas kernels for 5%

profile of v2, /device:TPU:0, one launch (start us, length us, event | category | flops | bytes accessed | tf_op | source)
XLA Modules:
  0.0 52.2 jit_solution(10292018948924544058)
XLA Ops:
  0.6 5.5 %shard_map.50 = (f32[4096,128]{1,0:T(8,128)S(1)}, f32[8,64,128]{2,1,0:T(8,128)S(1)}) custom-call(bf16[64,8192]{1,0:T(8,128)(2,1)} %x_hbm.1, s32[64,128]{1,0:T(8,128)} %bitcast.15, s32[2048]{0:T(1024)} %flat_hbm.3, s32[16,128]{1,0:T(8,128)} %bitcast.13), custom_call_target="tpu_custom_call" | custom-call | tf_op jit(solution)/shard_map/pallas_call | solution.py:115
  6.1 2.4 %collective-permute-start = (f32[8,64,128]{2,1,0:T(8,128)S(1)}, f32[8,64,128]{2,1,0:T(8,128)S(1)}, u32[]{:S(2)}, u32[]{:S(2)}) collective-permute-start(f32[8,64,128]{2,1,0:T(8,128)S(1)} %get-tuple-element.7), channel_id=1, source_target_pairs={{0,2},{4,6},{8,10},{12,14},{16,18},{20,22},{24,26},{28,30},{1,3},{... | collective-permute-start | bytes 786440 | tf_op jit(solution)/shard_map/ppermute | solution.py:165
  8.5 1.1 %collective-permute-done = f32[8,64,128]{2,1,0:T(8,128)S(1)} collective-permute-done((f32[8,64,128]{2,1,0:T(8,128)S(1)}, f32[8,64,128]{2,1,0:T(8,128)S(1)}, u32[]{:S(2)}, u32[]{:S(2)}) %collective-permute-start) | collective-permute-done | bytes 262176 | tf_op jit(solution)/shard_map/ppermute | solution.py:165
  9.7 0.7 %collective-permute-start.2 = (f32[8,64,128]{2,1,0:T(8,128)S(1)}, f32[8,64,128]{2,1,0:T(8,128)S(1)}, u32[]{:S(2)}, u32[]{:S(2)}) collective-permute-start(f32[8,64,128]{2,1,0:T(8,128)S(1)} %add.24), channel_id=1, source_target_pairs={{2,6},{6,2},{10,14},{14,10},{18,22},{22,18},{26,30},{30,26},{3,7},... | collective-permute-start | bytes 786440 | tf_op jit(solution)/shard_map/ppermute | solution.py:161
  10.4 2.6 %shard_map.51 = f32[8,64,128]{2,1,0:T(8,128)S(1)} custom-call(f32[4096,128]{1,0:T(8,128)S(1)} %get-tuple-element.8.t_ref, s32[2048]{0:T(1024)} %flat_hbm.3, s32[16,128]{1,0:T(8,128)} %bitcast.14), custom_call_target="tpu_custom_call" | custom-call | tf_op jit(solution)/shard_map/pallas_call | solution.py:145
  13.0 5.6 %collective-permute-start.1 = (f32[8,64,128]{2,1,0:T(8,128)S(1)}, f32[8,64,128]{2,1,0:T(8,128)S(1)}, u32[]{:S(2)}, u32[]{:S(2)}) collective-permute-start(f32[8,64,128]{2,1,0:T(8,128)S(1)} %shard_map.51), channel_id=1, source_target_pairs={{0,2},{4,6},{8,10},{12,14},{16,18},{20,22},{24,26},{28,30},{1,3},{... | collective-permute-start | bytes 786440 | tf_op jit(solution)/shard_map/ppermute | solution.py:165
  18.6 0.0 collective-permute-done.2
  18.6 1.1 %collective-permute-done.1 = f32[8,64,128]{2,1,0:T(8,128)S(1)} collective-permute-done((f32[8,64,128]{2,1,0:T(8,128)S(1)}, f32[8,64,128]{2,1,0:T(8,128)S(1)}, u32[]{:S(2)}, u32[]{:S(2)}) %collective-permute-start.1) | collective-permute-done | bytes 262176 | tf_op jit(solution)/shard_map/ppermute | solution.py:165
  19.7 0.1 add_add_fusion
  19.8 0.7 %collective-permute-start.3 = (f32[4,64,128]{2,1,0:T(8,128)S(1)}, f32[4,64,128]{2,1,0:T(8,128)S(1)}, u32[]{:S(2)}, u32[]{:S(2)}) collective-permute-start(f32[4,64,128]{2,1,0:T(8,128)S(1)} %slice.33), channel_id=1, source_target_pairs={{2,10},{6,14},{10,2},{14,6},{18,26},{22,30},{26,18},{30,22},{3,11}... | collective-permute-start | bytes 393224 | tf_op jit(solution)/shard_map/ppermute | solution.py:161
  20.4 0.0 collective-permute-done.3
  20.5 0.7 %collective-permute-start.4 = (f32[4,64,128]{2,1,0:T(8,128)S(1)}, f32[4,64,128]{2,1,0:T(8,128)S(1)}, u32[]{:S(2)}, u32[]{:S(2)}) collective-permute-start(f32[4,64,128]{2,1,0:T(8,128)S(1)} %slice_add_fusion), channel_id=1, source_target_pairs={{2,18},{6,22},{10,26},{14,30},{18,2},{22,6},{26,10},{30,14},{3,19}... | collective-permute-start | bytes 393224 | tf_op jit(solution)/shard_map/ppermute | solution.py:161
  21.1 0.0 collective-permute-done.4
  21.2 0.7 %collective-permute-start.6 = (f32[4,64,128]{2,1,0:T(8,128)S(1)}, f32[4,64,128]{2,1,0:T(8,128)S(1)}, u32[]{:S(2)}, u32[]{:S(2)}) collective-permute-start(f32[4,64,128]{2,1,0:T(8,128)S(1)} %pad_maximum_fusion), channel_id=1, source_target_pairs={{2,3},{3,2},{6,7},{7,6},{10,11},{11,10},{14,15},{15,14},{18,19},{1... | collective-permute-start | bytes 393224 | tf_op jit(solution)/shard_map/ppermute | solution.py:192
  21.9 0.0 collective-permute-done.6
  21.9 0.3 convolution_bitcast_fusion
  22.2 0.3 broadcast_select_fusion.1
  22.4 0.1 maximum_multiply_fusion
  22.5 0.7 %collective-permute-start.7 = (f32[64,128]{1,0:T(8,128)S(1)}, f32[64,128]{1,0:T(8,128)S(1)}, u32[]{:S(2)}, u32[]{:S(2)}) collective-permute-start(f32[64,128]{1,0:T(8,128)S(1)} %maximum_multiply_fusion), channel_id=1, source_target_pairs={{2,6},{6,2},{10,14},{14,10},{18,22},{22,18},{26,30},{30,26},{3,7},... | collective-permute-start | bytes 98312 | tf_op jit(solution)/shard_map/ppermute | solution.py:161
  23.2 0.0 collective-permute-done.7
  23.2 0.1 fusion.2
  23.3 0.7 %collective-permute-start.8 = (f32[64,128]{1,0:T(8,128)S(1)}, f32[64,128]{1,0:T(8,128)S(1)}, u32[]{:S(2)}, u32[]{:S(2)}) collective-permute-start(f32[64,128]{1,0:T(8,128)S(1)} %fusion.2), channel_id=1, source_target_pairs={{2,10},{6,14},{10,2},{14,6},{18,26},{22,30},{26,18},{30,22},{3,11}... | collective-permute-start | bytes 98312 | tf_op jit(solution)/shard_map/ppermute | solution.py:161
  23.9 1.3 %collective-permute-start.5 = (f32[64,128]{1,0:T(8,128)S(1)}, f32[64,128]{1,0:T(8,128)S(1)}, u32[]{:S(2)}, u32[]{:S(2)}) collective-permute-start(f32[64,128]{1,0:T(8,128)S(1)} %slice_bitcast_fusion), channel_id=1, source_target_pairs={{2,0},{6,4},{10,8},{14,12},{18,16},{22,20},{26,24},{30,28},{3,1},{... | collective-permute-start | bytes 98312 | tf_op jit(solution)/shard_map/ppermute | solution.py:169
  25.2 0.0 collective-permute-done.8
  25.3 1.3 %collective-permute-start.9 = (f32[64,128]{1,0:T(8,128)S(1)}, f32[64,128]{1,0:T(8,128)S(1)}, u32[]{:S(2)}, u32[]{:S(2)}) collective-permute-start(f32[64,128]{1,0:T(8,128)S(1)} %add.31), channel_id=1, source_target_pairs={{2,0},{6,4},{10,8},{14,12},{18,16},{22,20},{26,24},{30,28},{3,1},{... | collective-permute-start | bytes 98312 | tf_op jit(solution)/shard_map/ppermute | solution.py:169
  26.6 23.0 %collective-permute-done.5 = f32[64,128]{1,0:T(8,128)S(1)} collective-permute-done((f32[64,128]{1,0:T(8,128)S(1)}, f32[64,128]{1,0:T(8,128)S(1)}, u32[]{:S(2)}, u32[]{:S(2)}) %collective-permute-start.5) | collective-permute-done | bytes 32800 | tf_op jit(solution)/shard_map/ppermute | solution.py:169
  49.6 0.6 %fusion = f32[64,128]{1,0:T(8,128)} fusion(f32[64,128]{1,0:T(8,128)S(1)} %collective-permute-done.5, f32[2,64,128]{2,1,0:T(8,128)S(1)} %get-tuple-element.11, pred[]{:T(512)S(6)} %eq.6), kind=kLoop, calls=%fused_computation.9 | loop fusion | flops 8192 | bytes 98305 | tf_op jit(solution)/shard_map/jit(_where)/select_n | solution.py:193
  50.2 1.4 %collective-permute-done.9 = f32[64,128]{1,0:T(8,128)S(1)} collective-permute-done((f32[64,128]{1,0:T(8,128)S(1)}, f32[64,128]{1,0:T(8,128)S(1)}, u32[]{:S(2)}, u32[]{:S(2)}) %collective-permute-start.9) | collective-permute-done | bytes 32800 | tf_op jit(solution)/shard_map/ppermute | solution.py:169
  51.6 0.6 %broadcast_select_fusion.2 = f32[64,128]{1,0:T(8,128)} fusion(f32[64,128]{1,0:T(8,128)S(1)} %add.31, f32[64,128]{1,0:T(8,128)S(1)} %collective-permute-done.9, pred[]{:T(512)S(6)} %eq.6), kind=kLoop, calls=%fused_computation.13 | loop fusion | flops 8192 | bytes 98305 | tf_op jit(solution)/shard_map/jit(_where)/select_n | solution.py:201
  (7 shorter events, 0.1 us)
Async XLA Ops:
  6.1 3.5 %collective-permute-start = (f32[8,64,128]{2,1,0:T(8,128)S(1)}, f32[8,64,128]{2,1,0:T(8,128)S(1)}, u32[]{:S(2)}, u32[]{:S(2)}) collective-permute-start(f32[8,64,128]{2,1,0:T(8,128)S(1)} %get-tuple-element.7), channel_id=1, source_target_pairs={{0,2},{4,6},{8,10},{12,14},{16,18},{20,22},{24,26},{28,30},{1,3},{... | collective-permute-start | bytes 786440 | tf_op jit(solution)/shard_map/ppermute | solution.py:165
  9.7 8.8 %collective-permute-start.2 = (f32[8,64,128]{2,1,0:T(8,128)S(1)}, f32[8,64,128]{2,1,0:T(8,128)S(1)}, u32[]{:S(2)}, u32[]{:S(2)}) collective-permute-start(f32[8,64,128]{2,1,0:T(8,128)S(1)} %add.24), channel_id=1, source_target_pairs={{2,6},{6,2},{10,14},{14,10},{18,22},{22,18},{26,30},{30,26},{3,7},... | collective-permute-start | bytes 786440 | tf_op jit(solution)/shard_map/ppermute | solution.py:161
  13.0 6.7 %collective-permute-start.1 = (f32[8,64,128]{2,1,0:T(8,128)S(1)}, f32[8,64,128]{2,1,0:T(8,128)S(1)}, u32[]{:S(2)}, u32[]{:S(2)}) collective-permute-start(f32[8,64,128]{2,1,0:T(8,128)S(1)} %shard_map.51), channel_id=1, source_target_pairs={{0,2},{4,6},{8,10},{12,14},{16,18},{20,22},{24,26},{28,30},{1,3},{... | collective-permute-start | bytes 786440 | tf_op jit(solution)/shard_map/ppermute | solution.py:165
  19.8 0.7 %collective-permute-start.3 = (f32[4,64,128]{2,1,0:T(8,128)S(1)}, f32[4,64,128]{2,1,0:T(8,128)S(1)}, u32[]{:S(2)}, u32[]{:S(2)}) collective-permute-start(f32[4,64,128]{2,1,0:T(8,128)S(1)} %slice.33), channel_id=1, source_target_pairs={{2,10},{6,14},{10,2},{14,6},{18,26},{22,30},{26,18},{30,22},{3,11}... | collective-permute-start | bytes 393224 | tf_op jit(solution)/shard_map/ppermute | solution.py:161
  20.5 0.7 %collective-permute-start.4 = (f32[4,64,128]{2,1,0:T(8,128)S(1)}, f32[4,64,128]{2,1,0:T(8,128)S(1)}, u32[]{:S(2)}, u32[]{:S(2)}) collective-permute-start(f32[4,64,128]{2,1,0:T(8,128)S(1)} %slice_add_fusion), channel_id=1, source_target_pairs={{2,18},{6,22},{10,26},{14,30},{18,2},{22,6},{26,10},{30,14},{3,19}... | collective-permute-start | bytes 393224 | tf_op jit(solution)/shard_map/ppermute | solution.py:161
  21.2 0.7 %collective-permute-start.6 = (f32[4,64,128]{2,1,0:T(8,128)S(1)}, f32[4,64,128]{2,1,0:T(8,128)S(1)}, u32[]{:S(2)}, u32[]{:S(2)}) collective-permute-start(f32[4,64,128]{2,1,0:T(8,128)S(1)} %pad_maximum_fusion), channel_id=1, source_target_pairs={{2,3},{3,2},{6,7},{7,6},{10,11},{11,10},{14,15},{15,14},{18,19},{1... | collective-permute-start | bytes 393224 | tf_op jit(solution)/shard_map/ppermute | solution.py:192
  22.5 0.7 %collective-permute-start.7 = (f32[64,128]{1,0:T(8,128)S(1)}, f32[64,128]{1,0:T(8,128)S(1)}, u32[]{:S(2)}, u32[]{:S(2)}) collective-permute-start(f32[64,128]{1,0:T(8,128)S(1)} %maximum_multiply_fusion), channel_id=1, source_target_pairs={{2,6},{6,2},{10,14},{14,10},{18,22},{22,18},{26,30},{30,26},{3,7},... | collective-permute-start | bytes 98312 | tf_op jit(solution)/shard_map/ppermute | solution.py:161
  23.3 2.0 %collective-permute-start.8 = (f32[64,128]{1,0:T(8,128)S(1)}, f32[64,128]{1,0:T(8,128)S(1)}, u32[]{:S(2)}, u32[]{:S(2)}) collective-permute-start(f32[64,128]{1,0:T(8,128)S(1)} %fusion.2), channel_id=1, source_target_pairs={{2,10},{6,14},{10,2},{14,6},{18,26},{22,30},{26,18},{30,22},{3,11}... | collective-permute-start | bytes 98312 | tf_op jit(solution)/shard_map/ppermute | solution.py:161
  23.9 25.6 %collective-permute-start.5 = (f32[64,128]{1,0:T(8,128)S(1)}, f32[64,128]{1,0:T(8,128)S(1)}, u32[]{:S(2)}, u32[]{:S(2)}) collective-permute-start(f32[64,128]{1,0:T(8,128)S(1)} %slice_bitcast_fusion), channel_id=1, source_target_pairs={{2,0},{6,4},{10,8},{14,12},{18,16},{22,20},{26,24},{30,28},{3,1},{... | collective-permute-start | bytes 98312 | tf_op jit(solution)/shard_map/ppermute | solution.py:169
  25.3 26.3 %collective-permute-start.9 = (f32[64,128]{1,0:T(8,128)S(1)}, f32[64,128]{1,0:T(8,128)S(1)}, u32[]{:S(2)}, u32[]{:S(2)}) collective-permute-start(f32[64,128]{1,0:T(8,128)S(1)} %add.31), channel_id=1, source_target_pairs={{2,0},{6,4},{10,8},{14,12},{18,16},{22,20},{26,24},{30,28},{3,1},{... | collective-permute-start | bytes 98312 | tf_op jit(solution)/shard_map/ppermute | solution.py:169

commit v3 on v2

--- a/solution.py
+++ b/solution.py
@@ -6,6 +6,7 @@
 from jax.experimental.pallas import tpu as pltpu
 from jax.sharding import PartitionSpec as P
 
+
 WIDE = 256
 LANES = 128
 VMEM_GRANT = 16 << 20
@@ -23,7 +24,7 @@
 
 
 def mix_blocks(x_hbm, s_ref, s_copy, x_ref, t_ref, sems):
-    columns, length = x_ref.shape
+    _, length = x_ref.shape
     slabs = length // WIDE // 2
     groups = slabs // 2
     span = 2 * WIDE
@@ -70,7 +71,11 @@
     lax.fori_loop(0, WIDE // 8, butterfly, 0, unroll=4)
 
 
-def gather_blocks(devices, length, columns, base, rows_smem, rows_ref, t_ref, g_ref, out_ref):
+def step_of(k):
+    return (1 << k) | 1
+
+
+def gather_blocks(devices, length, columns, corner, rows_smem, rows_ref, t_ref, g_ref, out_ref):
     per = rows_ref.shape[1]
     half = length // 2
     bits = devices.bit_length() - 1
@@ -79,10 +84,9 @@
     me = lax.axis_index("row")
 
     def gather(i, _):
-        p = base + i
-        dest = (me & -2) ^ (p & 1)
-        for k in range(1, bits):
-            dest = dest ^ (((p >> k) & 1) << (bits - k))
+        dest = me ^ corner
+        for k in range(2, bits):
+            dest = dest ^ (((i >> (bits - 1 - k)) & 1) * step_of(k))
         for t in range(per):
             row = rows_smem[dest * per + t] & (half - 1)
             g_ref[t:t + 1, :] = t_ref[pl.ds(row, 1), :]
@@ -97,11 +101,14 @@
     lax.fori_loop(0, out_ref.shape[0], gather, 0)
 
 
-def mix(matrix_panel, row_signs, sample_rows, devices):
+def corner_of(c0, c1):
+    return c0 * step_of(0) ^ c1 * step_of(1)
+
+
+def mix(matrix_panel, row_signs, sample_rows, devices, corner):
     columns, length = matrix_panel.shape
     per = sample_rows.shape[0] // devices
-    half = devices // 2
-    anywhere = pl.BlockSpec(memory_space=pltpu.HBM)
+    hbm = pl.BlockSpec(memory_space=pltpu.HBM)
 
     def kernel(x_hbm, s_hbm, flat_hbm, rows_hbm, t_ref, out_ref, x_ref, s_ref, flat_ref, rows_ref, g_ref, sems, more):
         fetch = [pltpu.make_async_copy(a, b, more.at[k]) for k, (a, b) in enumerate(((s_hbm, s_ref), (flat_hbm, flat_ref), (rows_hbm, rows_ref)))]
@@ -110,12 +117,12 @@
         mix_blocks(x_hbm, s_ref, fetch[0], x_ref, t_ref, sems)
         fetch[1].wait()
         fetch[2].wait()
-        gather_blocks(devices, length, columns, half, flat_ref, rows_ref, t_ref, g_ref, out_ref)
+        gather_blocks(devices, length, columns, corner, flat_ref, rows_ref, t_ref, g_ref, out_ref)
 
     return pl.pallas_call(
         kernel,
-        out_shape=(pltpu.VMEM((length // 2, LANES), jnp.float32), pltpu.VMEM((half, columns, per), jnp.float32)),
-        in_specs=[anywhere] * 4,
+        out_shape=(pltpu.VMEM((length // 2, LANES), jnp.float32), pltpu.VMEM((devices // 4, columns, per), jnp.float32)),
+        in_specs=[hbm] * 4,
         scratch_shapes=[
             pltpu.VMEM((columns, length), jnp.bfloat16),
             pltpu.VMEM((length // LANES, LANES), jnp.int32),
@@ -129,10 +136,9 @@
     )(*(in_hbm(a) for a in (matrix_panel, row_signs.reshape(length // LANES, LANES), sample_rows, sample_rows.reshape(devices, per))))
 
 
-def pick(table, sample_rows, columns, length, devices):
+def pick(table, sample_rows, columns, length, devices, corner):
     per = sample_rows.shape[0] // devices
-    half = devices // 2
-    anywhere = pl.BlockSpec(memory_space=pltpu.HBM)
+    hbm = pl.BlockSpec(memory_space=pltpu.HBM)
 
     def kernel(t_ref, flat_hbm, rows_hbm, out_ref, flat_ref, rows_ref, g_ref, more):
         fetch = [pltpu.make_async_copy(a, b, more.at[k]) for k, (a, b) in enumerate(((flat_hbm, flat_ref), (rows_hbm, rows_ref)))]
@@ -140,12 +146,12 @@
             copy.start()
         for copy in fetch:
             copy.wait()
-        gather_blocks(devices, length, columns, 0, flat_ref, rows_ref, t_ref, g_ref, out_ref)
+        gather_blocks(devices, length, columns, corner, flat_ref, rows_ref, t_ref, g_ref, out_ref)
 
     return pl.pallas_call(
         kernel,
-        out_shape=pltpu.VMEM((half, columns, per), jnp.float32),
-        in_specs=[pl.BlockSpec(memory_space=pltpu.VMEM), anywhere, anywhere],
+        out_shape=pltpu.VMEM((devices // 4, columns, per), jnp.float32),
+        in_specs=[pl.BlockSpec(memory_space=pltpu.VMEM), hbm, hbm],
         scratch_shapes=[
             pltpu.SMEM(sample_rows.shape, jnp.int32),
             pltpu.VMEM((devices, per), jnp.int32),
@@ -156,17 +162,31 @@
     )(pltpu.with_memory_space_constraint(table, pltpu.VMEM), in_hbm(sample_rows), in_hbm(sample_rows.reshape(devices, per)))
 
 
-def chips(value, bit):
-    size = lax.axis_size("row")
-    return lax.ppermute(value, "row", [(i, i ^ bit) for i in range(1, size, 2)])
-
-
-def up(value):
-    return lax.ppermute(value, "row", [(i, i + 1) for i in range(0, lax.axis_size("row"), 2)])
-
-
-def down(value):
-    return lax.ppermute(value, "row", [(i + 1, i) for i in range(0, lax.axis_size("row"), 2)])
+def products(full, other, everything):
+    blocks, columns, _ = full.shape
+
+    def kernel(a_ref, b_ref, o_ref):
+        own = jnp.zeros((columns, columns), jnp.float32)
+        cross = jnp.zeros((columns, columns), jnp.float32)
+        dims = (((1,), (1,)), ((), ()))
+        for i in range(blocks):
+            own = own + lax.dot_general(a_ref[i], a_ref[i], dims, precision=lax.Precision.HIGHEST)
+            cross = cross + lax.dot_general(a_ref[i], b_ref[i], dims, precision=lax.Precision.HIGHEST)
+        first = lax.axis_index("col") == 0
+        both = jnp.concatenate([jnp.where(first, own, cross), jnp.where(first, cross, own)], axis=1)
+        o_ref[...] = both * (1.0 / everything)
+
+    vmem = pl.BlockSpec(memory_space=pltpu.VMEM)
+    return pl.pallas_call(
+        kernel,
+        out_shape=pltpu.VMEM((columns, 2 * columns), jnp.float32),
+        in_specs=[vmem, vmem],
+        compiler_params=pltpu.CompilerParams(vmem_limit_bytes=VMEM_GRANT),
+    )(pltpu.with_memory_space_constraint(full, pltpu.VMEM), pltpu.with_memory_space_constraint(other, pltpu.VMEM))
+
+
+def swap(value, k):
+    return lax.ppermute(value, "row", [(i, i ^ step_of(k)) for i in range(lax.axis_size("row"))])
 
 
 def body(matrix_panel, row_signs, sample_rows):
@@ -174,32 +194,31 @@
     columns, length = matrix_panel.shape
     everything = sample_rows.shape[0]
     bits = devices.bit_length() - 1
-    odd = (lax.axis_index("row") & 1) == 1
-    table, send = mix(matrix_panel, row_signs, sample_rows, devices)
-    send = send + up(send)
+
+    def part(table, c0, c1):
+        return pick(table, sample_rows, columns, length, devices, corner_of(c0, c1))
+
+    table, far = mix(matrix_panel, row_signs, sample_rows, devices, corner_of(1, 1))
+    send = part(table, 0, 1) + swap(far, 0)
     table, send = lax.optimization_barrier((table, send))
-    moved = chips(send, 2)
-    keep = pick(table, sample_rows, columns, length, devices)
-    total = (keep + up(keep)) + moved
+    moved = swap(send, 1)
+    far = part(table, 1, 0)
+    near = swap(far, 0)
+    table, far = lax.optimization_barrier((table, far))
+    rest = part(table, 0, 0)
+    total = (rest + near) + moved
     for k in range(2, bits - 1):
         half = total.shape[0] // 2
-        total = total[:half] + chips(total[half:], 1 << k)
-    moved = chips(total, 1 << (bits - 1))
-    mine = total[:2] + moved[2:]
-    theirs = total[2:] + moved[:2]
+        total = total[:half] + swap(total[half:], k)
+    moved = swap(total, bits - 1)
+    mine = total[:1] + moved[1:]
+    theirs = total[1:] + moved[:1]
     full = jnp.concatenate([mine, theirs], axis=0)
-    pairs = [((2 * i + 1) * 2 + c, (2 * i + 1) * 2 + 1 - c) for i in range(devices // 2) for c in range(2)]
-    other = lax.ppermute(full, ("row", "col"), pairs)
-    sketch = jnp.where(odd, mine[1], down(mine[0]))
-    own = jnp.einsum("bcs,bds->cd", full, full, precision=lax.Precision.HIGHEST)
-    cross = jnp.einsum("bcs,bds->cd", full, other, precision=lax.Precision.HIGHEST)
-    first = lax.axis_index("col") == 0
-    gram = jnp.concatenate([jnp.where(first, own, cross), jnp.where(first, cross, own)], axis=1)
-    gram = gram / everything
-    for k in range(1, bits - 1):
-        gram = gram + chips(gram, 1 << k)
-    gram = jnp.where(odd, gram, down(gram))
-    return (sketch, gram)
+    other = lax.ppermute(full, "col", [(0, 1), (1, 0)])
+    gram = products(full, other, everything)
+    for k in range(bits - 1):
+        gram = gram + swap(gram, k)
+    return (mine[0], gram)
 
 
 def solution(mesh):

time: 52.6 us -> 39.8 us (0.76)
  waiting for transfers between devices: 26.7 us -> 12.6 us
  Pallas kernels: 8.07 us -> 10.1 us
  other arithmetic: 1.55 us -> 0.69 us
  starting transfers between devices: 14.5 us -> 15.3 us
    ppermute x10 -> x9, waiting for transfers between devices: 26.7 us -> 12.6 us  [the longest x8 10.4 us: swap(): lax.ppermute(value, 'row', [(i, i ^ step_of(k)) for i in range(lax.axis_s...]
    pallas_call x1 -> x4, Pallas kernels: 2.59 us -> 5.49 us  [the longest x3 5.1 us: pick(): pl.pallas_call(kernel, out_shape=pltpu.VMEM((devices // 4, columns, per),...]
    select_n x2 -> x0, other arithmetic: 1.24 us -> none  [the longest x1 0.62 us: body(): sketch = jnp.where(odd, mine[1], down(mine[0]))]
    pallas_call x1, Pallas kernels: 5.48 us -> 4.6 us  [mix(): pl.pallas_call(kernel, out_shape=(pltpu.VMEM((length // 2, LANES), jnp.fl...]
    ppermute x10 -> x9, starting transfers between devices: 14.5 us -> 15.3 us  [the longest x8 13.2 us: swap(): lax.ppermute(value, 'row', [(i, i ^ step_of(k)) for i in range(lax.axis_s...]
  transfers between devices with their start and end apart: 10 -> 9, of which waited for: 4 -> 7; matrix products, arithmetic and copies ran while one was open for 1% -> 0% of each run, Pallas kernels for 5% -> 9%
where the time goes in v3:
time: 39.8 us; the launch traced here: 39.4 us
  starting transfers between devices  15.3 us (38%)
  waiting for transfers between devices  12.6 us (32%)
  Pallas kernels  10.1 us (25%)
  between operations  0.74 us (2%)
  other arithmetic  0.69 us (2%)
    ppermute x8, starting transfers between devices, swap(): lax.ppermute(value, 'row', [(i, i ^ step_of(k)) for i in range(lax.axis_s...  13.2 us
    ppermute x8, waiting for transfers between devices, swap(): lax.ppermute(value, 'row', [(i, i ^ step_of(k)) for i in range(lax.axis_s...  10.4 us
    pallas_call x3, Pallas kernels, pick(): pl.pallas_call(kernel, out_shape=pltpu.VMEM((devices // 4, columns, per),...  5.1 us
    pallas_call x1, Pallas kernels, mix(): pl.pallas_call(kernel, out_shape=(pltpu.VMEM((length // 2, LANES), jnp.fl...  4.6 us
    ppermute x1, waiting for transfers between devices, body(): other = lax.ppermute(full, 'col', [(0, 1), (1, 0)])  2.25 us
    ppermute x1, starting transfers between devices, body(): other = lax.ppermute(full, 'col', [(0, 1), (1, 0)])  2.09 us
  transfers between devices with their start and end apart: 9, of which 7 were waited for; matrix products, arithmetic and copies ran while one was open for 0% of the time, Pallas kernels for 9%

profile of v3, /device:TPU:0, one launch (start us, length us, event | category | flops | bytes accessed | tf_op | source)
XLA Modules:
  0.0 39.4 jit_solution(1547463603550947838)
XLA Ops:
  0.6 4.6 %shard_map.50 = (f32[4096,128]{1,0:T(8,128)S(1)}, f32[4,64,128]{2,1,0:T(8,128)S(1)}) custom-call(bf16[64,8192]{1,0:T(8,128)(2,1)} %x_hbm.1, s32[64,128]{1,0:T(8,128)} %bitcast.8, s32[2048]{0:T(1024)} %flat_hbm.7, s32[16,128]{1,0:T(8,128)} %bitcast.3), custom_call_target="tpu_custom_call" | custom-call | tf_op jit(solution)/shard_map/pallas_call | solution.py:122
  5.2 0.6 %collective-permute-start = (f32[4,64,128]{2,1,0:T(8,128)S(1)}, f32[4,64,128]{2,1,0:T(8,128)S(1)}, u32[]{:S(2)}, u32[]{:S(2)}) collective-permute-start(f32[4,64,128]{2,1,0:T(8,128)S(1)} %get-tuple-element.8), channel_id=1, source_target_pairs={{0,2},{2,0},{4,6},{6,4},{8,10},{10,8},{12,14},{14,12},{16,18},{18,... | collective-permute-start | bytes 393224 | tf_op jit(solution)/shard_map/ppermute | solution.py:189
  5.8 1.7 %shard_map.51 = f32[4,64,128]{2,1,0:T(8,128)S(1)} custom-call(f32[4096,128]{1,0:T(8,128)S(1)} %get-tuple-element.10.t_ref, s32[2048]{0:T(1024)} %flat_hbm.7, s32[16,128]{1,0:T(8,128)} %bitcast.4), custom_call_target="tpu_custom_call" | custom-call | tf_op jit(solution)/shard_map/pallas_call | solution.py:151
  7.5 0.0 collective-permute-done
  7.5 1.7 %shard_map.52 = f32[4,64,128]{2,1,0:T(8,128)S(1)} custom-call(f32[4096,128]{1,0:T(8,128)S(1)} %get-tuple-element.10.t_ref, s32[2048]{0:T(1024)} %flat_hbm.7, s32[16,128]{1,0:T(8,128)} %bitcast.5), custom_call_target="tpu_custom_call" | custom-call | tf_op jit(solution)/shard_map/pallas_call | solution.py:151
  9.2 0.1 collective-permute-start.1
  9.3 2.7 %collective-permute-start.2 = (f32[4,64,128]{2,1,0:T(8,128)S(1)}, f32[4,64,128]{2,1,0:T(8,128)S(1)}, u32[]{:S(2)}, u32[]{:S(2)}) collective-permute-start(f32[4,64,128]{2,1,0:T(8,128)S(1)} %add.27), channel_id=1, source_target_pairs={{0,6},{2,4},{4,2},{6,0},{8,14},{10,12},{12,10},{14,8},{16,22},{18,... | collective-permute-start | bytes 393224 | tf_op jit(solution)/shard_map/ppermute | solution.py:189
  12.0 1.7 %shard_map.53 = f32[4,64,128]{2,1,0:T(8,128)S(1)} custom-call(f32[4096,128]{1,0:T(8,128)S(1)} %get-tuple-element.10.t_ref, s32[2048]{0:T(1024)} %flat_hbm.7, s32[16,128]{1,0:T(8,128)} %bitcast.6), custom_call_target="tpu_custom_call" | custom-call | tf_op jit(solution)/shard_map/pallas_call | solution.py:151
  13.7 0.0 collective-permute-done.1
  13.7 1.9 %collective-permute-done.2 = f32[4,64,128]{2,1,0:T(8,128)S(1)} collective-permute-done((f32[4,64,128]{2,1,0:T(8,128)S(1)}, f32[4,64,128]{2,1,0:T(8,128)S(1)}, u32[]{:S(2)}, u32[]{:S(2)}) %collective-permute-start.2) | collective-permute-done | bytes 131104 | tf_op jit(solution)/shard_map/ppermute | solution.py:189
  15.7 2.1 %collective-permute-start.3 = (f32[2,64,128]{2,1,0:T(8,128)S(1)}, f32[2,64,128]{2,1,0:T(8,128)S(1)}, u32[]{:S(2)}, u32[]{:S(2)}) collective-permute-start(f32[2,64,128]{2,1,0:T(8,128)S(1)} %slice.25), channel_id=1, source_target_pairs={{0,10},{2,8},{4,14},{6,12},{8,2},{10,0},{12,6},{14,4},{16,26},{18,... | collective-permute-start | bytes 196616 | tf_op jit(solution)/shard_map/ppermute | solution.py:189
  17.7 2.2 %collective-permute-done.3 = f32[2,64,128]{2,1,0:T(8,128)S(1)} collective-permute-done((f32[2,64,128]{2,1,0:T(8,128)S(1)}, f32[2,64,128]{2,1,0:T(8,128)S(1)}, u32[]{:S(2)}, u32[]{:S(2)}) %collective-permute-start.3) | collective-permute-done | bytes 65568 | tf_op jit(solution)/shard_map/ppermute | solution.py:189
  19.9 3.0 %collective-permute-start.4 = (f32[2,64,128]{2,1,0:T(8,128)S(1)}, f32[2,64,128]{2,1,0:T(8,128)S(1)}, u32[]{:S(2)}, u32[]{:S(2)}) collective-permute-start(f32[2,64,128]{2,1,0:T(8,128)S(1)} %slice_add_fusion), channel_id=1, source_target_pairs={{0,18},{2,16},{4,22},{6,20},{8,26},{10,24},{12,30},{14,28},{16,2},... | collective-permute-start | bytes 196616 | tf_op jit(solution)/shard_map/ppermute | solution.py:189
  22.9 2.2 %collective-permute-done.4 = f32[2,64,128]{2,1,0:T(8,128)S(1)} collective-permute-done((f32[2,64,128]{2,1,0:T(8,128)S(1)}, f32[2,64,128]{2,1,0:T(8,128)S(1)}, u32[]{:S(2)}, u32[]{:S(2)}) %collective-permute-start.4) | collective-permute-done | bytes 65568 | tf_op jit(solution)/shard_map/ppermute | solution.py:189
  25.1 0.0 copy-start
  25.2 2.1 %collective-permute-start.5 = (f32[2,64,128]{2,1,0:T(8,128)S(1)}, f32[2,64,128]{2,1,0:T(8,128)S(1)}, u32[]{:S(2)}, u32[]{:S(2)}) collective-permute-start(f32[2,64,128]{2,1,0:T(8,128)S(1)} %pad_maximum_fusion.a_ref), channel_id=1, source_target_pairs={{0,1},{1,0},{2,3},{3,2},{4,5},{5,4},{6,7},{7,6},{8,9},{9,8},{10,11... | collective-permute-start | bytes 196616 | tf_op jit(solution)/shard_map/ppermute | solution.py:217
  27.3 2.2 %collective-permute-done.5.b_ref = f32[2,64,128]{2,1,0:T(8,128)S(1)} collective-permute-done((f32[2,64,128]{2,1,0:T(8,128)S(1)}, f32[2,64,128]{2,1,0:T(8,128)S(1)}, u32[]{:S(2)}, u32[]{:S(2)}) %collective-permute-start.5) | collective-permute-done | bytes 65568 | tf_op jit(solution)/shard_map/ppermute | solution.py:217
  29.5 0.4 shard_map.54
  29.9 0.7 %collective-permute-start.6 = (f32[64,128]{1,0:T(8,128)S(1)}, f32[64,128]{1,0:T(8,128)S(1)}, u32[]{:S(2)}, u32[]{:S(2)}) collective-permute-start(f32[64,128]{1,0:T(8,128)S(1)} %shard_map.54), channel_id=1, source_target_pairs={{0,2},{2,0},{4,6},{6,4},{8,10},{10,8},{12,14},{14,12},{16,18},{18,... | collective-permute-start | bytes 98312 | tf_op jit(solution)/shard_map/ppermute | solution.py:189
  30.6 0.9 %collective-permute-done.6 = f32[64,128]{1,0:T(8,128)S(1)} collective-permute-done((f32[64,128]{1,0:T(8,128)S(1)}, f32[64,128]{1,0:T(8,128)S(1)}, u32[]{:S(2)}, u32[]{:S(2)}) %collective-permute-start.6) | collective-permute-done | bytes 32800 | tf_op jit(solution)/shard_map/ppermute | solution.py:189
  31.5 1.8 %collective-permute-start.7 = (f32[64,128]{1,0:T(8,128)S(1)}, f32[64,128]{1,0:T(8,128)S(1)}, u32[]{:S(2)}, u32[]{:S(2)}) collective-permute-start(f32[64,128]{1,0:T(8,128)S(1)} %add.33), channel_id=1, source_target_pairs={{0,6},{2,4},{4,2},{6,0},{8,14},{10,12},{12,10},{14,8},{16,22},{18,... | collective-permute-start | bytes 98312 | tf_op jit(solution)/shard_map/ppermute | solution.py:189
  33.3 1.6 %collective-permute-done.7 = f32[64,128]{1,0:T(8,128)S(1)} collective-permute-done((f32[64,128]{1,0:T(8,128)S(1)}, f32[64,128]{1,0:T(8,128)S(1)}, u32[]{:S(2)}, u32[]{:S(2)}) %collective-permute-start.7) | collective-permute-done | bytes 32800 | tf_op jit(solution)/shard_map/ppermute | solution.py:189
  34.9 2.3 %collective-permute-start.8 = (f32[64,128]{1,0:T(8,128)S(1)}, f32[64,128]{1,0:T(8,128)S(1)}, u32[]{:S(2)}, u32[]{:S(2)}) collective-permute-start(f32[64,128]{1,0:T(8,128)S(1)} %add.34), channel_id=1, source_target_pairs={{0,10},{2,8},{4,14},{6,12},{8,2},{10,0},{12,6},{14,4},{16,26},{18,... | collective-permute-start | bytes 98312 | tf_op jit(solution)/shard_map/ppermute | solution.py:189
  37.2 1.6 %collective-permute-done.8 = f32[64,128]{1,0:T(8,128)S(1)} collective-permute-done((f32[64,128]{1,0:T(8,128)S(1)}, f32[64,128]{1,0:T(8,128)S(1)}, u32[]{:S(2)}, u32[]{:S(2)}) %collective-permute-start.8) | collective-permute-done | bytes 32800 | tf_op jit(solution)/shard_map/ppermute | solution.py:189
  38.8 0.6 %add.35 = f32[64,128]{1,0:T(8,128)} add(f32[64,128]{1,0:T(8,128)S(1)} %add.34, f32[64,128]{1,0:T(8,128)S(1)} %collective-permute-done.8) | non-fusion elementwise | flops 8192 | bytes 98304 | tf_op jit(solution)/shard_map/add | solution.py:220
  39.4 0.0 copy-done
  (8 shorter events, 0.1 us)
Async XLA Ops:
  5.2 2.3 %collective-permute-start = (f32[4,64,128]{2,1,0:T(8,128)S(1)}, f32[4,64,128]{2,1,0:T(8,128)S(1)}, u32[]{:S(2)}, u32[]{:S(2)}) collective-permute-start(f32[4,64,128]{2,1,0:T(8,128)S(1)} %get-tuple-element.8), channel_id=1, source_target_pairs={{0,2},{2,0},{4,6},{6,4},{8,10},{10,8},{12,14},{14,12},{16,18},{18,... | collective-permute-start | bytes 393224 | tf_op jit(solution)/shard_map/ppermute | solution.py:189
  9.2 4.4 %collective-permute-start.1 = (f32[4,64,128]{2,1,0:T(8,128)S(1)}, f32[4,64,128]{2,1,0:T(8,128)S(1)}, u32[]{:S(2)}, u32[]{:S(2)}) collective-permute-start(f32[4,64,128]{2,1,0:T(8,128)S(1)} %shard_map.52), channel_id=1, source_target_pairs={{0,2},{2,0},{4,6},{6,4},{8,10},{10,8},{12,14},{14,12},{16,18},{18,... | collective-permute-start | bytes 393224 | tf_op jit(solution)/shard_map/ppermute | solution.py:189
  9.3 6.3 %collective-permute-start.2 = (f32[4,64,128]{2,1,0:T(8,128)S(1)}, f32[4,64,128]{2,1,0:T(8,128)S(1)}, u32[]{:S(2)}, u32[]{:S(2)}) collective-permute-start(f32[4,64,128]{2,1,0:T(8,128)S(1)} %add.27), channel_id=1, source_target_pairs={{0,6},{2,4},{4,2},{6,0},{8,14},{10,12},{12,10},{14,8},{16,22},{18,... | collective-permute-start | bytes 393224 | tf_op jit(solution)/shard_map/ppermute | solution.py:189
  15.7 4.3 %collective-permute-start.3 = (f32[2,64,128]{2,1,0:T(8,128)S(1)}, f32[2,64,128]{2,1,0:T(8,128)S(1)}, u32[]{:S(2)}, u32[]{:S(2)}) collective-permute-start(f32[2,64,128]{2,1,0:T(8,128)S(1)} %slice.25), channel_id=1, source_target_pairs={{0,10},{2,8},{4,14},{6,12},{8,2},{10,0},{12,6},{14,4},{16,26},{18,... | collective-permute-start | bytes 196616 | tf_op jit(solution)/shard_map/ppermute | solution.py:189
  19.9 5.2 %collective-permute-start.4 = (f32[2,64,128]{2,1,0:T(8,128)S(1)}, f32[2,64,128]{2,1,0:T(8,128)S(1)}, u32[]{:S(2)}, u32[]{:S(2)}) collective-permute-start(f32[2,64,128]{2,1,0:T(8,128)S(1)} %slice_add_fusion), channel_id=1, source_target_pairs={{0,18},{2,16},{4,22},{6,20},{8,26},{10,24},{12,30},{14,28},{16,2},... | collective-permute-start | bytes 196616 | tf_op jit(solution)/shard_map/ppermute | solution.py:189
  25.1 14.3 %copy-start = (f32[1,64,128]{2,1,0:T(8,128)}, f32[1,64,128]{2,1,0:T(8,128)S(1)}, u32[]{:S(2)}) copy-start(f32[1,64,128]{2,1,0:T(8,128)S(1)} %get-tuple-element.13) | copy-start | bytes 98308
  25.2 4.3 %collective-permute-start.5 = (f32[2,64,128]{2,1,0:T(8,128)S(1)}, f32[2,64,128]{2,1,0:T(8,128)S(1)}, u32[]{:S(2)}, u32[]{:S(2)}) collective-permute-start(f32[2,64,128]{2,1,0:T(8,128)S(1)} %pad_maximum_fusion.a_ref), channel_id=1, source_target_pairs={{0,1},{1,0},{2,3},{3,2},{4,5},{5,4},{6,7},{7,6},{8,9},{9,8},{10,11... | collective-permute-start | bytes 196616 | tf_op jit(solution)/shard_map/ppermute | solution.py:217
  29.9 1.6 %collective-permute-start.6 = (f32[64,128]{1,0:T(8,128)S(1)}, f32[64,128]{1,0:T(8,128)S(1)}, u32[]{:S(2)}, u32[]{:S(2)}) collective-permute-start(f32[64,128]{1,0:T(8,128)S(1)} %shard_map.54), channel_id=1, source_target_pairs={{0,2},{2,0},{4,6},{6,4},{8,10},{10,8},{12,14},{14,12},{16,18},{18,... | collective-permute-start | bytes 98312 | tf_op jit(solution)/shard_map/ppermute | solution.py:189
  31.5 3.4 %collective-permute-start.7 = (f32[64,128]{1,0:T(8,128)S(1)}, f32[64,128]{1,0:T(8,128)S(1)}, u32[]{:S(2)}, u32[]{:S(2)}) collective-permute-start(f32[64,128]{1,0:T(8,128)S(1)} %add.33), channel_id=1, source_target_pairs={{0,6},{2,4},{4,2},{6,0},{8,14},{10,12},{12,10},{14,8},{16,22},{18,... | collective-permute-start | bytes 98312 | tf_op jit(solution)/shard_map/ppermute | solution.py:189
  34.9 3.9 %collective-permute-start.8 = (f32[64,128]{1,0:T(8,128)S(1)}, f32[64,128]{1,0:T(8,128)S(1)}, u32[]{:S(2)}, u32[]{:S(2)}) collective-permute-start(f32[64,128]{1,0:T(8,128)S(1)} %add.34), channel_id=1, source_target_pairs={{0,10},{2,8},{4,14},{6,12},{8,2},{10,0},{12,6},{14,4},{16,26},{18,... | collective-permute-start | bytes 98312 | tf_op jit(solution)/shard_map/ppermute | solution.py:189

commit v4 on v3

--- a/solution.py
+++ b/solution.py
@@ -10,10 +10,12 @@
 WIDE = 256
 LANES = 128
 VMEM_GRANT = 16 << 20
-
-
-def in_hbm(value):
-    return pltpu.with_memory_space_constraint(value, pltpu.HBM)
+CHUNKS = 1
+SLOTS = 4
+
+
+def in_space(value, space):
+    return pltpu.with_memory_space_constraint(value, space)
 
 
 def parity(value, bits):
@@ -30,9 +32,10 @@
     span = 2 * WIDE
     half = length // 2
     copies = []
-    for g in range(groups):
+    chunk = groups * span // CHUNKS
+    for g in range(CHUNKS):
         for h in range(2):
-            window = pl.ds(h * half + g * span, span)
+            window = pl.ds(h * half + g * chunk, chunk)
             copies.append(pltpu.make_async_copy(x_hbm.at[:, window], x_ref.at[:, window], sems.at[g, h]))
             copies[-1].start()
     left = lax.broadcasted_iota(jnp.int32, (WIDE, WIDE), 0)
@@ -40,8 +43,10 @@
     mat = (1 - 2 * parity(left & right, WIDE.bit_length() - 1)).astype(jnp.float32).astype(jnp.bfloat16)
     s_copy.wait()
     for g in range(groups):
-        copies[2 * g].wait()
-        copies[2 * g + 1].wait()
+        if g % (groups // CHUNKS) == 0:
+            first = g // (groups // CHUNKS)
+            copies[2 * first].wait()
+            copies[2 * first + 1].wait()
         parts = []
         for q in range(2):
             for h in range(2):
@@ -83,22 +88,26 @@
     scale = float(1.0 / np.sqrt(float(length) * devices))
     me = lax.axis_index("row")
 
-    def gather(i, _):
+    def gather(i, slot):
         dest = me ^ corner
         for k in range(2, bits):
             dest = dest ^ (((i >> (bits - 1 - k)) & 1) * step_of(k))
         for t in range(per):
             row = rows_smem[dest * per + t] & (half - 1)
-            g_ref[t:t + 1, :] = t_ref[pl.ds(row, 1), :]
-        turned = g_ref[...].T
+            g_ref[slot][t:t + 1, :] = t_ref[pl.ds(row, 1), :]
+        turned = g_ref[slot][...].T
         samples = rows_ref[pl.ds(dest, 1), :]
         flip = parity((samples >> (top + 1)) & me, bits)
         first = jnp.where(flip == 1, -scale, scale)
         second = jnp.where((flip ^ ((samples >> top) & 1)) == 1, -scale, scale)
         out_ref[i] = turned[:columns, :] * first + turned[columns:, :] * second
+
+    def several(j, _):
+        for slot in range(SLOTS):
+            gather(j * SLOTS + slot, slot)
         return 0
 
-    lax.fori_loop(0, out_ref.shape[0], gather, 0)
+    lax.fori_loop(0, out_ref.shape[0] // SLOTS, several, 0)
 
 
 def corner_of(c0, c1):
@@ -108,9 +117,10 @@
 def mix(matrix_panel, row_signs, sample_rows, devices, corner):
     columns, length = matrix_panel.shape
     per = sample_rows.shape[0] // devices
-    hbm = pl.BlockSpec(memory_space=pltpu.HBM)
-
-    def kernel(x_hbm, s_hbm, flat_hbm, rows_hbm, t_ref, out_ref, x_ref, s_ref, flat_ref, rows_ref, g_ref, sems, more):
+    hbm, vmem, smem = (pl.BlockSpec(memory_space=m) for m in (pltpu.HBM, pltpu.VMEM, pltpu.SMEM))
+
+    def kernel(x_hbm, s_hbm, flat_hbm, rows_hbm, t_ref, out_ref, flat_ref, rows_ref, x_ref, s_ref, *rest):
+        g_ref, (sems, more) = rest[:SLOTS], rest[SLOTS:]
         fetch = [pltpu.make_async_copy(a, b, more.at[k]) for k, (a, b) in enumerate(((s_hbm, s_ref), (flat_hbm, flat_ref), (rows_hbm, rows_ref)))]
         for copy in fetch:
             copy.start()
@@ -121,45 +131,40 @@
 
     return pl.pallas_call(
         kernel,
-        out_shape=(pltpu.VMEM((length // 2, LANES), jnp.float32), pltpu.VMEM((devices // 4, columns, per), jnp.float32)),
+        out_shape=(
+            pltpu.VMEM((length // 2, LANES), jnp.float32),
+            pltpu.VMEM((devices // 4, columns, per), jnp.float32),
+            pltpu.SMEM(sample_rows.shape, jnp.int32),
+            pltpu.VMEM((devices, per), jnp.int32),
+        ),
         in_specs=[hbm] * 4,
+        out_specs=(vmem, vmem, smem, vmem),
         scratch_shapes=[
             pltpu.VMEM((columns, length), jnp.bfloat16),
             pltpu.VMEM((length // LANES, LANES), jnp.int32),
-            pltpu.SMEM(sample_rows.shape, jnp.int32),
-            pltpu.VMEM((devices, per), jnp.int32),
-            pltpu.VMEM((per, LANES), jnp.float32),
-            pltpu.SemaphoreType.DMA((length // WIDE // 4, 2)),
+            *[pltpu.VMEM((per, LANES), jnp.float32)] * SLOTS,
+            pltpu.SemaphoreType.DMA((CHUNKS, 2)),
             pltpu.SemaphoreType.DMA((3,)),
         ],
         compiler_params=pltpu.CompilerParams(vmem_limit_bytes=VMEM_GRANT),
-    )(*(in_hbm(a) for a in (matrix_panel, row_signs.reshape(length // LANES, LANES), sample_rows, sample_rows.reshape(devices, per))))
-
-
-def pick(table, sample_rows, columns, length, devices, corner):
-    per = sample_rows.shape[0] // devices
-    hbm = pl.BlockSpec(memory_space=pltpu.HBM)
-
-    def kernel(t_ref, flat_hbm, rows_hbm, out_ref, flat_ref, rows_ref, g_ref, more):
-        fetch = [pltpu.make_async_copy(a, b, more.at[k]) for k, (a, b) in enumerate(((flat_hbm, flat_ref), (rows_hbm, rows_ref)))]
-        for copy in fetch:
-            copy.start()
-        for copy in fetch:
-            copy.wait()
+    )(*(in_space(a, pltpu.HBM) for a in (matrix_panel, row_signs.reshape(length // LANES, LANES), sample_rows, sample_rows.reshape(devices, per))))
+
+
+def pick(table, flat, rows, columns, corner):
+    devices, per = rows.shape
+    vmem, smem = pl.BlockSpec(memory_space=pltpu.VMEM), pl.BlockSpec(memory_space=pltpu.SMEM)
+    length = 2 * table.shape[0]
+
+    def kernel(t_ref, flat_ref, rows_ref, out_ref, *g_ref):
         gather_blocks(devices, length, columns, corner, flat_ref, rows_ref, t_ref, g_ref, out_ref)
 
     return pl.pallas_call(
         kernel,
         out_shape=pltpu.VMEM((devices // 4, columns, per), jnp.float32),
-        in_specs=[pl.BlockSpec(memory_space=pltpu.VMEM), hbm, hbm],
-        scratch_shapes=[
-            pltpu.SMEM(sample_rows.shape, jnp.int32),
-            pltpu.VMEM((devices, per), jnp.int32),
-            pltpu.VMEM((per, LANES), jnp.float32),
-            pltpu.SemaphoreType.DMA((2,)),
-        ],
+        in_specs=[vmem, smem, vmem],
+        scratch_shapes=[pltpu.VMEM((per, LANES), jnp.float32)] * SLOTS,
         compiler_params=pltpu.CompilerParams(vmem_limit_bytes=VMEM_GRANT),
-    )(pltpu.with_memory_space_constraint(table, pltpu.VMEM), in_hbm(sample_rows), in_hbm(sample_rows.reshape(devices, per)))
+    )(in_space(table, pltpu.VMEM), in_space(flat, pltpu.SMEM), in_space(rows, pltpu.VMEM))
 
 
 def products(full, other, everything):
@@ -182,7 +187,7 @@
         out_shape=pltpu.VMEM((columns, 2 * columns), jnp.float32),
         in_specs=[vmem, vmem],
         compiler_params=pltpu.CompilerParams(vmem_limit_bytes=VMEM_GRANT),
-    )(pltpu.with_memory_space_constraint(full, pltpu.VMEM), pltpu.with_memory_space_constraint(other, pltpu.VMEM))
+    )(in_space(full, pltpu.VMEM), in_space(other, pltpu.VMEM))
 
 
 def swap(value, k):
@@ -191,14 +196,14 @@
 
 def body(matrix_panel, row_signs, sample_rows):
     devices = lax.axis_size("row")
-    columns, length = matrix_panel.shape
+    columns, _ = matrix_panel.shape
     everything = sample_rows.shape[0]
     bits = devices.bit_length() - 1
 
     def part(table, c0, c1):
-        return pick(table, sample_rows, columns, length, devices, corner_of(c0, c1))
-
-    table, far = mix(matrix_panel, row_signs, sample_rows, devices, corner_of(1, 1))
+        return pick(table, flat, rows, columns, corner_of(c0, c1))
+
+    table, far, flat, rows = mix(matrix_panel, row_signs, sample_rows, devices, corner_of(1, 1))
     send = part(table, 0, 1) + swap(far, 0)
     table, send = lax.optimization_barrier((table, send))
     moved = swap(send, 1)

time: 39.8 us -> 36.6 us (0.920)
  waiting for transfers between devices: 12.6 us -> 21.3 us
  starting transfers between devices: 15.3 us -> 8.51 us
  Pallas kernels: 10.1 us -> 5.19 us
    ppermute x8, waiting for transfers between devices: 10.4 us -> 17 us  [swap(): lax.ppermute(value, 'row', [(i, i ^ step_of(k)) for i in range(lax.axis_s...]
    ppermute x8, starting transfers between devices: 13.2 us -> 8.44 us  [swap(): lax.ppermute(value, 'row', [(i, i ^ step_of(k)) for i in range(lax.axis_s...]
    pallas_call x3, Pallas kernels: 5.1 us -> 2 us  [pick(): pl.pallas_call(kernel, out_shape=pltpu.VMEM((devices // 4, columns, per),...]
    ppermute x1, starting transfers between devices: 2.09 us -> 0.07 us  [body(): other = lax.ppermute(full, 'col', [(0, 1), (1, 0)])]
    ppermute x1, waiting for transfers between devices: 2.25 us -> 4.25 us  [body(): other = lax.ppermute(full, 'col', [(0, 1), (1, 0)])]
    pallas_call x1, Pallas kernels: 4.6 us -> 2.8 us  [mix(): pl.pallas_call(kernel, out_shape=(pltpu.VMEM((length // 2, LANES), jnp.fl...]
  transfers between devices with their start and end apart: 9 -> 9, of which waited for: 7 -> 8; matrix products, arithmetic and copies ran while one was open for 0% -> 0% of each run, Pallas kernels for 9% -> 4%
where the time goes in v4:
time: 36.6 us; the launch traced here: 36.4 us
  waiting for transfers between devices  21.3 us (58%)
  starting transfers between devices  8.51 us (23%)
  Pallas kernels  5.19 us (14%)
  between operations  0.73 us (2%)
  other arithmetic  0.69 us (2%)
    ppermute x8, waiting for transfers between devices, swap(): lax.ppermute(value, 'row', [(i, i ^ step_of(k)) for i in range(lax.axis_s...  17 us
    ppermute x8, starting transfers between devices, swap(): lax.ppermute(value, 'row', [(i, i ^ step_of(k)) for i in range(lax.axis_s...  8.44 us
    ppermute x1, waiting for transfers between devices, body(): other = lax.ppermute(full, 'col', [(0, 1), (1, 0)])  4.25 us
    pallas_call x1, Pallas kernels, mix(): pl.pallas_call(kernel, out_shape=(pltpu.VMEM((length // 2, LANES), jnp.fl...  2.8 us
    pallas_call x3, Pallas kernels, pick(): pl.pallas_call(kernel, out_shape=pltpu.VMEM((devices // 4, columns, per),...  2 us
  transfers between devices with their start and end apart: 9, of which 8 were waited for; matrix products, arithmetic and copies ran while one was open for 0% of the time, Pallas kernels for 4%

profile of v4, /device:TPU:0, one launch (start us, length us, event | category | flops | bytes accessed | tf_op | source)
XLA Modules:
  0.0 36.4 jit_solution(5414159534728057845)
XLA Ops:
  0.6 2.8 %shard_map.50 = (f32[4096,128]{1,0:T(8,128)S(1)}, f32[4,64,128]{2,1,0:T(8,128)S(1)}, s32[2048]{0:T(1024)S(4)}, s32[16,128]{1,0:T(8,128)S(1)}) custom-call(bf16[64,8192]{1,0:T(8,128)(2,1)} %x_hbm.1, s32[64,128]{1,0:T(8,128)} %bitcast.5, s32[2048]{0:T(1024)} %flat_hbm.1, s32[16,128]{1,0:T(8,128)} %bitcast.4), custom_call_target="tpu_custom_call" | custom-call | tf_op jit(solution)/shard_map/pallas_call | solution.py:132
  3.4 0.6 %collective-permute-start = (f32[4,64,128]{2,1,0:T(8,128)S(1)}, f32[4,64,128]{2,1,0:T(8,128)S(1)}, u32[]{:S(2)}, u32[]{:S(2)}) collective-permute-start(f32[4,64,128]{2,1,0:T(8,128)S(1)} %get-tuple-element.12), channel_id=1, source_target_pairs={{0,2},{2,0},{4,6},{6,4},{8,10},{10,8},{12,14},{14,12},{16,18},{18,... | collective-permute-start | bytes 393224 | tf_op jit(solution)/shard_map/ppermute | solution.py:194
  4.0 0.7 %shard_map.51 = f32[4,64,128]{2,1,0:T(8,128)S(1)} custom-call(f32[4096,128]{1,0:T(8,128)S(1)} %get-tuple-element.14.t_ref, s32[2048]{0:T(1024)S(4)} %get-tuple-element.10.flat_ref, s32[16,128]{1,0:T(8,128)S(1)} %get-tuple-element.11.rows_ref), custom_call_target="tpu_custom_call" | custom-call | tf_op jit(solution)/shard_map/pallas_call | solution.py:161
  4.7 0.3 collective-permute-done
  5.0 0.7 %shard_map.52 = f32[4,64,128]{2,1,0:T(8,128)S(1)} custom-call(f32[4096,128]{1,0:T(8,128)S(1)} %get-tuple-element.14.t_ref, s32[2048]{0:T(1024)S(4)} %get-tuple-element.10.flat_ref, s32[16,128]{1,0:T(8,128)S(1)} %get-tuple-element.11.rows_ref), custom_call_target="tpu_custom_call" | custom-call | tf_op jit(solution)/shard_map/pallas_call | solution.py:161
  5.7 0.4 %collective-permute-start.1 = (f32[4,64,128]{2,1,0:T(8,128)S(1)}, f32[4,64,128]{2,1,0:T(8,128)S(1)}, u32[]{:S(2)}, u32[]{:S(2)}) collective-permute-start(f32[4,64,128]{2,1,0:T(8,128)S(1)} %shard_map.52), channel_id=1, source_target_pairs={{0,2},{2,0},{4,6},{6,4},{8,10},{10,8},{12,14},{14,12},{16,18},{18,... | collective-permute-start | bytes 393224 | tf_op jit(solution)/shard_map/ppermute | solution.py:194
  6.1 2.6 %collective-permute-start.2 = (f32[4,64,128]{2,1,0:T(8,128)S(1)}, f32[4,64,128]{2,1,0:T(8,128)S(1)}, u32[]{:S(2)}, u32[]{:S(2)}) collective-permute-start(f32[4,64,128]{2,1,0:T(8,128)S(1)} %add.27), channel_id=1, source_target_pairs={{0,6},{2,4},{4,2},{6,0},{8,14},{10,12},{12,10},{14,8},{16,22},{18,... | collective-permute-start | bytes 393224 | tf_op jit(solution)/shard_map/ppermute | solution.py:194
  8.7 0.6 %shard_map.53 = f32[4,64,128]{2,1,0:T(8,128)S(1)} custom-call(f32[4096,128]{1,0:T(8,128)S(1)} %get-tuple-element.14.t_ref, s32[2048]{0:T(1024)S(4)} %get-tuple-element.10.flat_ref, s32[16,128]{1,0:T(8,128)S(1)} %get-tuple-element.11.rows_ref), custom_call_target="tpu_custom_call" | custom-call | tf_op jit(solution)/shard_map/pallas_call | solution.py:161
  9.4 0.0 collective-permute-done.1
  9.4 3.1 %collective-permute-done.2 = f32[4,64,128]{2,1,0:T(8,128)S(1)} collective-permute-done((f32[4,64,128]{2,1,0:T(8,128)S(1)}, f32[4,64,128]{2,1,0:T(8,128)S(1)}, u32[]{:S(2)}, u32[]{:S(2)}) %collective-permute-start.2) | collective-permute-done | bytes 131104 | tf_op jit(solution)/shard_map/ppermute | solution.py:194
  12.5 1.7 %collective-permute-start.3 = (f32[2,64,128]{2,1,0:T(8,128)S(1)}, f32[2,64,128]{2,1,0:T(8,128)S(1)}, u32[]{:S(2)}, u32[]{:S(2)}) collective-permute-start(f32[2,64,128]{2,1,0:T(8,128)S(1)} %slice.25), channel_id=1, source_target_pairs={{0,10},{2,8},{4,14},{6,12},{8,2},{10,0},{12,6},{14,4},{16,26},{18,... | collective-permute-start | bytes 196616 | tf_op jit(solution)/shard_map/ppermute | solution.py:194
  14.2 2.4 %collective-permute-done.3 = f32[2,64,128]{2,1,0:T(8,128)S(1)} collective-permute-done((f32[2,64,128]{2,1,0:T(8,128)S(1)}, f32[2,64,128]{2,1,0:T(8,128)S(1)}, u32[]{:S(2)}, u32[]{:S(2)}) %collective-permute-start.3) | collective-permute-done | bytes 65568 | tf_op jit(solution)/shard_map/ppermute | solution.py:194
  16.6 2.5 %collective-permute-start.4 = (f32[2,64,128]{2,1,0:T(8,128)S(1)}, f32[2,64,128]{2,1,0:T(8,128)S(1)}, u32[]{:S(2)}, u32[]{:S(2)}) collective-permute-start(f32[2,64,128]{2,1,0:T(8,128)S(1)} %slice_add_fusion), channel_id=1, source_target_pairs={{0,18},{2,16},{4,22},{6,20},{8,26},{10,24},{12,30},{14,28},{16,2},... | collective-permute-start | bytes 196616 | tf_op jit(solution)/shard_map/ppermute | solution.py:194
  19.1 4.0 %collective-permute-done.4 = f32[2,64,128]{2,1,0:T(8,128)S(1)} collective-permute-done((f32[2,64,128]{2,1,0:T(8,128)S(1)}, f32[2,64,128]{2,1,0:T(8,128)S(1)}, u32[]{:S(2)}, u32[]{:S(2)}) %collective-permute-start.4) | collective-permute-done | bytes 65568 | tf_op jit(solution)/shard_map/ppermute | solution.py:194
  23.1 0.0 copy-start
  23.1 0.1 collective-permute-start.5
  23.2 4.3 %collective-permute-done.5.b_ref = f32[2,64,128]{2,1,0:T(8,128)S(1)} collective-permute-done((f32[2,64,128]{2,1,0:T(8,128)S(1)}, f32[2,64,128]{2,1,0:T(8,128)S(1)}, u32[]{:S(2)}, u32[]{:S(2)}) %collective-permute-start.5) | collective-permute-done | bytes 65568 | tf_op jit(solution)/shard_map/ppermute | solution.py:222
  27.4 0.4 %shard_map.54 = f32[64,128]{1,0:T(8,128)S(1)} custom-call(f32[2,64,128]{2,1,0:T(8,128)S(1)} %pad_maximum_fusion.a_ref, f32[2,64,128]{2,1,0:T(8,128)S(1)} %collective-permute-done.5.b_ref), custom_call_target="tpu_custom_call" | custom-call | tf_op jit(solution)/shard_map/pallas_call | solution.py:185
  27.8 0.1 collective-permute-start.6
  27.9 1.2 %collective-permute-done.6 = f32[64,128]{1,0:T(8,128)S(1)} collective-permute-done((f32[64,128]{1,0:T(8,128)S(1)}, f32[64,128]{1,0:T(8,128)S(1)}, u32[]{:S(2)}, u32[]{:S(2)}) %collective-permute-start.6) | collective-permute-done | bytes 32800 | tf_op jit(solution)/shard_map/ppermute | solution.py:194
  29.1 0.0 collective-permute-start.7
  29.1 3.3 %collective-permute-done.7 = f32[64,128]{1,0:T(8,128)S(1)} collective-permute-done((f32[64,128]{1,0:T(8,128)S(1)}, f32[64,128]{1,0:T(8,128)S(1)}, u32[]{:S(2)}, u32[]{:S(2)}) %collective-permute-start.7) | collective-permute-done | bytes 32800 | tf_op jit(solution)/shard_map/ppermute | solution.py:194
  32.4 0.6 %collective-permute-start.8 = (f32[64,128]{1,0:T(8,128)S(1)}, f32[64,128]{1,0:T(8,128)S(1)}, u32[]{:S(2)}, u32[]{:S(2)}) collective-permute-start(f32[64,128]{1,0:T(8,128)S(1)} %add.34), channel_id=1, source_target_pairs={{0,10},{2,8},{4,14},{6,12},{8,2},{10,0},{12,6},{14,4},{16,26},{18,... | collective-permute-start | bytes 98312 | tf_op jit(solution)/shard_map/ppermute | solution.py:194
  33.1 2.7 %collective-permute-done.8 = f32[64,128]{1,0:T(8,128)S(1)} collective-permute-done((f32[64,128]{1,0:T(8,128)S(1)}, f32[64,128]{1,0:T(8,128)S(1)}, u32[]{:S(2)}, u32[]{:S(2)}) %collective-permute-start.8) | collective-permute-done | bytes 32800 | tf_op jit(solution)/shard_map/ppermute | solution.py:194
  35.8 0.6 %add.35 = f32[64,128]{1,0:T(8,128)} add(f32[64,128]{1,0:T(8,128)S(1)} %add.34, f32[64,128]{1,0:T(8,128)S(1)} %collective-permute-done.8) | non-fusion elementwise | flops 8192 | bytes 98304 | tf_op jit(solution)/shard_map/add | solution.py:225
  36.4 0.0 copy-done
  (8 shorter events, 0.1 us)
Async XLA Ops:
  3.4 1.5 %collective-permute-start = (f32[4,64,128]{2,1,0:T(8,128)S(1)}, f32[4,64,128]{2,1,0:T(8,128)S(1)}, u32[]{:S(2)}, u32[]{:S(2)}) collective-permute-start(f32[4,64,128]{2,1,0:T(8,128)S(1)} %get-tuple-element.12), channel_id=1, source_target_pairs={{0,2},{2,0},{4,6},{6,4},{8,10},{10,8},{12,14},{14,12},{16,18},{18,... | collective-permute-start | bytes 393224 | tf_op jit(solution)/shard_map/ppermute | solution.py:194
  5.7 3.7 %collective-permute-start.1 = (f32[4,64,128]{2,1,0:T(8,128)S(1)}, f32[4,64,128]{2,1,0:T(8,128)S(1)}, u32[]{:S(2)}, u32[]{:S(2)}) collective-permute-start(f32[4,64,128]{2,1,0:T(8,128)S(1)} %shard_map.52), channel_id=1, source_target_pairs={{0,2},{2,0},{4,6},{6,4},{8,10},{10,8},{12,14},{14,12},{16,18},{18,... | collective-permute-start | bytes 393224 | tf_op jit(solution)/shard_map/ppermute | solution.py:194
  6.1 6.3 %collective-permute-start.2 = (f32[4,64,128]{2,1,0:T(8,128)S(1)}, f32[4,64,128]{2,1,0:T(8,128)S(1)}, u32[]{:S(2)}, u32[]{:S(2)}) collective-permute-start(f32[4,64,128]{2,1,0:T(8,128)S(1)} %add.27), channel_id=1, source_target_pairs={{0,6},{2,4},{4,2},{6,0},{8,14},{10,12},{12,10},{14,8},{16,22},{18,... | collective-permute-start | bytes 393224 | tf_op jit(solution)/shard_map/ppermute | solution.py:194
  12.5 4.1 %collective-permute-start.3 = (f32[2,64,128]{2,1,0:T(8,128)S(1)}, f32[2,64,128]{2,1,0:T(8,128)S(1)}, u32[]{:S(2)}, u32[]{:S(2)}) collective-permute-start(f32[2,64,128]{2,1,0:T(8,128)S(1)} %slice.25), channel_id=1, source_target_pairs={{0,10},{2,8},{4,14},{6,12},{8,2},{10,0},{12,6},{14,4},{16,26},{18,... | collective-permute-start | bytes 196616 | tf_op jit(solution)/shard_map/ppermute | solution.py:194
  16.6 6.4 %collective-permute-start.4 = (f32[2,64,128]{2,1,0:T(8,128)S(1)}, f32[2,64,128]{2,1,0:T(8,128)S(1)}, u32[]{:S(2)}, u32[]{:S(2)}) collective-permute-start(f32[2,64,128]{2,1,0:T(8,128)S(1)} %slice_add_fusion), channel_id=1, source_target_pairs={{0,18},{2,16},{4,22},{6,20},{8,26},{10,24},{12,30},{14,28},{16,2},... | collective-permute-start | bytes 196616 | tf_op jit(solution)/shard_map/ppermute | solution.py:194
  23.1 13.4 %copy-start = (f32[1,64,128]{2,1,0:T(8,128)}, f32[1,64,128]{2,1,0:T(8,128)S(1)}, u32[]{:S(2)}) copy-start(f32[1,64,128]{2,1,0:T(8,128)S(1)} %get-tuple-element.17) | copy-start | bytes 98308
  23.1 4.3 %collective-permute-start.5 = (f32[2,64,128]{2,1,0:T(8,128)S(1)}, f32[2,64,128]{2,1,0:T(8,128)S(1)}, u32[]{:S(2)}, u32[]{:S(2)}) collective-permute-start(f32[2,64,128]{2,1,0:T(8,128)S(1)} %pad_maximum_fusion.a_ref), channel_id=1, source_target_pairs={{0,1},{1,0},{2,3},{3,2},{4,5},{5,4},{6,7},{7,6},{8,9},{9,8},{10,11... | collective-permute-start | bytes 196616 | tf_op jit(solution)/shard_map/ppermute | solution.py:222
  27.8 1.3 %collective-permute-start.6 = (f32[64,128]{1,0:T(8,128)S(1)}, f32[64,128]{1,0:T(8,128)S(1)}, u32[]{:S(2)}, u32[]{:S(2)}) collective-permute-start(f32[64,128]{1,0:T(8,128)S(1)} %shard_map.54), channel_id=1, source_target_pairs={{0,2},{2,0},{4,6},{6,4},{8,10},{10,8},{12,14},{14,12},{16,18},{18,... | collective-permute-start | bytes 98312 | tf_op jit(solution)/shard_map/ppermute | solution.py:194
  29.1 3.3 %collective-permute-start.7 = (f32[64,128]{1,0:T(8,128)S(1)}, f32[64,128]{1,0:T(8,128)S(1)}, u32[]{:S(2)}, u32[]{:S(2)}) collective-permute-start(f32[64,128]{1,0:T(8,128)S(1)} %add.33), channel_id=1, source_target_pairs={{0,6},{2,4},{4,2},{6,0},{8,14},{10,12},{12,10},{14,8},{16,22},{18,... | collective-permute-start | bytes 98312 | tf_op jit(solution)/shard_map/ppermute | solution.py:194
  32.4 3.3 %collective-permute-start.8 = (f32[64,128]{1,0:T(8,128)S(1)}, f32[64,128]{1,0:T(8,128)S(1)}, u32[]{:S(2)}, u32[]{:S(2)}) collective-permute-start(f32[64,128]{1,0:T(8,128)S(1)} %add.34), channel_id=1, source_target_pairs={{0,10},{2,8},{4,14},{6,12},{8,2},{10,0},{12,6},{14,4},{16,26},{18,... | collective-permute-start | bytes 98312 | tf_op jit(solution)/shard_map/ppermute | solution.py:194

commit v5 on v4

--- a/solution.py
+++ b/solution.py
@@ -167,27 +167,37 @@
     )(in_space(table, pltpu.VMEM), in_space(flat, pltpu.SMEM), in_space(rows, pltpu.VMEM))
 
 
-def products(full, other, everything):
-    blocks, columns, _ = full.shape
-
-    def kernel(a_ref, b_ref, o_ref):
-        own = jnp.zeros((columns, columns), jnp.float32)
-        cross = jnp.zeros((columns, columns), jnp.float32)
-        dims = (((1,), (1,)), ((), ()))
-        for i in range(blocks):
-            own = own + lax.dot_general(a_ref[i], a_ref[i], dims, precision=lax.Precision.HIGHEST)
-            cross = cross + lax.dot_general(a_ref[i], b_ref[i], dims, precision=lax.Precision.HIGHEST)
+def times(left, right):
+    return lax.dot_general(left, right, (((1,), (1,)), ((), ())), precision=lax.Precision.HIGHEST)
+
+
+def on_chip(kernel, shape, *operands):
+    return pl.pallas_call(
+        kernel,
+        out_shape=pltpu.VMEM(shape, jnp.float32),
+        in_specs=[pl.BlockSpec(memory_space=pltpu.VMEM)] * len(operands),
+        compiler_params=pltpu.CompilerParams(vmem_limit_bytes=VMEM_GRANT),
+    )(*(in_space(a, pltpu.VMEM) for a in operands))
+
+
+def square(mine):
+    def kernel(a_ref, o_ref):
+        o_ref[...] = times(a_ref[...], a_ref[...])
+
+    return on_chip(kernel, (mine.shape[0], mine.shape[0]), mine)
+
+
+def products(own, mine, theirs, other_mine, other_theirs, everything):
+    columns = mine.shape[0]
+
+    def kernel(own_ref, a_ref, b_ref, c_ref, d_ref, o_ref):
+        own = own_ref[...] + times(b_ref[...], b_ref[...])
+        cross = times(a_ref[...], c_ref[...]) + times(b_ref[...], d_ref[...])
         first = lax.axis_index("col") == 0
         both = jnp.concatenate([jnp.where(first, own, cross), jnp.where(first, cross, own)], axis=1)
         o_ref[...] = both * (1.0 / everything)
 
-    vmem = pl.BlockSpec(memory_space=pltpu.VMEM)
-    return pl.pallas_call(
-        kernel,
-        out_shape=pltpu.VMEM((columns, 2 * columns), jnp.float32),
-        in_specs=[vmem, vmem],
-        compiler_params=pltpu.CompilerParams(vmem_limit_bytes=VMEM_GRANT),
-    )(in_space(full, pltpu.VMEM), in_space(other, pltpu.VMEM))
+    return on_chip(kernel, (columns, 2 * columns), own, mine, theirs, other_mine, other_theirs)
 
 
 def swap(value, k):
@@ -206,24 +216,41 @@
     table, far, flat, rows = mix(matrix_panel, row_signs, sample_rows, devices, corner_of(1, 1))
     send = part(table, 0, 1) + swap(far, 0)
     table, send = lax.optimization_barrier((table, send))
-    moved = swap(send, 1)
+    half = send.shape[0] // 2
+    first = swap(send[half:], 1)
+    second = swap(send[:half], 1)
     far = part(table, 1, 0)
     near = swap(far, 0)
     table, far = lax.optimization_barrier((table, far))
     rest = part(table, 0, 0)
-    total = (rest + near) + moved
+    keep = rest + near
     for k in range(2, bits - 1):
-        half = total.shape[0] // 2
-        total = total[:half] + swap(total[half:], k)
-    moved = swap(total, bits - 1)
-    mine = total[:1] + moved[1:]
-    theirs = total[1:] + moved[:1]
-    full = jnp.concatenate([mine, theirs], axis=0)
-    other = lax.ppermute(full, "col", [(0, 1), (1, 0)])
-    gram = products(full, other, everything)
+        send = keep[half:] + first
+        send, low = lax.optimization_barrier((send, keep[:half]))
+        half = half // 2
+        if k < bits - 2:
+            first, later = swap(send[half:], k), swap(send[:half], k)
+            keep = low + second
+            second = later
+        else:
+            moved = swap(send, k)
+            keep = low + second
+    theirs = keep[1] + moved[1]
+    mine = keep[0] + moved[0]
+    theirs, mine = lax.optimization_barrier((theirs, mine))
+    around = [(0, 1), (1, 0)]
+    first = swap(theirs, bits - 1)
+    second = swap(mine, bits - 1)
+    mine = mine + first
+    mine, theirs = lax.optimization_barrier((mine, theirs))
+    theirs = theirs + second
+    other_mine = lax.ppermute(mine, "col", around)
+    own = square(mine)
+    other_theirs = lax.ppermute(theirs, "col", around)
+    gram = products(own, mine, theirs, other_mine, other_theirs, everything)
     for k in range(bits - 1):
         gram = gram + swap(gram, k)
-    return (mine[0], gram)
+    return (mine, gram)
 
 
 def solution(mesh):

time: 36.6 us -> 36.9 us (level)
  starting transfers between devices: 8.51 us -> 13.4 us
  waiting for transfers between devices: 21.3 us -> 16.6 us
    ppermute x8 -> x10, waiting for transfers between devices: 17 us -> 13.4 us  [swap(): lax.ppermute(value, 'row', [(i, i ^ step_of(k)) for i in range(lax.axis_s...]
    ppermute x8 -> x10, starting transfers between devices: 8.44 us -> 11.4 us  [swap(): lax.ppermute(value, 'row', [(i, i ^ step_of(k)) for i in range(lax.axis_s...]
    ppermute x1 -> x2, starting transfers between devices: 0.07 us -> 2.03 us  [the longest x1 1.52 us: body(): other_theirs = lax.ppermute(theirs, 'col', around)]
    ppermute x1 -> x2, waiting for transfers between devices: 4.25 us -> 3.24 us  [the longest x1 1.72 us: body(): other_theirs = lax.ppermute(theirs, 'col', around)]
  transfers between devices with their start and end apart: 9 -> 12, of which waited for: 8 -> 10; matrix products, arithmetic and copies ran while one was open for 0% -> 0% of each run, Pallas kernels for 4% -> 4%
where the time goes in v5:
time: 36.9 us; the launch traced here: 36.8 us
  waiting for transfers between devices  16.6 us (45%)
  starting transfers between devices  13.4 us (36%)
  Pallas kernels  5.32 us (14%)
  other arithmetic  0.71 us (2%)
  between operations  0.7 us (2%)
    ppermute x10, waiting for transfers between devices, swap(): lax.ppermute(value, 'row', [(i, i ^ step_of(k)) for i in range(lax.axis_s...  13.4 us
    ppermute x10, starting transfers between devices, swap(): lax.ppermute(value, 'row', [(i, i ^ step_of(k)) for i in range(lax.axis_s...  11.4 us
    pallas_call x1, Pallas kernels, mix(): pl.pallas_call(kernel, out_shape=(pltpu.VMEM((length // 2, LANES), jnp.fl...  2.8 us
    pallas_call x3, Pallas kernels, pick(): pl.pallas_call(kernel, out_shape=pltpu.VMEM((devices // 4, columns, per),...  2 us
    ppermute x1, waiting for transfers between devices, body(): other_theirs = lax.ppermute(theirs, 'col', around)  1.72 us
    ppermute x1, starting transfers between devices, body(): other_theirs = lax.ppermute(theirs, 'col', around)  1.52 us
    ppermute x1, waiting for transfers between devices, body(): other_mine = lax.ppermute(mine, 'col', around)  1.52 us
  transfers between devices with their start and end apart: 12, of which 10 were waited for; matrix products, arithmetic and copies ran while one was open for 0% of the time, Pallas kernels for 4%

profile of v5, /device:TPU:0, one launch (start us, length us, event | category | flops | bytes accessed | tf_op | source)
XLA Modules:
  0.0 36.8 jit_solution(836538897687990028)
XLA Ops:
  0.6 2.8 %shard_map.50 = (f32[4096,128]{1,0:T(8,128)S(1)}, f32[4,64,128]{2,1,0:T(8,128)S(1)}, s32[2048]{0:T(1024)S(4)}, s32[16,128]{1,0:T(8,128)S(1)}) custom-call(bf16[64,8192]{1,0:T(8,128)(2,1)} %x_hbm.1, s32[64,128]{1,0:T(8,128)} %bitcast.7, s32[2048]{0:T(1024)} %flat_hbm.1, s32[16,128]{1,0:T(8,128)} %bitcast.6), custom_call_target="tpu_custom_call" | custom-call | tf_op jit(solution)/shard_map/pallas_call | solution.py:132
  3.4 0.6 %collective-permute-start = (f32[4,64,128]{2,1,0:T(8,128)S(1)}, f32[4,64,128]{2,1,0:T(8,128)S(1)}, u32[]{:S(2)}, u32[]{:S(2)}) collective-permute-start(f32[4,64,128]{2,1,0:T(8,128)S(1)} %get-tuple-element.18), channel_id=1, source_target_pairs={{0,2},{2,0},{4,6},{6,4},{8,10},{10,8},{12,14},{14,12},{16,18},{18,... | collective-permute-start | bytes 393224 | tf_op jit(solution)/shard_map/ppermute | solution.py:204
  4.0 0.7 %shard_map.51 = f32[4,64,128]{2,1,0:T(8,128)S(1)} custom-call(f32[4096,128]{1,0:T(8,128)S(1)} %get-tuple-element.20.t_ref, s32[2048]{0:T(1024)S(4)} %get-tuple-element.16.flat_ref, s32[16,128]{1,0:T(8,128)S(1)} %get-tuple-element.17.rows_ref), custom_call_target="tpu_custom_call" | custom-call | tf_op jit(solution)/shard_map/pallas_call | solution.py:161
  4.7 0.3 collective-permute-done
  5.0 0.7 %shard_map.52 = f32[4,64,128]{2,1,0:T(8,128)S(1)} custom-call(f32[4096,128]{1,0:T(8,128)S(1)} %get-tuple-element.20.t_ref, s32[2048]{0:T(1024)S(4)} %get-tuple-element.16.flat_ref, s32[16,128]{1,0:T(8,128)S(1)} %get-tuple-element.17.rows_ref), custom_call_target="tpu_custom_call" | custom-call | tf_op jit(solution)/shard_map/pallas_call | solution.py:161
  5.7 0.4 %collective-permute-start.1 = (f32[4,64,128]{2,1,0:T(8,128)S(1)}, f32[4,64,128]{2,1,0:T(8,128)S(1)}, u32[]{:S(2)}, u32[]{:S(2)}) collective-permute-start(f32[4,64,128]{2,1,0:T(8,128)S(1)} %shard_map.52), channel_id=1, source_target_pairs={{0,2},{2,0},{4,6},{6,4},{8,10},{10,8},{12,14},{14,12},{16,18},{18,... | collective-permute-start | bytes 393224 | tf_op jit(solution)/shard_map/ppermute | solution.py:204
  6.1 2.7 %collective-permute-start.2 = (f32[2,64,128]{2,1,0:T(8,128)S(1)}, f32[2,64,128]{2,1,0:T(8,128)S(1)}, u32[]{:S(2)}, u32[]{:S(2)}) collective-permute-start(f32[2,64,128]{2,1,0:T(8,128)S(1)} %get-tuple-element.31), channel_id=1, source_target_pairs={{0,6},{2,4},{4,2},{6,0},{8,14},{10,12},{12,10},{14,8},{16,22},{18,... | collective-permute-start | bytes 196616 | tf_op jit(solution)/shard_map/ppermute | solution.py:204
  8.8 0.1 collective-permute-start.3
  8.9 0.6 %shard_map.53 = f32[4,64,128]{2,1,0:T(8,128)S(1)} custom-call(f32[4096,128]{1,0:T(8,128)S(1)} %get-tuple-element.20.t_ref, s32[2048]{0:T(1024)S(4)} %get-tuple-element.16.flat_ref, s32[16,128]{1,0:T(8,128)S(1)} %get-tuple-element.17.rows_ref), custom_call_target="tpu_custom_call" | custom-call | tf_op jit(solution)/shard_map/pallas_call | solution.py:161
  9.5 0.0 collective-permute-done.1
  9.5 1.7 %collective-permute-done.2 = f32[2,64,128]{2,1,0:T(8,128)S(1)} collective-permute-done((f32[2,64,128]{2,1,0:T(8,128)S(1)}, f32[2,64,128]{2,1,0:T(8,128)S(1)}, u32[]{:S(2)}, u32[]{:S(2)}) %collective-permute-start.2) | collective-permute-done | bytes 65568 | tf_op jit(solution)/shard_map/ppermute | solution.py:204
  11.3 1.5 %collective-permute-start.4 = (f32[2,64,128]{2,1,0:T(8,128)S(1)}, f32[2,64,128]{2,1,0:T(8,128)S(1)}, u32[]{:S(2)}, u32[]{:S(2)}) collective-permute-start(f32[2,64,128]{2,1,0:T(8,128)S(1)} %get-tuple-element.23), channel_id=1, source_target_pairs={{0,10},{2,8},{4,14},{6,12},{8,2},{10,0},{12,6},{14,4},{16,26},{18,... | collective-permute-start | bytes 196616 | tf_op jit(solution)/shard_map/ppermute | solution.py:204
  12.8 0.0 collective-permute-done.3
  12.9 2.7 %collective-permute-done.4 = f32[2,64,128]{2,1,0:T(8,128)S(1)} collective-permute-done((f32[2,64,128]{2,1,0:T(8,128)S(1)}, f32[2,64,128]{2,1,0:T(8,128)S(1)}, u32[]{:S(2)}, u32[]{:S(2)}) %collective-permute-start.4) | collective-permute-done | bytes 65568 | tf_op jit(solution)/shard_map/ppermute | solution.py:204
  15.6 2.3 %collective-permute-start.5 = (f32[64,128]{1,0:T(8,128)S(1)}, f32[64,128]{1,0:T(8,128)S(1)}, u32[]{:S(2)}, u32[]{:S(2)}) collective-permute-start(f32[64,128]{1,0:T(8,128)S(1)} %get-tuple-element.27), channel_id=1, source_target_pairs={{0,18},{2,16},{4,22},{6,20},{8,26},{10,24},{12,30},{14,28},{16,2},... | collective-permute-start | bytes 98312 | tf_op jit(solution)/shard_map/ppermute | solution.py:204
  17.8 0.5 %collective-permute-start.6 = (f32[64,128]{1,0:T(8,128)S(1)}, f32[64,128]{1,0:T(8,128)S(1)}, u32[]{:S(2)}, u32[]{:S(2)}) collective-permute-start(f32[64,128]{1,0:T(8,128)S(1)} %get-tuple-element.24), channel_id=1, source_target_pairs={{0,18},{2,16},{4,22},{6,20},{8,26},{10,24},{12,30},{14,28},{16,2},... | collective-permute-start | bytes 98312 | tf_op jit(solution)/shard_map/ppermute | solution.py:204
  18.3 1.6 %collective-permute-done.5 = f32[64,128]{1,0:T(8,128)S(1)} collective-permute-done((f32[64,128]{1,0:T(8,128)S(1)}, f32[64,128]{1,0:T(8,128)S(1)}, u32[]{:S(2)}, u32[]{:S(2)}) %collective-permute-start.5) | collective-permute-done | bytes 32800 | tf_op jit(solution)/shard_map/ppermute | solution.py:204
  19.9 0.0 copy-start
  20.0 2.1 %collective-permute-done.6 = f32[64,128]{1,0:T(8,128)S(1)} collective-permute-done((f32[64,128]{1,0:T(8,128)S(1)}, f32[64,128]{1,0:T(8,128)S(1)}, u32[]{:S(2)}, u32[]{:S(2)}) %collective-permute-start.6) | collective-permute-done | bytes 32800 | tf_op jit(solution)/shard_map/ppermute | solution.py:204
  22.1 1.5 %collective-permute-start.8 = (f32[64,128]{1,0:T(8,128)S(1)}, f32[64,128]{1,0:T(8,128)S(1)}, u32[]{:S(2)}, u32[]{:S(2)}) collective-permute-start(f32[64,128]{1,0:T(8,128)S(1)} %add.48.b_ref), channel_id=1, source_target_pairs={{0,1},{1,0},{2,3},{3,2},{4,5},{5,4},{6,7},{7,6},{8,9},{9,8},{10,11... | collective-permute-start | bytes 98312 | tf_op jit(solution)/shard_map/ppermute | solution.py:249
  23.6 0.5 %collective-permute-start.7 = (f32[64,128]{1,0:T(8,128)S(1)}, f32[64,128]{1,0:T(8,128)S(1)}, u32[]{:S(2)}, u32[]{:S(2)}) collective-permute-start(f32[64,128]{1,0:T(8,128)S(1)} %add.47.a_ref), channel_id=1, source_target_pairs={{0,1},{1,0},{2,3},{3,2},{4,5},{5,4},{6,7},{7,6},{8,9},{9,8},{10,11... | collective-permute-start | bytes 98312 | tf_op jit(solution)/shard_map/ppermute | solution.py:247
  24.1 0.2 shard_map.54.own_ref
  24.3 1.7 %collective-permute-done.8.d_ref = f32[64,128]{1,0:T(8,128)S(1)} collective-permute-done((f32[64,128]{1,0:T(8,128)S(1)}, f32[64,128]{1,0:T(8,128)S(1)}, u32[]{:S(2)}, u32[]{:S(2)}) %collective-permute-start.8) | collective-permute-done | bytes 32800 | tf_op jit(solution)/shard_map/ppermute | solution.py:249
  26.0 1.5 %collective-permute-done.7.c_ref = f32[64,128]{1,0:T(8,128)S(1)} collective-permute-done((f32[64,128]{1,0:T(8,128)S(1)}, f32[64,128]{1,0:T(8,128)S(1)}, u32[]{:S(2)}, u32[]{:S(2)}) %collective-permute-start.7) | collective-permute-done | bytes 32800 | tf_op jit(solution)/shard_map/ppermute | solution.py:247
  27.5 0.4 shard_map.55
  27.9 0.1 collective-permute-start.9
  27.9 1.2 %collective-permute-done.9 = f32[64,128]{1,0:T(8,128)S(1)} collective-permute-done((f32[64,128]{1,0:T(8,128)S(1)}, f32[64,128]{1,0:T(8,128)S(1)}, u32[]{:S(2)}, u32[]{:S(2)}) %collective-permute-start.9) | collective-permute-done | bytes 32800 | tf_op jit(solution)/shard_map/ppermute | solution.py:204
  29.1 2.1 %collective-permute-start.10 = (f32[64,128]{1,0:T(8,128)S(1)}, f32[64,128]{1,0:T(8,128)S(1)}, u32[]{:S(2)}, u32[]{:S(2)}) collective-permute-start(f32[64,128]{1,0:T(8,128)S(1)} %add.49), channel_id=1, source_target_pairs={{0,6},{2,4},{4,2},{6,0},{8,14},{10,12},{12,10},{14,8},{16,22},{18,... | collective-permute-start | bytes 98312 | tf_op jit(solution)/shard_map/ppermute | solution.py:204
  31.2 1.6 %collective-permute-done.10 = f32[64,128]{1,0:T(8,128)S(1)} collective-permute-done((f32[64,128]{1,0:T(8,128)S(1)}, f32[64,128]{1,0:T(8,128)S(1)}, u32[]{:S(2)}, u32[]{:S(2)}) %collective-permute-start.10) | collective-permute-done | bytes 32800 | tf_op jit(solution)/shard_map/ppermute | solution.py:204
  32.8 1.3 %collective-permute-start.11 = (f32[64,128]{1,0:T(8,128)S(1)}, f32[64,128]{1,0:T(8,128)S(1)}, u32[]{:S(2)}, u32[]{:S(2)}) collective-permute-start(f32[64,128]{1,0:T(8,128)S(1)} %add.50), channel_id=1, source_target_pairs={{0,10},{2,8},{4,14},{6,12},{8,2},{10,0},{12,6},{14,4},{16,26},{18,... | collective-permute-start | bytes 98312 | tf_op jit(solution)/shard_map/ppermute | solution.py:204
  34.1 2.0 %collective-permute-done.11 = f32[64,128]{1,0:T(8,128)S(1)} collective-permute-done((f32[64,128]{1,0:T(8,128)S(1)}, f32[64,128]{1,0:T(8,128)S(1)}, u32[]{:S(2)}, u32[]{:S(2)}) %collective-permute-start.11) | collective-permute-done | bytes 32800 | tf_op jit(solution)/shard_map/ppermute | solution.py:204
  36.2 0.6 %add.51 = f32[64,128]{1,0:T(8,128)} add(f32[64,128]{1,0:T(8,128)S(1)} %add.50, f32[64,128]{1,0:T(8,128)S(1)} %collective-permute-done.11) | non-fusion elementwise | flops 8192 | bytes 98304 | tf_op jit(solution)/shard_map/add | solution.py:252
  36.8 0.0 copy-done
  (10 shorter events, 0.1 us)
Async XLA Ops:
  3.4 1.5 %collective-permute-start = (f32[4,64,128]{2,1,0:T(8,128)S(1)}, f32[4,64,128]{2,1,0:T(8,128)S(1)}, u32[]{:S(2)}, u32[]{:S(2)}) collective-permute-start(f32[4,64,128]{2,1,0:T(8,128)S(1)} %get-tuple-element.18), channel_id=1, source_target_pairs={{0,2},{2,0},{4,6},{6,4},{8,10},{10,8},{12,14},{14,12},{16,18},{18,... | collective-permute-start | bytes 393224 | tf_op jit(solution)/shard_map/ppermute | solution.py:204
  5.7 3.8 %collective-permute-start.1 = (f32[4,64,128]{2,1,0:T(8,128)S(1)}, f32[4,64,128]{2,1,0:T(8,128)S(1)}, u32[]{:S(2)}, u32[]{:S(2)}) collective-permute-start(f32[4,64,128]{2,1,0:T(8,128)S(1)} %shard_map.52), channel_id=1, source_target_pairs={{0,2},{2,0},{4,6},{6,4},{8,10},{10,8},{12,14},{14,12},{16,18},{18,... | collective-permute-start | bytes 393224 | tf_op jit(solution)/shard_map/ppermute | solution.py:204
  6.1 5.1 %collective-permute-start.2 = (f32[2,64,128]{2,1,0:T(8,128)S(1)}, f32[2,64,128]{2,1,0:T(8,128)S(1)}, u32[]{:S(2)}, u32[]{:S(2)}) collective-permute-start(f32[2,64,128]{2,1,0:T(8,128)S(1)} %get-tuple-element.31), channel_id=1, source_target_pairs={{0,6},{2,4},{4,2},{6,0},{8,14},{10,12},{12,10},{14,8},{16,22},{18,... | collective-permute-start | bytes 196616 | tf_op jit(solution)/shard_map/ppermute | solution.py:204
  8.8 4.1 %collective-permute-start.3 = (f32[2,64,128]{2,1,0:T(8,128)S(1)}, f32[2,64,128]{2,1,0:T(8,128)S(1)}, u32[]{:S(2)}, u32[]{:S(2)}) collective-permute-start(f32[2,64,128]{2,1,0:T(8,128)S(1)} %get-tuple-element.30), channel_id=1, source_target_pairs={{0,6},{2,4},{4,2},{6,0},{8,14},{10,12},{12,10},{14,8},{16,22},{18,... | collective-permute-start | bytes 196616 | tf_op jit(solution)/shard_map/ppermute | solution.py:204
  11.3 4.3 %collective-permute-start.4 = (f32[2,64,128]{2,1,0:T(8,128)S(1)}, f32[2,64,128]{2,1,0:T(8,128)S(1)}, u32[]{:S(2)}, u32[]{:S(2)}) collective-permute-start(f32[2,64,128]{2,1,0:T(8,128)S(1)} %get-tuple-element.23), channel_id=1, source_target_pairs={{0,10},{2,8},{4,14},{6,12},{8,2},{10,0},{12,6},{14,4},{16,26},{18,... | collective-permute-start | bytes 196616 | tf_op jit(solution)/shard_map/ppermute | solution.py:204
  15.6 4.4 %collective-permute-start.5 = (f32[64,128]{1,0:T(8,128)S(1)}, f32[64,128]{1,0:T(8,128)S(1)}, u32[]{:S(2)}, u32[]{:S(2)}) collective-permute-start(f32[64,128]{1,0:T(8,128)S(1)} %get-tuple-element.27), channel_id=1, source_target_pairs={{0,18},{2,16},{4,22},{6,20},{8,26},{10,24},{12,30},{14,28},{16,2},... | collective-permute-start | bytes 98312 | tf_op jit(solution)/shard_map/ppermute | solution.py:204
  17.8 4.2 %collective-permute-start.6 = (f32[64,128]{1,0:T(8,128)S(1)}, f32[64,128]{1,0:T(8,128)S(1)}, u32[]{:S(2)}, u32[]{:S(2)}) collective-permute-start(f32[64,128]{1,0:T(8,128)S(1)} %get-tuple-element.24), channel_id=1, source_target_pairs={{0,18},{2,16},{4,22},{6,20},{8,26},{10,24},{12,30},{14,28},{16,2},... | collective-permute-start | bytes 98312 | tf_op jit(solution)/shard_map/ppermute | solution.py:204
  19.9 16.8 %copy-start = (f32[64,128]{1,0:T(8,128)}, f32[64,128]{1,0:T(8,128)S(1)}, u32[]{:S(2)}) copy-start(f32[64,128]{1,0:T(8,128)S(1)} %add.47.a_ref) | copy-start | bytes 98308
  22.1 3.9 %collective-permute-start.8 = (f32[64,128]{1,0:T(8,128)S(1)}, f32[64,128]{1,0:T(8,128)S(1)}, u32[]{:S(2)}, u32[]{:S(2)}) collective-permute-start(f32[64,128]{1,0:T(8,128)S(1)} %add.48.b_ref), channel_id=1, source_target_pairs={{0,1},{1,0},{2,3},{3,2},{4,5},{5,4},{6,7},{7,6},{8,9},{9,8},{10,11... | collective-permute-start | bytes 98312 | tf_op jit(solution)/shard_map/ppermute | solution.py:249
  23.6 3.9 %collective-permute-start.7 = (f32[64,128]{1,0:T(8,128)S(1)}, f32[64,128]{1,0:T(8,128)S(1)}, u32[]{:S(2)}, u32[]{:S(2)}) collective-permute-start(f32[64,128]{1,0:T(8,128)S(1)} %add.47.a_ref), channel_id=1, source_target_pairs={{0,1},{1,0},{2,3},{3,2},{4,5},{5,4},{6,7},{7,6},{8,9},{9,8},{10,11... | collective-permute-start | bytes 98312 | tf_op jit(solution)/shard_map/ppermute | solution.py:247
  27.9 1.3 %collective-permute-start.9 = (f32[64,128]{1,0:T(8,128)S(1)}, f32[64,128]{1,0:T(8,128)S(1)}, u32[]{:S(2)}, u32[]{:S(2)}) collective-permute-start(f32[64,128]{1,0:T(8,128)S(1)} %shard_map.55), channel_id=1, source_target_pairs={{0,2},{2,0},{4,6},{6,4},{8,10},{10,8},{12,14},{14,12},{16,18},{18,... | collective-permute-start | bytes 98312 | tf_op jit(solution)/shard_map/ppermute | solution.py:204
  29.1 3.7 %collective-permute-start.10 = (f32[64,128]{1,0:T(8,128)S(1)}, f32[64,128]{1,0:T(8,128)S(1)}, u32[]{:S(2)}, u32[]{:S(2)}) collective-permute-start(f32[64,128]{1,0:T(8,128)S(1)} %add.49), channel_id=1, source_target_pairs={{0,6},{2,4},{4,2},{6,0},{8,14},{10,12},{12,10},{14,8},{16,22},{18,... | collective-permute-start | bytes 98312 | tf_op jit(solution)/shard_map/ppermute | solution.py:204
  32.8 3.3 %collective-permute-start.11 = (f32[64,128]{1,0:T(8,128)S(1)}, f32[64,128]{1,0:T(8,128)S(1)}, u32[]{:S(2)}, u32[]{:S(2)}) collective-permute-start(f32[64,128]{1,0:T(8,128)S(1)} %add.50), channel_id=1, source_target_pairs={{0,10},{2,8},{4,14},{6,12},{8,2},{10,0},{12,6},{14,4},{16,26},{18,... | collective-permute-start | bytes 98312 | tf_op jit(solution)/shard_map/ppermute | solution.py:204

commit v6 on v5

--- a/solution.py
+++ b/solution.py
@@ -76,8 +76,11 @@
     lax.fori_loop(0, WIDE // 8, butterfly, 0, unroll=4)
 
 
-def step_of(k):
-    return (1 << k) | 1
+def step_of(k, odd):
+    straight, crossed = (1 << k) | 1, (1 << {1: 2, 2: 1}.get(k, k)) | 1
+    if isinstance(odd, int):
+        return crossed if odd else straight
+    return straight + odd * (crossed - straight)
 
 
 def gather_blocks(devices, length, columns, corner, rows_smem, rows_ref, t_ref, g_ref, out_ref):
@@ -87,11 +90,16 @@
     top = length.bit_length() - 2
     scale = float(1.0 / np.sqrt(float(length) * devices))
     me = lax.axis_index("row")
+    c0, c1 = corner
+    odd = c0
+    for k in range(bits):
+        odd = odd ^ ((me >> k) & 1)
+    origin = me ^ c0 ^ (c1 * step_of(1, odd))
 
     def gather(i, slot):
-        dest = me ^ corner
+        dest = origin
         for k in range(2, bits):
-            dest = dest ^ (((i >> (bits - 1 - k)) & 1) * step_of(k))
+            dest = dest ^ (((i >> (bits - 1 - k)) & 1) * step_of(k, odd))
         for t in range(per):
             row = rows_smem[dest * per + t] & (half - 1)
             g_ref[slot][t:t + 1, :] = t_ref[pl.ds(row, 1), :]
@@ -108,10 +116,6 @@
         return 0
 
     lax.fori_loop(0, out_ref.shape[0] // SLOTS, several, 0)
-
-
-def corner_of(c0, c1):
-    return c0 * step_of(0) ^ c1 * step_of(1)
 
 
 def mix(matrix_panel, row_signs, sample_rows, devices, corner):
@@ -180,28 +184,22 @@
     )(*(in_space(a, pltpu.VMEM) for a in operands))
 
 
-def square(mine):
-    def kernel(a_ref, o_ref):
-        o_ref[...] = times(a_ref[...], a_ref[...])
-
-    return on_chip(kernel, (mine.shape[0], mine.shape[0]), mine)
-
-
-def products(own, mine, theirs, other_mine, other_theirs, everything):
-    columns = mine.shape[0]
-
-    def kernel(own_ref, a_ref, b_ref, c_ref, d_ref, o_ref):
-        own = own_ref[...] + times(b_ref[...], b_ref[...])
-        cross = times(a_ref[...], c_ref[...]) + times(b_ref[...], d_ref[...])
+def products(full, other, everything):
+    blocks, columns, _ = full.shape
+
+    def kernel(a_ref, b_ref, o_ref):
+        own = sum(times(a_ref[i], a_ref[i]) for i in range(blocks))
+        cross = sum(times(a_ref[i], b_ref[i]) for i in range(blocks))
         first = lax.axis_index("col") == 0
         both = jnp.concatenate([jnp.where(first, own, cross), jnp.where(first, cross, own)], axis=1)
         o_ref[...] = both * (1.0 / everything)
 
-    return on_chip(kernel, (columns, 2 * columns), own, mine, theirs, other_mine, other_theirs)
+    return on_chip(kernel, (columns, 2 * columns), full, other)
 
 
 def swap(value, k):
-    return lax.ppermute(value, "row", [(i, i ^ step_of(k)) for i in range(lax.axis_size("row"))])
+    size = lax.axis_size("row")
+    return lax.ppermute(value, "row", [(i, i ^ (step_of(k, i.bit_count() & 1) if k else 1)) for i in range(size)])
 
 
 def body(matrix_panel, row_signs, sample_rows):
@@ -211,9 +209,9 @@
     bits = devices.bit_length() - 1
 
     def part(table, c0, c1):
-        return pick(table, flat, rows, columns, corner_of(c0, c1))
-
-    table, far, flat, rows = mix(matrix_panel, row_signs, sample_rows, devices, corner_of(1, 1))
+        return pick(table, flat, rows, columns, (c0, c1))
+
+    table, far, flat, rows = mix(matrix_panel, row_signs, sample_rows, devices, (1, 1))
     send = part(table, 0, 1) + swap(far, 0)
     table, send = lax.optimization_barrier((table, send))
     half = send.shape[0] // 2
@@ -235,19 +233,13 @@
         else:
             moved = swap(send, k)
             keep = low + second
-    theirs = keep[1] + moved[1]
-    mine = keep[0] + moved[0]
-    theirs, mine = lax.optimization_barrier((theirs, mine))
-    around = [(0, 1), (1, 0)]
-    first = swap(theirs, bits - 1)
-    second = swap(mine, bits - 1)
-    mine = mine + first
-    mine, theirs = lax.optimization_barrier((mine, theirs))
-    theirs = theirs + second
-    other_mine = lax.ppermute(mine, "col", around)
-    own = square(mine)
-    other_theirs = lax.ppermute(theirs, "col", around)
-    gram = products(own, mine, theirs, other_mine, other_theirs, everything)
+    total = keep + moved
+    moved = swap(total, bits - 1)
+    mine = total[0] + moved[1]
+    theirs = total[1] + moved[0]
+    full = jnp.concatenate([mine[None], theirs[None]], axis=0)
+    other = lax.ppermute(full, "col", [(0, 1), (1, 0)])
+    gram = products(full, other, everything)
     for k in range(bits - 1):
         gram = gram + swap(gram, k)
     return (mine, gram)

time: 36.9 us -> 34.9 us (0.946)
  starting transfers between devices: 13.4 us -> 9.54 us
  waiting for transfers between devices: 16.6 us -> 18.6 us
    ppermute x12 -> x10, starting transfers between devices: 13.4 us -> 9.54 us  [the longest x9 9.47 us: swap(): lax.ppermute(value, 'row', [(i, i ^ (step_of(k, i.bit_count() & 1) if k e...]
    ppermute x12 -> x10, waiting for transfers between devices: 16.6 us -> 18.6 us  [the longest x9 14.3 us: swap(): lax.ppermute(value, 'row', [(i, i ^ (step_of(k, i.bit_count() & 1) if k e...]
  transfers between devices with their start and end apart: 12 -> 10, of which waited for: 10 -> 8; matrix products, arithmetic and copies ran while one was open for 0% -> 0% of each run, Pallas kernels for 4% -> 4%
where the time goes in v6:
time: 34.9 us; the launch traced here: 34.7 us
  waiting for transfers between devices  18.6 us (53%)
  starting transfers between devices  9.54 us (27%)
  Pallas kernels  5.13 us (15%)
  between operations  0.72 us (2%)
  other arithmetic  0.71 us (2%)
    ppermute x9, waiting for transfers between devices, swap(): lax.ppermute(value, 'row', [(i, i ^ (step_of(k, i.bit_count() & 1) if k e...  14.3 us
    ppermute x9, starting transfers between devices, swap(): lax.ppermute(value, 'row', [(i, i ^ (step_of(k, i.bit_count() & 1) if k e...  9.47 us
    ppermute x1, waiting for transfers between devices, body(): other = lax.ppermute(full, 'col', [(0, 1), (1, 0)])  4.25 us
    pallas_call x1, Pallas kernels, mix(): pl.pallas_call(kernel, out_shape=(pltpu.VMEM((length // 2, LANES), jnp.fl...  2.78 us
    pallas_call x3, Pallas kernels, pick(): pl.pallas_call(kernel, out_shape=pltpu.VMEM((devices // 4, columns, per),...  1.96 us
  transfers between devices with their start and end apart: 10, of which 8 were waited for; matrix products, arithmetic and copies ran while one was open for 0% of the time, Pallas kernels for 4%

profile of v6, /device:TPU:0, one launch (start us, length us, event | category | flops | bytes accessed | tf_op | source)
XLA Modules:
  0.0 34.7 jit_solution(12134822481728032493)
XLA Ops:
  0.6 2.8 %shard_map.50 = (f32[4096,128]{1,0:T(8,128)S(1)}, f32[4,64,128]{2,1,0:T(8,128)S(1)}, s32[2048]{0:T(1024)S(4)}, s32[16,128]{1,0:T(8,128)S(1)}) custom-call(bf16[64,8192]{1,0:T(8,128)(2,1)} %x_hbm.1, s32[64,128]{1,0:T(8,128)} %bitcast.5, s32[2048]{0:T(1024)} %flat_hbm.1, s32[16,128]{1,0:T(8,128)} %bitcast.4), custom_call_target="tpu_custom_call" | custom-call | tf_op jit(solution)/shard_map/pallas_call | solution.py:136
  3.4 0.6 %collective-permute-start = (f32[4,64,128]{2,1,0:T(8,128)S(1)}, f32[4,64,128]{2,1,0:T(8,128)S(1)}, u32[]{:S(2)}, u32[]{:S(2)}) collective-permute-start(f32[4,64,128]{2,1,0:T(8,128)S(1)} %get-tuple-element.14), channel_id=1, source_target_pairs={{0,2},{2,0},{4,6},{6,4},{8,10},{10,8},{12,14},{14,12},{16,18},{18,... | collective-permute-start | bytes 393224 | tf_op jit(solution)/shard_map/ppermute | solution.py:202
  4.0 0.6 %shard_map.51 = f32[4,64,128]{2,1,0:T(8,128)S(1)} custom-call(f32[4096,128]{1,0:T(8,128)S(1)} %get-tuple-element.16.t_ref, s32[2048]{0:T(1024)S(4)} %get-tuple-element.12.flat_ref, s32[16,128]{1,0:T(8,128)S(1)} %get-tuple-element.13.rows_ref), custom_call_target="tpu_custom_call" | custom-call | tf_op jit(solution)/shard_map/pallas_call | solution.py:165
  4.6 0.3 collective-permute-done
  5.0 0.7 %shard_map.52 = f32[4,64,128]{2,1,0:T(8,128)S(1)} custom-call(f32[4096,128]{1,0:T(8,128)S(1)} %get-tuple-element.16.t_ref, s32[2048]{0:T(1024)S(4)} %get-tuple-element.12.flat_ref, s32[16,128]{1,0:T(8,128)S(1)} %get-tuple-element.13.rows_ref), custom_call_target="tpu_custom_call" | custom-call | tf_op jit(solution)/shard_map/pallas_call | solution.py:165
  5.7 0.4 %collective-permute-start.1 = (f32[4,64,128]{2,1,0:T(8,128)S(1)}, f32[4,64,128]{2,1,0:T(8,128)S(1)}, u32[]{:S(2)}, u32[]{:S(2)}) collective-permute-start(f32[4,64,128]{2,1,0:T(8,128)S(1)} %shard_map.52), channel_id=1, source_target_pairs={{0,2},{2,0},{4,6},{6,4},{8,10},{10,8},{12,14},{14,12},{16,18},{18,... | collective-permute-start | bytes 393224 | tf_op jit(solution)/shard_map/ppermute | solution.py:202
  6.1 2.7 %collective-permute-start.2 = (f32[2,64,128]{2,1,0:T(8,128)S(1)}, f32[2,64,128]{2,1,0:T(8,128)S(1)}, u32[]{:S(2)}, u32[]{:S(2)}) collective-permute-start(f32[2,64,128]{2,1,0:T(8,128)S(1)} %get-tuple-element.23), channel_id=1, source_target_pairs={{0,6},{2,8},{4,14},{6,0},{8,2},{10,12},{12,10},{14,4},{16,26},{18,... | collective-permute-start | bytes 196616 | tf_op jit(solution)/shard_map/ppermute | solution.py:202
  8.8 0.1 collective-permute-start.3
  8.8 0.6 %shard_map.53 = f32[4,64,128]{2,1,0:T(8,128)S(1)} custom-call(f32[4096,128]{1,0:T(8,128)S(1)} %get-tuple-element.16.t_ref, s32[2048]{0:T(1024)S(4)} %get-tuple-element.12.flat_ref, s32[16,128]{1,0:T(8,128)S(1)} %get-tuple-element.13.rows_ref), custom_call_target="tpu_custom_call" | custom-call | tf_op jit(solution)/shard_map/pallas_call | solution.py:165
  9.5 0.0 collective-permute-done.1
  9.5 1.2 %collective-permute-done.2 = f32[2,64,128]{2,1,0:T(8,128)S(1)} collective-permute-done((f32[2,64,128]{2,1,0:T(8,128)S(1)}, f32[2,64,128]{2,1,0:T(8,128)S(1)}, u32[]{:S(2)}, u32[]{:S(2)}) %collective-permute-start.2) | collective-permute-done | bytes 65568 | tf_op jit(solution)/shard_map/ppermute | solution.py:202
  10.7 2.2 %collective-permute-start.4 = (f32[2,64,128]{2,1,0:T(8,128)S(1)}, f32[2,64,128]{2,1,0:T(8,128)S(1)}, u32[]{:S(2)}, u32[]{:S(2)}) collective-permute-start(f32[2,64,128]{2,1,0:T(8,128)S(1)} %get-tuple-element.19), channel_id=1, source_target_pairs={{0,10},{2,4},{4,2},{6,12},{8,14},{10,0},{12,6},{14,8},{16,22},{18,... | collective-permute-start | bytes 196616 | tf_op jit(solution)/shard_map/ppermute | solution.py:202
  12.9 0.0 collective-permute-done.3
  12.9 1.9 %collective-permute-done.4 = f32[2,64,128]{2,1,0:T(8,128)S(1)} collective-permute-done((f32[2,64,128]{2,1,0:T(8,128)S(1)}, f32[2,64,128]{2,1,0:T(8,128)S(1)}, u32[]{:S(2)}, u32[]{:S(2)}) %collective-permute-start.4) | collective-permute-done | bytes 65568 | tf_op jit(solution)/shard_map/ppermute | solution.py:202
  14.9 2.5 %collective-permute-start.5 = (f32[2,64,128]{2,1,0:T(8,128)S(1)}, f32[2,64,128]{2,1,0:T(8,128)S(1)}, u32[]{:S(2)}, u32[]{:S(2)}) collective-permute-start(f32[2,64,128]{2,1,0:T(8,128)S(1)} %add_add_fusion), channel_id=1, source_target_pairs={{0,18},{2,16},{4,22},{6,20},{8,26},{10,24},{12,30},{14,28},{16,2},... | collective-permute-start | bytes 196616 | tf_op jit(solution)/shard_map/ppermute | solution.py:202
  17.4 3.9 %collective-permute-done.5 = f32[2,64,128]{2,1,0:T(8,128)S(1)} collective-permute-done((f32[2,64,128]{2,1,0:T(8,128)S(1)}, f32[2,64,128]{2,1,0:T(8,128)S(1)}, u32[]{:S(2)}, u32[]{:S(2)}) %collective-permute-start.5) | collective-permute-done | bytes 65568 | tf_op jit(solution)/shard_map/ppermute | solution.py:202
  21.4 0.0 copy-start
  21.4 0.1 collective-permute-start.6
  21.5 4.3 %collective-permute-done.6.b_ref = f32[2,64,128]{2,1,0:T(8,128)S(1)} collective-permute-done((f32[2,64,128]{2,1,0:T(8,128)S(1)}, f32[2,64,128]{2,1,0:T(8,128)S(1)}, u32[]{:S(2)}, u32[]{:S(2)}) %collective-permute-start.6) | collective-permute-done | bytes 65568 | tf_op jit(solution)/shard_map/ppermute | solution.py:241
  25.7 0.4 %shard_map.54 = f32[64,128]{1,0:T(8,128)S(1)} custom-call(f32[2,64,128]{2,1,0:T(8,128)S(1)} %pad_maximum_fusion.a_ref, f32[2,64,128]{2,1,0:T(8,128)S(1)} %collective-permute-done.6.b_ref), custom_call_target="tpu_custom_call" | custom-call | tf_op jit(solution)/shard_map/pallas_call | solution.py:179
  26.1 0.1 collective-permute-start.7
  26.2 1.2 %collective-permute-done.7 = f32[64,128]{1,0:T(8,128)S(1)} collective-permute-done((f32[64,128]{1,0:T(8,128)S(1)}, f32[64,128]{1,0:T(8,128)S(1)}, u32[]{:S(2)}, u32[]{:S(2)}) %collective-permute-start.7) | collective-permute-done | bytes 32800 | tf_op jit(solution)/shard_map/ppermute | solution.py:202
  27.4 0.3 collective-permute-start.8
  27.7 3.0 %collective-permute-done.8 = f32[64,128]{1,0:T(8,128)S(1)} collective-permute-done((f32[64,128]{1,0:T(8,128)S(1)}, f32[64,128]{1,0:T(8,128)S(1)}, u32[]{:S(2)}, u32[]{:S(2)}) %collective-permute-start.8) | collective-permute-done | bytes 32800 | tf_op jit(solution)/shard_map/ppermute | solution.py:202
  30.7 0.7 %collective-permute-start.9 = (f32[64,128]{1,0:T(8,128)S(1)}, f32[64,128]{1,0:T(8,128)S(1)}, u32[]{:S(2)}, u32[]{:S(2)}) collective-permute-start(f32[64,128]{1,0:T(8,128)S(1)} %add.44), channel_id=1, source_target_pairs={{0,10},{2,4},{4,2},{6,12},{8,14},{10,0},{12,6},{14,8},{16,22},{18,... | collective-permute-start | bytes 98312 | tf_op jit(solution)/shard_map/ppermute | solution.py:202
  31.4 2.7 %collective-permute-done.9 = f32[64,128]{1,0:T(8,128)S(1)} collective-permute-done((f32[64,128]{1,0:T(8,128)S(1)}, f32[64,128]{1,0:T(8,128)S(1)}, u32[]{:S(2)}, u32[]{:S(2)}) %collective-permute-start.9) | collective-permute-done | bytes 32800 | tf_op jit(solution)/shard_map/ppermute | solution.py:202
  34.1 0.6 %add.45 = f32[64,128]{1,0:T(8,128)} add(f32[64,128]{1,0:T(8,128)S(1)} %add.44, f32[64,128]{1,0:T(8,128)S(1)} %collective-permute-done.9) | non-fusion elementwise | flops 8192 | bytes 98304 | tf_op jit(solution)/shard_map/add | solution.py:244
  34.7 0.0 copy-done
  (9 shorter events, 0.1 us)
Async XLA Ops:
  3.4 1.5 %collective-permute-start = (f32[4,64,128]{2,1,0:T(8,128)S(1)}, f32[4,64,128]{2,1,0:T(8,128)S(1)}, u32[]{:S(2)}, u32[]{:S(2)}) collective-permute-start(f32[4,64,128]{2,1,0:T(8,128)S(1)} %get-tuple-element.14), channel_id=1, source_target_pairs={{0,2},{2,0},{4,6},{6,4},{8,10},{10,8},{12,14},{14,12},{16,18},{18,... | collective-permute-start | bytes 393224 | tf_op jit(solution)/shard_map/ppermute | solution.py:202
  5.7 3.8 %collective-permute-start.1 = (f32[4,64,128]{2,1,0:T(8,128)S(1)}, f32[4,64,128]{2,1,0:T(8,128)S(1)}, u32[]{:S(2)}, u32[]{:S(2)}) collective-permute-start(f32[4,64,128]{2,1,0:T(8,128)S(1)} %shard_map.52), channel_id=1, source_target_pairs={{0,2},{2,0},{4,6},{6,4},{8,10},{10,8},{12,14},{14,12},{16,18},{18,... | collective-permute-start | bytes 393224 | tf_op jit(solution)/shard_map/ppermute | solution.py:202
  6.1 4.6 %collective-permute-start.2 = (f32[2,64,128]{2,1,0:T(8,128)S(1)}, f32[2,64,128]{2,1,0:T(8,128)S(1)}, u32[]{:S(2)}, u32[]{:S(2)}) collective-permute-start(f32[2,64,128]{2,1,0:T(8,128)S(1)} %get-tuple-element.23), channel_id=1, source_target_pairs={{0,6},{2,8},{4,14},{6,0},{8,2},{10,12},{12,10},{14,4},{16,26},{18,... | collective-permute-start | bytes 196616 | tf_op jit(solution)/shard_map/ppermute | solution.py:202
  8.8 4.2 %collective-permute-start.3 = (f32[2,64,128]{2,1,0:T(8,128)S(1)}, f32[2,64,128]{2,1,0:T(8,128)S(1)}, u32[]{:S(2)}, u32[]{:S(2)}) collective-permute-start(f32[2,64,128]{2,1,0:T(8,128)S(1)} %get-tuple-element.22), channel_id=1, source_target_pairs={{0,6},{2,8},{4,14},{6,0},{8,2},{10,12},{12,10},{14,4},{16,26},{18,... | collective-permute-start | bytes 196616 | tf_op jit(solution)/shard_map/ppermute | solution.py:202
  10.7 4.1 %collective-permute-start.4 = (f32[2,64,128]{2,1,0:T(8,128)S(1)}, f32[2,64,128]{2,1,0:T(8,128)S(1)}, u32[]{:S(2)}, u32[]{:S(2)}) collective-permute-start(f32[2,64,128]{2,1,0:T(8,128)S(1)} %get-tuple-element.19), channel_id=1, source_target_pairs={{0,10},{2,4},{4,2},{6,12},{8,14},{10,0},{12,6},{14,8},{16,22},{18,... | collective-permute-start | bytes 196616 | tf_op jit(solution)/shard_map/ppermute | solution.py:202
  14.9 6.5 %collective-permute-start.5 = (f32[2,64,128]{2,1,0:T(8,128)S(1)}, f32[2,64,128]{2,1,0:T(8,128)S(1)}, u32[]{:S(2)}, u32[]{:S(2)}) collective-permute-start(f32[2,64,128]{2,1,0:T(8,128)S(1)} %add_add_fusion), channel_id=1, source_target_pairs={{0,18},{2,16},{4,22},{6,20},{8,26},{10,24},{12,30},{14,28},{16,2},... | collective-permute-start | bytes 196616 | tf_op jit(solution)/shard_map/ppermute | solution.py:202
  21.4 13.3 %copy-start = (f32[1,64,128]{2,1,0:T(8,128)}, f32[1,64,128]{2,1,0:T(8,128)S(1)}, u32[]{:S(2)}) copy-start(f32[1,64,128]{2,1,0:T(8,128)S(1)} %get-tuple-element.21) | copy-start | bytes 98308
  21.4 4.3 %collective-permute-start.6 = (f32[2,64,128]{2,1,0:T(8,128)S(1)}, f32[2,64,128]{2,1,0:T(8,128)S(1)}, u32[]{:S(2)}, u32[]{:S(2)}) collective-permute-start(f32[2,64,128]{2,1,0:T(8,128)S(1)} %pad_maximum_fusion.a_ref), channel_id=1, source_target_pairs={{0,1},{1,0},{2,3},{3,2},{4,5},{5,4},{6,7},{7,6},{8,9},{9,8},{10,11... | collective-permute-start | bytes 196616 | tf_op jit(solution)/shard_map/ppermute | solution.py:241
  26.1 1.3 %collective-permute-start.7 = (f32[64,128]{1,0:T(8,128)S(1)}, f32[64,128]{1,0:T(8,128)S(1)}, u32[]{:S(2)}, u32[]{:S(2)}) collective-permute-start(f32[64,128]{1,0:T(8,128)S(1)} %shard_map.54), channel_id=1, source_target_pairs={{0,2},{2,0},{4,6},{6,4},{8,10},{10,8},{12,14},{14,12},{16,18},{18,... | collective-permute-start | bytes 98312 | tf_op jit(solution)/shard_map/ppermute | solution.py:202
  27.4 3.3 %collective-permute-start.8 = (f32[64,128]{1,0:T(8,128)S(1)}, f32[64,128]{1,0:T(8,128)S(1)}, u32[]{:S(2)}, u32[]{:S(2)}) collective-permute-start(f32[64,128]{1,0:T(8,128)S(1)} %add.43), channel_id=1, source_target_pairs={{0,6},{2,8},{4,14},{6,0},{8,2},{10,12},{12,10},{14,4},{16,26},{18,... | collective-permute-start | bytes 98312 | tf_op jit(solution)/shard_map/ppermute | solution.py:202
  30.7 3.3 %collective-permute-start.9 = (f32[64,128]{1,0:T(8,128)S(1)}, f32[64,128]{1,0:T(8,128)S(1)}, u32[]{:S(2)}, u32[]{:S(2)}) collective-permute-start(f32[64,128]{1,0:T(8,128)S(1)} %add.44), channel_id=1, source_target_pairs={{0,10},{2,4},{4,2},{6,12},{8,14},{10,0},{12,6},{14,8},{16,22},{18,... | collective-permute-start | bytes 98312 | tf_op jit(solution)/shard_map/ppermute | solution.py:202

commit v7 on v6

--- a/solution.py
+++ b/solution.py
@@ -94,7 +94,7 @@
     odd = c0
     for k in range(bits):
         odd = odd ^ ((me >> k) & 1)
-    origin = me ^ c0 ^ (c1 * step_of(1, odd))
+    origin = me ^ (lax.axis_index("col") & 1) ^ c0 ^ (c1 * step_of(1, odd))
 
     def gather(i, slot):
         dest = origin
@@ -184,17 +184,33 @@
     )(*(in_space(a, pltpu.VMEM) for a in operands))
 
 
-def products(full, other, everything):
+def square(full):
     blocks, columns, _ = full.shape
 
-    def kernel(a_ref, b_ref, o_ref):
-        own = sum(times(a_ref[i], a_ref[i]) for i in range(blocks))
+    def kernel(a_ref, o_ref):
+        o_ref[...] = sum(times(a_ref[i], a_ref[i]) for i in range(blocks))
+
+    return on_chip(kernel, (columns, columns), full)
+
+
+def products(own, full, other, everything):
+    blocks, columns, _ = full.shape
+
+    def kernel(own_ref, a_ref, b_ref, o_ref):
+        own = own_ref[...]
         cross = sum(times(a_ref[i], b_ref[i]) for i in range(blocks))
         first = lax.axis_index("col") == 0
         both = jnp.concatenate([jnp.where(first, own, cross), jnp.where(first, cross, own)], axis=1)
         o_ref[...] = both * (1.0 / everything)
 
-    return on_chip(kernel, (columns, 2 * columns), full, other)
+    return on_chip(kernel, (columns, 2 * columns), own, full, other)
+
+
+def choose(mine, traded):
+    def kernel(a_ref, b_ref, o_ref):
+        o_ref[...] = jnp.where(lax.axis_index("col") & 1 == 0, a_ref[...], b_ref[...])
+
+    return on_chip(kernel, mine.shape, mine, traded)
 
 
 def swap(value, k):
@@ -238,11 +254,16 @@
     mine = total[0] + moved[1]
     theirs = total[1] + moved[0]
     full = jnp.concatenate([mine[None], theirs[None]], axis=0)
-    other = lax.ppermute(full, "col", [(0, 1), (1, 0)])
-    gram = products(full, other, everything)
+    size = lax.axis_size("col")
+    around = [(r * size + c, (r ^ 1) * size + (c ^ 1)) for r in range(devices) for c in range(size)]
+    other = lax.ppermute(full, ("row", "col"), around)
+    traded = swap(mine, 0)
+    own = square(full)
+    gram = products(own, full, other, everything)
     for k in range(bits - 1):
         gram = gram + swap(gram, k)
-    return (mine, gram)
+    sketch = choose(mine, traded)
+    return (sketch, gram)
 
 
 def solution(mesh):

time: 34.9 us -> 34.6 us (level)
  waiting for transfers between devices: 18.6 us -> 15.4 us
  starting transfers between devices: 9.54 us -> 11.7 us
  local copies, waits for them, and re-layouts: 0.02 us -> 0.63 us
    ppermute x1, waiting for transfers between devices: 4.25 us -> 2.62 us  [body(): other = lax.ppermute(full, ('row', 'col'), around)]
    ppermute x9 -> x10, waiting for transfers between devices: 14.3 us -> 12.7 us  [swap(): lax.ppermute(value, 'row', [(i, i ^ (step_of(k, i.bit_count() & 1) if k e...]
    ppermute x1, starting transfers between devices: 0.07 us -> 1.31 us  [body(): other = lax.ppermute(full, ('row', 'col'), around)]
    ppermute x9 -> x10, starting transfers between devices: 9.47 us -> 10.4 us  [swap(): lax.ppermute(value, 'row', [(i, i ^ (step_of(k, i.bit_count() & 1) if k e...]
    unnamed x2 -> x1, local copies, waits for them, and re-layouts: 0.01 us -> 0.62 us
  transfers between devices with their start and end apart: 10 -> 11, of which waited for: 8 -> 8; matrix products, arithmetic and copies ran while one was open for 0% -> 2% of each run, Pallas kernels for 4% -> 4%
where the time goes in v7:
time: 34.6 us; the launch traced here: 34.4 us
  waiting for transfers between devices  15.4 us (45%)
  starting transfers between devices  11.7 us (34%)
  Pallas kernels  5.27 us (15%)
  other arithmetic  0.71 us (2%)
  between operations  0.7 us (2%)
  local copies, waits for them, and re-layouts  0.63 us (2%)
    ppermute x10, waiting for transfers between devices, swap(): lax.ppermute(value, 'row', [(i, i ^ (step_of(k, i.bit_count() & 1) if k e...  12.7 us
    ppermute x10, starting transfers between devices, swap(): lax.ppermute(value, 'row', [(i, i ^ (step_of(k, i.bit_count() & 1) if k e...  10.4 us
    pallas_call x1, Pallas kernels, mix(): pl.pallas_call(kernel, out_shape=(pltpu.VMEM((length // 2, LANES), jnp.fl...  2.78 us
    ppermute x1, waiting for transfers between devices, body(): other = lax.ppermute(full, ('row', 'col'), around)  2.62 us
    pallas_call x3, Pallas kernels, pick(): pl.pallas_call(kernel, out_shape=pltpu.VMEM((devices // 4, columns, per),...  1.97 us
    ppermute x1, starting transfers between devices, body(): other = lax.ppermute(full, ('row', 'col'), around)  1.31 us
  transfers between devices with their start and end apart: 11, of which 8 were waited for; matrix products, arithmetic and copies ran while one was open for 2% of the time, Pallas kernels for 4%

profile of v7, /device:TPU:0, one launch (start us, length us, event | category | flops | bytes accessed | tf_op | source)
XLA Modules:
  0.0 34.4 jit_solution(15787333387835630641)
XLA Ops:
  0.6 2.8 %shard_map.50 = (f32[4096,128]{1,0:T(8,128)S(1)}, f32[4,64,128]{2,1,0:T(8,128)S(1)}, s32[2048]{0:T(1024)S(4)}, s32[16,128]{1,0:T(8,128)S(1)}) custom-call(bf16[64,8192]{1,0:T(8,128)(2,1)} %x_hbm.1, s32[64,128]{1,0:T(8,128)} %bitcast.6, s32[2048]{0:T(1024)} %flat_hbm.1, s32[16,128]{1,0:T(8,128)} %bitcast.5), custom_call_target="tpu_custom_call" | custom-call | tf_op jit(solution)/shard_map/pallas_call | solution.py:136
  3.4 0.6 %collective-permute-start = (f32[4,64,128]{2,1,0:T(8,128)S(1)}, f32[4,64,128]{2,1,0:T(8,128)S(1)}, u32[]{:S(2)}, u32[]{:S(2)}) collective-permute-start(f32[4,64,128]{2,1,0:T(8,128)S(1)} %get-tuple-element.14), channel_id=1, source_target_pairs={{0,2},{2,0},{4,6},{6,4},{8,10},{10,8},{12,14},{14,12},{16,18},{18,... | collective-permute-start | bytes 393224 | tf_op jit(solution)/shard_map/ppermute | solution.py:218
  4.0 0.6 %shard_map.51 = f32[4,64,128]{2,1,0:T(8,128)S(1)} custom-call(f32[4096,128]{1,0:T(8,128)S(1)} %get-tuple-element.16.t_ref, s32[2048]{0:T(1024)S(4)} %get-tuple-element.12.flat_ref, s32[16,128]{1,0:T(8,128)S(1)} %get-tuple-element.13.rows_ref), custom_call_target="tpu_custom_call" | custom-call | tf_op jit(solution)/shard_map/pallas_call | solution.py:165
  4.6 0.3 collective-permute-done
  5.0 0.7 %shard_map.52 = f32[4,64,128]{2,1,0:T(8,128)S(1)} custom-call(f32[4096,128]{1,0:T(8,128)S(1)} %get-tuple-element.16.t_ref, s32[2048]{0:T(1024)S(4)} %get-tuple-element.12.flat_ref, s32[16,128]{1,0:T(8,128)S(1)} %get-tuple-element.13.rows_ref), custom_call_target="tpu_custom_call" | custom-call | tf_op jit(solution)/shard_map/pallas_call | solution.py:165
  5.7 0.4 %collective-permute-start.1 = (f32[4,64,128]{2,1,0:T(8,128)S(1)}, f32[4,64,128]{2,1,0:T(8,128)S(1)}, u32[]{:S(2)}, u32[]{:S(2)}) collective-permute-start(f32[4,64,128]{2,1,0:T(8,128)S(1)} %shard_map.52), channel_id=1, source_target_pairs={{0,2},{2,0},{4,6},{6,4},{8,10},{10,8},{12,14},{14,12},{16,18},{18,... | collective-permute-start | bytes 393224 | tf_op jit(solution)/shard_map/ppermute | solution.py:218
  6.1 2.7 %collective-permute-start.2 = (f32[2,64,128]{2,1,0:T(8,128)S(1)}, f32[2,64,128]{2,1,0:T(8,128)S(1)}, u32[]{:S(2)}, u32[]{:S(2)}) collective-permute-start(f32[2,64,128]{2,1,0:T(8,128)S(1)} %get-tuple-element.23), channel_id=1, source_target_pairs={{0,6},{2,8},{4,14},{6,0},{8,2},{10,12},{12,10},{14,4},{16,26},{18,... | collective-permute-start | bytes 196616 | tf_op jit(solution)/shard_map/ppermute | solution.py:218
  8.8 0.1 collective-permute-start.3
  8.8 0.6 %shard_map.53 = f32[4,64,128]{2,1,0:T(8,128)S(1)} custom-call(f32[4096,128]{1,0:T(8,128)S(1)} %get-tuple-element.16.t_ref, s32[2048]{0:T(1024)S(4)} %get-tuple-element.12.flat_ref, s32[16,128]{1,0:T(8,128)S(1)} %get-tuple-element.13.rows_ref), custom_call_target="tpu_custom_call" | custom-call | tf_op jit(solution)/shard_map/pallas_call | solution.py:165
  9.5 0.0 collective-permute-done.1
  9.5 1.2 %collective-permute-done.2 = f32[2,64,128]{2,1,0:T(8,128)S(1)} collective-permute-done((f32[2,64,128]{2,1,0:T(8,128)S(1)}, f32[2,64,128]{2,1,0:T(8,128)S(1)}, u32[]{:S(2)}, u32[]{:S(2)}) %collective-permute-start.2) | collective-permute-done | bytes 65568 | tf_op jit(solution)/shard_map/ppermute | solution.py:218
  10.7 2.2 %collective-permute-start.4 = (f32[2,64,128]{2,1,0:T(8,128)S(1)}, f32[2,64,128]{2,1,0:T(8,128)S(1)}, u32[]{:S(2)}, u32[]{:S(2)}) collective-permute-start(f32[2,64,128]{2,1,0:T(8,128)S(1)} %get-tuple-element.19), channel_id=1, source_target_pairs={{0,10},{2,4},{4,2},{6,12},{8,14},{10,0},{12,6},{14,8},{16,22},{18,... | collective-permute-start | bytes 196616 | tf_op jit(solution)/shard_map/ppermute | solution.py:218
  12.9 0.0 collective-permute-done.3
  12.9 1.9 %collective-permute-done.4 = f32[2,64,128]{2,1,0:T(8,128)S(1)} collective-permute-done((f32[2,64,128]{2,1,0:T(8,128)S(1)}, f32[2,64,128]{2,1,0:T(8,128)S(1)}, u32[]{:S(2)}, u32[]{:S(2)}) %collective-permute-start.4) | collective-permute-done | bytes 65568 | tf_op jit(solution)/shard_map/ppermute | solution.py:218
  14.9 2.5 %collective-permute-start.5 = (f32[2,64,128]{2,1,0:T(8,128)S(1)}, f32[2,64,128]{2,1,0:T(8,128)S(1)}, u32[]{:S(2)}, u32[]{:S(2)}) collective-permute-start(f32[2,64,128]{2,1,0:T(8,128)S(1)} %add_add_fusion), channel_id=1, source_target_pairs={{0,18},{2,16},{4,22},{6,20},{8,26},{10,24},{12,30},{14,28},{16,2},... | collective-permute-start | bytes 196616 | tf_op jit(solution)/shard_map/ppermute | solution.py:218
  17.4 3.9 %collective-permute-done.5 = f32[2,64,128]{2,1,0:T(8,128)S(1)} collective-permute-done((f32[2,64,128]{2,1,0:T(8,128)S(1)}, f32[2,64,128]{2,1,0:T(8,128)S(1)}, u32[]{:S(2)}, u32[]{:S(2)}) %collective-permute-start.5) | collective-permute-done | bytes 65568 | tf_op jit(solution)/shard_map/ppermute | solution.py:218
  21.4 1.3 %collective-permute-start.7 = (f32[2,64,128]{2,1,0:T(8,128)S(1)}, f32[2,64,128]{2,1,0:T(8,128)S(1)}, u32[]{:S(2)}, u32[]{:S(2)}) collective-permute-start(f32[2,64,128]{2,1,0:T(8,128)S(1)} %pad_maximum_fusion.a_ref), channel_id=1, source_target_pairs={{0,3},{1,2},{2,1},{3,0},{4,7},{5,6},{6,5},{7,4},{8,11},{9,10},{10,... | collective-permute-start | bytes 196616 | tf_op jit(solution)/shard_map/ppermute | solution.py:259
  22.7 0.2 shard_map.55.own_ref
  22.9 2.6 %collective-permute-done.7.b_ref = f32[2,64,128]{2,1,0:T(8,128)S(1)} collective-permute-done((f32[2,64,128]{2,1,0:T(8,128)S(1)}, f32[2,64,128]{2,1,0:T(8,128)S(1)}, u32[]{:S(2)}, u32[]{:S(2)}) %collective-permute-start.7) | collective-permute-done | bytes 65568 | tf_op jit(solution)/shard_map/ppermute | solution.py:259
  25.5 0.3 shard_map.56
  25.8 0.2 collective-permute-start.8
  26.0 1.1 %collective-permute-done.8 = f32[64,128]{1,0:T(8,128)S(1)} collective-permute-done((f32[64,128]{1,0:T(8,128)S(1)}, f32[64,128]{1,0:T(8,128)S(1)}, u32[]{:S(2)}, u32[]{:S(2)}) %collective-permute-start.8) | collective-permute-done | bytes 32800 | tf_op jit(solution)/shard_map/ppermute | solution.py:218
  27.1 0.9 %collective-permute-start.9 = (f32[64,128]{1,0:T(8,128)S(1)}, f32[64,128]{1,0:T(8,128)S(1)}, u32[]{:S(2)}, u32[]{:S(2)}) collective-permute-start(f32[64,128]{1,0:T(8,128)S(1)} %add.41), channel_id=1, source_target_pairs={{0,6},{2,8},{4,14},{6,0},{8,2},{10,12},{12,10},{14,4},{16,26},{18,... | collective-permute-start | bytes 98312 | tf_op jit(solution)/shard_map/ppermute | solution.py:218
  28.0 0.2 collective-permute-start.6
  28.2 2.3 %collective-permute-done.9 = f32[64,128]{1,0:T(8,128)S(1)} collective-permute-done((f32[64,128]{1,0:T(8,128)S(1)}, f32[64,128]{1,0:T(8,128)S(1)}, u32[]{:S(2)}, u32[]{:S(2)}) %collective-permute-start.9) | collective-permute-done | bytes 32800 | tf_op jit(solution)/shard_map/ppermute | solution.py:218
  30.5 0.7 %collective-permute-start.10 = (f32[64,128]{1,0:T(8,128)S(1)}, f32[64,128]{1,0:T(8,128)S(1)}, u32[]{:S(2)}, u32[]{:S(2)}) collective-permute-start(f32[64,128]{1,0:T(8,128)S(1)} %add.42), channel_id=1, source_target_pairs={{0,10},{2,4},{4,2},{6,12},{8,14},{10,0},{12,6},{14,8},{16,22},{18,... | collective-permute-start | bytes 98312 | tf_op jit(solution)/shard_map/ppermute | solution.py:218
  31.2 0.0 collective-permute-done.6.b_ref
  31.2 0.6 %copy.5 = f32[64,128]{1,0:T(8,128)} copy(f32[64,128]{1,0:T(8,128)S(1)} %shard_map.54) | data formatting | bytes 65536
  31.8 2.0 %collective-permute-done.10 = f32[64,128]{1,0:T(8,128)S(1)} collective-permute-done((f32[64,128]{1,0:T(8,128)S(1)}, f32[64,128]{1,0:T(8,128)S(1)}, u32[]{:S(2)}, u32[]{:S(2)}) %collective-permute-start.10) | collective-permute-done | bytes 32800 | tf_op jit(solution)/shard_map/ppermute | solution.py:218
  33.8 0.6 %add.43 = f32[64,128]{1,0:T(8,128)} add(f32[64,128]{1,0:T(8,128)S(1)} %add.42, f32[64,128]{1,0:T(8,128)S(1)} %collective-permute-done.10) | non-fusion elementwise | flops 8192 | bytes 98304 | tf_op jit(solution)/shard_map/add | solution.py:264
  (10 shorter events, 0.1 us)
Async XLA Ops:
  3.4 1.5 %collective-permute-start = (f32[4,64,128]{2,1,0:T(8,128)S(1)}, f32[4,64,128]{2,1,0:T(8,128)S(1)}, u32[]{:S(2)}, u32[]{:S(2)}) collective-permute-start(f32[4,64,128]{2,1,0:T(8,128)S(1)} %get-tuple-element.14), channel_id=1, source_target_pairs={{0,2},{2,0},{4,6},{6,4},{8,10},{10,8},{12,14},{14,12},{16,18},{18,... | collective-permute-start | bytes 393224 | tf_op jit(solution)/shard_map/ppermute | solution.py:218
  5.7 3.8 %collective-permute-start.1 = (f32[4,64,128]{2,1,0:T(8,128)S(1)}, f32[4,64,128]{2,1,0:T(8,128)S(1)}, u32[]{:S(2)}, u32[]{:S(2)}) collective-permute-start(f32[4,64,128]{2,1,0:T(8,128)S(1)} %shard_map.52), channel_id=1, source_target_pairs={{0,2},{2,0},{4,6},{6,4},{8,10},{10,8},{12,14},{14,12},{16,18},{18,... | collective-permute-start | bytes 393224 | tf_op jit(solution)/shard_map/ppermute | solution.py:218
  6.1 4.6 %collective-permute-start.2 = (f32[2,64,128]{2,1,0:T(8,128)S(1)}, f32[2,64,128]{2,1,0:T(8,128)S(1)}, u32[]{:S(2)}, u32[]{:S(2)}) collective-permute-start(f32[2,64,128]{2,1,0:T(8,128)S(1)} %get-tuple-element.23), channel_id=1, source_target_pairs={{0,6},{2,8},{4,14},{6,0},{8,2},{10,12},{12,10},{14,4},{16,26},{18,... | collective-permute-start | bytes 196616 | tf_op jit(solution)/shard_map/ppermute | solution.py:218
  8.8 4.2 %collective-permute-start.3 = (f32[2,64,128]{2,1,0:T(8,128)S(1)}, f32[2,64,128]{2,1,0:T(8,128)S(1)}, u32[]{:S(2)}, u32[]{:S(2)}) collective-permute-start(f32[2,64,128]{2,1,0:T(8,128)S(1)} %get-tuple-element.22), channel_id=1, source_target_pairs={{0,6},{2,8},{4,14},{6,0},{8,2},{10,12},{12,10},{14,4},{16,26},{18,... | collective-permute-start | bytes 196616 | tf_op jit(solution)/shard_map/ppermute | solution.py:218
  10.7 4.1 %collective-permute-start.4 = (f32[2,64,128]{2,1,0:T(8,128)S(1)}, f32[2,64,128]{2,1,0:T(8,128)S(1)}, u32[]{:S(2)}, u32[]{:S(2)}) collective-permute-start(f32[2,64,128]{2,1,0:T(8,128)S(1)} %get-tuple-element.19), channel_id=1, source_target_pairs={{0,10},{2,4},{4,2},{6,12},{8,14},{10,0},{12,6},{14,8},{16,22},{18,... | collective-permute-start | bytes 196616 | tf_op jit(solution)/shard_map/ppermute | solution.py:218
  14.9 6.5 %collective-permute-start.5 = (f32[2,64,128]{2,1,0:T(8,128)S(1)}, f32[2,64,128]{2,1,0:T(8,128)S(1)}, u32[]{:S(2)}, u32[]{:S(2)}) collective-permute-start(f32[2,64,128]{2,1,0:T(8,128)S(1)} %add_add_fusion), channel_id=1, source_target_pairs={{0,18},{2,16},{4,22},{6,20},{8,26},{10,24},{12,30},{14,28},{16,2},... | collective-permute-start | bytes 196616 | tf_op jit(solution)/shard_map/ppermute | solution.py:218
  21.4 4.2 %collective-permute-start.7 = (f32[2,64,128]{2,1,0:T(8,128)S(1)}, f32[2,64,128]{2,1,0:T(8,128)S(1)}, u32[]{:S(2)}, u32[]{:S(2)}) collective-permute-start(f32[2,64,128]{2,1,0:T(8,128)S(1)} %pad_maximum_fusion.a_ref), channel_id=1, source_target_pairs={{0,3},{1,2},{2,1},{3,0},{4,7},{5,6},{6,5},{7,4},{8,11},{9,10},{10,... | collective-permute-start | bytes 196616 | tf_op jit(solution)/shard_map/ppermute | solution.py:259
  25.8 1.3 %collective-permute-start.8 = (f32[64,128]{1,0:T(8,128)S(1)}, f32[64,128]{1,0:T(8,128)S(1)}, u32[]{:S(2)}, u32[]{:S(2)}) collective-permute-start(f32[64,128]{1,0:T(8,128)S(1)} %shard_map.56), channel_id=1, source_target_pairs={{0,2},{2,0},{4,6},{6,4},{8,10},{10,8},{12,14},{14,12},{16,18},{18,... | collective-permute-start | bytes 98312 | tf_op jit(solution)/shard_map/ppermute | solution.py:218
  27.1 3.3 %collective-permute-start.9 = (f32[64,128]{1,0:T(8,128)S(1)}, f32[64,128]{1,0:T(8,128)S(1)}, u32[]{:S(2)}, u32[]{:S(2)}) collective-permute-start(f32[64,128]{1,0:T(8,128)S(1)} %add.41), channel_id=1, source_target_pairs={{0,6},{2,8},{4,14},{6,0},{8,2},{10,12},{12,10},{14,4},{16,26},{18,... | collective-permute-start | bytes 98312 | tf_op jit(solution)/shard_map/ppermute | solution.py:218
  28.0 3.2 %collective-permute-start.6 = (f32[64,128]{1,0:T(8,128)S(1)}, f32[64,128]{1,0:T(8,128)S(1)}, u32[]{:S(2)}, u32[]{:S(2)}) collective-permute-start(f32[64,128]{1,0:T(8,128)S(1)} %bitcast.3), channel_id=1, source_target_pairs={{0,2},{2,0},{4,6},{6,4},{8,10},{10,8},{12,14},{14,12},{16,18},{18,... | collective-permute-start | bytes 98312 | tf_op jit(solution)/shard_map/ppermute | solution.py:218
  30.5 3.3 %collective-permute-start.10 = (f32[64,128]{1,0:T(8,128)S(1)}, f32[64,128]{1,0:T(8,128)S(1)}, u32[]{:S(2)}, u32[]{:S(2)}) collective-permute-start(f32[64,128]{1,0:T(8,128)S(1)} %add.42), channel_id=1, source_target_pairs={{0,10},{2,4},{4,2},{6,12},{8,14},{10,0},{12,6},{14,8},{16,22},{18,... | collective-permute-start | bytes 98312 | tf_op jit(solution)/shard_map/ppermute | solution.py:218

commit v8 on v7

--- a/solution.py
+++ b/solution.py
@@ -25,7 +25,7 @@
     return total & 1
 
 
-def mix_blocks(x_hbm, s_ref, s_copy, x_ref, t_ref, sems):
+def mix_blocks(x_hbm, s_ref, ready, x_ref, t_ref, sems):
     _, length = x_ref.shape
     slabs = length // WIDE // 2
     groups = slabs // 2
@@ -41,7 +41,7 @@
     left = lax.broadcasted_iota(jnp.int32, (WIDE, WIDE), 0)
     right = lax.broadcasted_iota(jnp.int32, (WIDE, WIDE), 1)
     mat = (1 - 2 * parity(left & right, WIDE.bit_length() - 1)).astype(jnp.float32).astype(jnp.bfloat16)
-    s_copy.wait()
+    ready()
     for g in range(groups):
         if g % (groups // CHUNKS) == 0:
             first = g // (groups // CHUNKS)
@@ -83,9 +83,8 @@
     return straight + odd * (crossed - straight)
 
 
-def gather_blocks(devices, length, columns, corner, rows_smem, rows_ref, t_ref, g_ref, out_ref):
+def gather_blocks(devices, length, columns, corner, rows_smem, rows_ref, t_ref, out_ref):
     per = rows_ref.shape[1]
-    half = length // 2
     bits = devices.bit_length() - 1
     top = length.bit_length() - 2
     scale = float(1.0 / np.sqrt(float(length) * devices))
@@ -96,14 +95,11 @@
         odd = odd ^ ((me >> k) & 1)
     origin = me ^ (lax.axis_index("col") & 1) ^ c0 ^ (c1 * step_of(1, odd))
 
-    def gather(i, slot):
+    def gather(i):
         dest = origin
         for k in range(2, bits):
             dest = dest ^ (((i >> (bits - 1 - k)) & 1) * step_of(k, odd))
-        for t in range(per):
-            row = rows_smem[dest * per + t] & (half - 1)
-            g_ref[slot][t:t + 1, :] = t_ref[pl.ds(row, 1), :]
-        turned = g_ref[slot][...].T
+        turned = jnp.concatenate([t_ref[pl.ds(rows_smem[dest, t], 1), :] for t in range(per)], axis=0).T
         samples = rows_ref[pl.ds(dest, 1), :]
         flip = parity((samples >> (top + 1)) & me, bits)
         first = jnp.where(flip == 1, -scale, scale)
@@ -112,7 +108,7 @@
 
     def several(j, _):
         for slot in range(SLOTS):
-            gather(j * SLOTS + slot, slot)
+            gather(j * SLOTS + slot)
         return 0
 
     lax.fori_loop(0, out_ref.shape[0] // SLOTS, several, 0)
@@ -123,35 +119,41 @@
     per = sample_rows.shape[0] // devices
     hbm, vmem, smem = (pl.BlockSpec(memory_space=m) for m in (pltpu.HBM, pltpu.VMEM, pltpu.SMEM))
 
-    def kernel(x_hbm, s_hbm, flat_hbm, rows_hbm, t_ref, out_ref, flat_ref, rows_ref, x_ref, s_ref, *rest):
-        g_ref, (sems, more) = rest[:SLOTS], rest[SLOTS:]
-        fetch = [pltpu.make_async_copy(a, b, more.at[k]) for k, (a, b) in enumerate(((s_hbm, s_ref), (flat_hbm, flat_ref), (rows_hbm, rows_ref)))]
+    def kernel(x_hbm, s_hbm, rows_hbm, t_ref, out_ref, flat_ref, rows_ref, x_ref, s_ref, masked_ref, sems, more):
+        fetch = [pltpu.make_async_copy(a, b, more.at[k]) for k, (a, b) in enumerate(((s_hbm, s_ref), (rows_hbm, rows_ref)))]
         for copy in fetch:
             copy.start()
-        mix_blocks(x_hbm, s_ref, fetch[0], x_ref, t_ref, sems)
-        fetch[1].wait()
-        fetch[2].wait()
-        gather_blocks(devices, length, columns, corner, flat_ref, rows_ref, t_ref, g_ref, out_ref)
+        move = pltpu.make_async_copy(masked_ref, flat_ref, more.at[2])
+
+        def ready():
+            fetch[1].wait()
+            masked_ref[...] = rows_ref[...] & (length // 2 - 1)
+            move.start()
+            fetch[0].wait()
+
+        mix_blocks(x_hbm, s_ref, ready, x_ref, t_ref, sems)
+        move.wait()
+        gather_blocks(devices, length, columns, corner, flat_ref, rows_ref, t_ref, out_ref)
 
     return pl.pallas_call(
         kernel,
         out_shape=(
             pltpu.VMEM((length // 2, LANES), jnp.float32),
             pltpu.VMEM((devices // 4, columns, per), jnp.float32),
-            pltpu.SMEM(sample_rows.shape, jnp.int32),
+            pltpu.SMEM((devices, per), jnp.int32),
             pltpu.VMEM((devices, per), jnp.int32),
         ),
-        in_specs=[hbm] * 4,
+        in_specs=[hbm] * 3,
         out_specs=(vmem, vmem, smem, vmem),
         scratch_shapes=[
             pltpu.VMEM((columns, length), jnp.bfloat16),
             pltpu.VMEM((length // LANES, LANES), jnp.int32),
-            *[pltpu.VMEM((per, LANES), jnp.float32)] * SLOTS,
+            pltpu.VMEM((devices, per), jnp.int32),
             pltpu.SemaphoreType.DMA((CHUNKS, 2)),
             pltpu.SemaphoreType.DMA((3,)),
         ],
         compiler_params=pltpu.CompilerParams(vmem_limit_bytes=VMEM_GRANT),
-    )(*(in_space(a, pltpu.HBM) for a in (matrix_panel, row_signs.reshape(length // LANES, LANES), sample_rows, sample_rows.reshape(devices, per))))
+    )(*(in_space(a, pltpu.HBM) for a in (matrix_panel, row_signs.reshape(length // LANES, LANES), sample_rows.reshape(devices, per))))
 
 
 def pick(table, flat, rows, columns, corner):
@@ -159,14 +161,13 @@
     vmem, smem = pl.BlockSpec(memory_space=pltpu.VMEM), pl.BlockSpec(memory_space=pltpu.SMEM)
     length = 2 * table.shape[0]
 
-    def kernel(t_ref, flat_ref, rows_ref, out_ref, *g_ref):
-        gather_blocks(devices, length, columns, corner, flat_ref, rows_ref, t_ref, g_ref, out_ref)
+    def kernel(t_ref, flat_ref, rows_ref, out_ref):
+        gather_blocks(devices, length, columns, corner, flat_ref, rows_ref, t_ref, out_ref)
 
     return pl.pallas_call(
         kernel,
         out_shape=pltpu.VMEM((devices // 4, columns, per), jnp.float32),
         in_specs=[vmem, smem, vmem],
-        scratch_shapes=[pltpu.VMEM((per, LANES), jnp.float32)] * SLOTS,
         compiler_params=pltpu.CompilerParams(vmem_limit_bytes=VMEM_GRANT),
     )(in_space(table, pltpu.VMEM), in_space(flat, pltpu.SMEM), in_space(rows, pltpu.VMEM))
 

time: 34.6 us -> 34.2 us (0.988)
  Pallas kernels: 5.27 us -> 4.59 us
    pallas_call x3, Pallas kernels: 1.97 us -> 1.45 us  [pick(): pl.pallas_call(kernel, out_shape=pltpu.VMEM((devices // 4, columns, per),...]
  transfers between devices with their start and end apart: 11 -> 11, of which waited for: 8 -> 8; matrix products, arithmetic and copies ran while one was open for 2% -> 2% of each run, Pallas kernels for 4% -> 3%
where the time goes in v8:
time: 34.2 us; the launch traced here: 34.1 us
  waiting for transfers between devices  15.7 us (46%)
  starting transfers between devices  11.7 us (34%)
  Pallas kernels  4.59 us (13%)
  other arithmetic  0.71 us (2%)
  between operations  0.7 us (2%)
  local copies, waits for them, and re-layouts  0.63 us (2%)
    ppermute x10, waiting for transfers between devices, swap(): lax.ppermute(value, 'row', [(i, i ^ (step_of(k, i.bit_count() & 1) if k e...  13.1 us
    ppermute x10, starting transfers between devices, swap(): lax.ppermute(value, 'row', [(i, i ^ (step_of(k, i.bit_count() & 1) if k e...  10.4 us
    ppermute x1, waiting for transfers between devices, body(): other = lax.ppermute(full, ('row', 'col'), around)  2.62 us
    pallas_call x1, Pallas kernels, mix(): pl.pallas_call(kernel, out_shape=(pltpu.VMEM((length // 2, LANES), jnp.fl...  2.6 us
    pallas_call x3, Pallas kernels, pick(): pl.pallas_call(kernel, out_shape=pltpu.VMEM((devices // 4, columns, per),...  1.45 us
    ppermute x1, starting transfers between devices, body(): other = lax.ppermute(full, ('row', 'col'), around)  1.31 us
  transfers between devices with their start and end apart: 11, of which 8 were waited for; matrix products, arithmetic and copies ran while one was open for 2% of the time, Pallas kernels for 3%

profile of v8, /device:TPU:0, one launch (start us, length us, event | category | flops | bytes accessed | tf_op | source)
XLA Modules:
  0.0 34.1 jit_solution(6341507231002459392)
XLA Ops:
  0.6 2.6 %shard_map.50 = (f32[4096,128]{1,0:T(8,128)S(1)}, f32[4,64,128]{2,1,0:T(8,128)S(1)}, s32[16,128]{1,0:T(8,128)S(4)}, s32[16,128]{1,0:T(8,128)S(1)}) custom-call(bf16[64,8192]{1,0:T(8,128)(2,1)} %x_hbm.1, s32[64,128]{1,0:T(8,128)} %bitcast.5, s32[16,128]{1,0:T(8,128)} %bitcast.6), custom_call_target="tpu_custom_call" | custom-call | tf_op jit(solution)/shard_map/pallas_call | solution.py:138
  3.2 0.6 %collective-permute-start = (f32[4,64,128]{2,1,0:T(8,128)S(1)}, f32[4,64,128]{2,1,0:T(8,128)S(1)}, u32[]{:S(2)}, u32[]{:S(2)}) collective-permute-start(f32[4,64,128]{2,1,0:T(8,128)S(1)} %get-tuple-element.14), channel_id=1, source_target_pairs={{0,2},{2,0},{4,6},{6,4},{8,10},{10,8},{12,14},{14,12},{16,18},{18,... | collective-permute-start | bytes 393224 | tf_op jit(solution)/shard_map/ppermute | solution.py:219
  3.8 0.5 %shard_map.51 = f32[4,64,128]{2,1,0:T(8,128)S(1)} custom-call(f32[4096,128]{1,0:T(8,128)S(1)} %get-tuple-element.16.t_ref, s32[16,128]{1,0:T(8,128)S(4)} %get-tuple-element.12.flat_ref, s32[16,128]{1,0:T(8,128)S(1)} %get-tuple-element.13.rows_ref), custom_call_target="tpu_custom_call" | custom-call | tf_op jit(solution)/shard_map/pallas_call | solution.py:167
  4.3 0.5 %collective-permute-done = f32[4,64,128]{2,1,0:T(8,128)S(1)} collective-permute-done((f32[4,64,128]{2,1,0:T(8,128)S(1)}, f32[4,64,128]{2,1,0:T(8,128)S(1)}, u32[]{:S(2)}, u32[]{:S(2)}) %collective-permute-start) | collective-permute-done | bytes 131104 | tf_op jit(solution)/shard_map/ppermute | solution.py:219
  4.8 0.5 %shard_map.52 = f32[4,64,128]{2,1,0:T(8,128)S(1)} custom-call(f32[4096,128]{1,0:T(8,128)S(1)} %get-tuple-element.16.t_ref, s32[16,128]{1,0:T(8,128)S(4)} %get-tuple-element.12.flat_ref, s32[16,128]{1,0:T(8,128)S(1)} %get-tuple-element.13.rows_ref), custom_call_target="tpu_custom_call" | custom-call | tf_op jit(solution)/shard_map/pallas_call | solution.py:167
  5.3 0.4 %collective-permute-start.1 = (f32[4,64,128]{2,1,0:T(8,128)S(1)}, f32[4,64,128]{2,1,0:T(8,128)S(1)}, u32[]{:S(2)}, u32[]{:S(2)}) collective-permute-start(f32[4,64,128]{2,1,0:T(8,128)S(1)} %shard_map.52), channel_id=1, source_target_pairs={{0,2},{2,0},{4,6},{6,4},{8,10},{10,8},{12,14},{14,12},{16,18},{18,... | collective-permute-start | bytes 393224 | tf_op jit(solution)/shard_map/ppermute | solution.py:219
  5.7 2.7 %collective-permute-start.2 = (f32[2,64,128]{2,1,0:T(8,128)S(1)}, f32[2,64,128]{2,1,0:T(8,128)S(1)}, u32[]{:S(2)}, u32[]{:S(2)}) collective-permute-start(f32[2,64,128]{2,1,0:T(8,128)S(1)} %get-tuple-element.23), channel_id=1, source_target_pairs={{0,6},{2,8},{4,14},{6,0},{8,2},{10,12},{12,10},{14,4},{16,26},{18,... | collective-permute-start | bytes 196616 | tf_op jit(solution)/shard_map/ppermute | solution.py:219
  8.4 0.1 collective-permute-start.3
  8.5 0.5 %shard_map.53 = f32[4,64,128]{2,1,0:T(8,128)S(1)} custom-call(f32[4096,128]{1,0:T(8,128)S(1)} %get-tuple-element.16.t_ref, s32[16,128]{1,0:T(8,128)S(4)} %get-tuple-element.12.flat_ref, s32[16,128]{1,0:T(8,128)S(1)} %get-tuple-element.13.rows_ref), custom_call_target="tpu_custom_call" | custom-call | tf_op jit(solution)/shard_map/pallas_call | solution.py:167
  9.0 0.0 collective-permute-done.1
  9.0 1.4 %collective-permute-done.2 = f32[2,64,128]{2,1,0:T(8,128)S(1)} collective-permute-done((f32[2,64,128]{2,1,0:T(8,128)S(1)}, f32[2,64,128]{2,1,0:T(8,128)S(1)}, u32[]{:S(2)}, u32[]{:S(2)}) %collective-permute-start.2) | collective-permute-done | bytes 65568 | tf_op jit(solution)/shard_map/ppermute | solution.py:219
  10.4 2.2 %collective-permute-start.4 = (f32[2,64,128]{2,1,0:T(8,128)S(1)}, f32[2,64,128]{2,1,0:T(8,128)S(1)}, u32[]{:S(2)}, u32[]{:S(2)}) collective-permute-start(f32[2,64,128]{2,1,0:T(8,128)S(1)} %get-tuple-element.19), channel_id=1, source_target_pairs={{0,10},{2,4},{4,2},{6,12},{8,14},{10,0},{12,6},{14,8},{16,22},{18,... | collective-permute-start | bytes 196616 | tf_op jit(solution)/shard_map/ppermute | solution.py:219
  12.6 0.0 collective-permute-done.3
  12.6 1.9 %collective-permute-done.4 = f32[2,64,128]{2,1,0:T(8,128)S(1)} collective-permute-done((f32[2,64,128]{2,1,0:T(8,128)S(1)}, f32[2,64,128]{2,1,0:T(8,128)S(1)}, u32[]{:S(2)}, u32[]{:S(2)}) %collective-permute-start.4) | collective-permute-done | bytes 65568 | tf_op jit(solution)/shard_map/ppermute | solution.py:219
  14.5 2.5 %collective-permute-start.5 = (f32[2,64,128]{2,1,0:T(8,128)S(1)}, f32[2,64,128]{2,1,0:T(8,128)S(1)}, u32[]{:S(2)}, u32[]{:S(2)}) collective-permute-start(f32[2,64,128]{2,1,0:T(8,128)S(1)} %add_add_fusion), channel_id=1, source_target_pairs={{0,18},{2,16},{4,22},{6,20},{8,26},{10,24},{12,30},{14,28},{16,2},... | collective-permute-start | bytes 196616 | tf_op jit(solution)/shard_map/ppermute | solution.py:219
  17.0 3.9 %collective-permute-done.5 = f32[2,64,128]{2,1,0:T(8,128)S(1)} collective-permute-done((f32[2,64,128]{2,1,0:T(8,128)S(1)}, f32[2,64,128]{2,1,0:T(8,128)S(1)}, u32[]{:S(2)}, u32[]{:S(2)}) %collective-permute-start.5) | collective-permute-done | bytes 65568 | tf_op jit(solution)/shard_map/ppermute | solution.py:219
  21.0 1.3 %collective-permute-start.7 = (f32[2,64,128]{2,1,0:T(8,128)S(1)}, f32[2,64,128]{2,1,0:T(8,128)S(1)}, u32[]{:S(2)}, u32[]{:S(2)}) collective-permute-start(f32[2,64,128]{2,1,0:T(8,128)S(1)} %pad_maximum_fusion.a_ref), channel_id=1, source_target_pairs={{0,3},{1,2},{2,1},{3,0},{4,7},{5,6},{6,5},{7,4},{8,11},{9,10},{10,... | collective-permute-start | bytes 196616 | tf_op jit(solution)/shard_map/ppermute | solution.py:260
  22.3 0.2 shard_map.55.own_ref
  22.6 2.6 %collective-permute-done.7.b_ref = f32[2,64,128]{2,1,0:T(8,128)S(1)} collective-permute-done((f32[2,64,128]{2,1,0:T(8,128)S(1)}, f32[2,64,128]{2,1,0:T(8,128)S(1)}, u32[]{:S(2)}, u32[]{:S(2)}) %collective-permute-start.7) | collective-permute-done | bytes 65568 | tf_op jit(solution)/shard_map/ppermute | solution.py:260
  25.2 0.3 shard_map.56
  25.5 0.2 collective-permute-start.8
  25.7 1.1 %collective-permute-done.8 = f32[64,128]{1,0:T(8,128)S(1)} collective-permute-done((f32[64,128]{1,0:T(8,128)S(1)}, f32[64,128]{1,0:T(8,128)S(1)}, u32[]{:S(2)}, u32[]{:S(2)}) %collective-permute-start.8) | collective-permute-done | bytes 32800 | tf_op jit(solution)/shard_map/ppermute | solution.py:219
  26.8 0.9 %collective-permute-start.9 = (f32[64,128]{1,0:T(8,128)S(1)}, f32[64,128]{1,0:T(8,128)S(1)}, u32[]{:S(2)}, u32[]{:S(2)}) collective-permute-start(f32[64,128]{1,0:T(8,128)S(1)} %add.41), channel_id=1, source_target_pairs={{0,6},{2,8},{4,14},{6,0},{8,2},{10,12},{12,10},{14,4},{16,26},{18,... | collective-permute-start | bytes 98312 | tf_op jit(solution)/shard_map/ppermute | solution.py:219
  27.7 0.2 collective-permute-start.6
  27.8 2.3 %collective-permute-done.9 = f32[64,128]{1,0:T(8,128)S(1)} collective-permute-done((f32[64,128]{1,0:T(8,128)S(1)}, f32[64,128]{1,0:T(8,128)S(1)}, u32[]{:S(2)}, u32[]{:S(2)}) %collective-permute-start.9) | collective-permute-done | bytes 32800 | tf_op jit(solution)/shard_map/ppermute | solution.py:219
  30.1 0.7 %collective-permute-start.10 = (f32[64,128]{1,0:T(8,128)S(1)}, f32[64,128]{1,0:T(8,128)S(1)}, u32[]{:S(2)}, u32[]{:S(2)}) collective-permute-start(f32[64,128]{1,0:T(8,128)S(1)} %add.42), channel_id=1, source_target_pairs={{0,10},{2,4},{4,2},{6,12},{8,14},{10,0},{12,6},{14,8},{16,22},{18,... | collective-permute-start | bytes 98312 | tf_op jit(solution)/shard_map/ppermute | solution.py:219
  30.8 0.0 collective-permute-done.6.b_ref
  30.9 0.6 %copy.5 = f32[64,128]{1,0:T(8,128)} copy(f32[64,128]{1,0:T(8,128)S(1)} %shard_map.54) | data formatting | bytes 65536
  31.5 2.0 %collective-permute-done.10 = f32[64,128]{1,0:T(8,128)S(1)} collective-permute-done((f32[64,128]{1,0:T(8,128)S(1)}, f32[64,128]{1,0:T(8,128)S(1)}, u32[]{:S(2)}, u32[]{:S(2)}) %collective-permute-start.10) | collective-permute-done | bytes 32800 | tf_op jit(solution)/shard_map/ppermute | solution.py:219
  33.4 0.6 %add.43 = f32[64,128]{1,0:T(8,128)} add(f32[64,128]{1,0:T(8,128)S(1)} %add.42, f32[64,128]{1,0:T(8,128)S(1)} %collective-permute-done.10) | non-fusion elementwise | flops 8192 | bytes 98304 | tf_op jit(solution)/shard_map/add | solution.py:265
  (10 shorter events, 0.1 us)
Async XLA Ops:
  3.2 1.5 %collective-permute-start = (f32[4,64,128]{2,1,0:T(8,128)S(1)}, f32[4,64,128]{2,1,0:T(8,128)S(1)}, u32[]{:S(2)}, u32[]{:S(2)}) collective-permute-start(f32[4,64,128]{2,1,0:T(8,128)S(1)} %get-tuple-element.14), channel_id=1, source_target_pairs={{0,2},{2,0},{4,6},{6,4},{8,10},{10,8},{12,14},{14,12},{16,18},{18,... | collective-permute-start | bytes 393224 | tf_op jit(solution)/shard_map/ppermute | solution.py:219
  5.3 3.7 %collective-permute-start.1 = (f32[4,64,128]{2,1,0:T(8,128)S(1)}, f32[4,64,128]{2,1,0:T(8,128)S(1)}, u32[]{:S(2)}, u32[]{:S(2)}) collective-permute-start(f32[4,64,128]{2,1,0:T(8,128)S(1)} %shard_map.52), channel_id=1, source_target_pairs={{0,2},{2,0},{4,6},{6,4},{8,10},{10,8},{12,14},{14,12},{16,18},{18,... | collective-permute-start | bytes 393224 | tf_op jit(solution)/shard_map/ppermute | solution.py:219
  5.7 4.6 %collective-permute-start.2 = (f32[2,64,128]{2,1,0:T(8,128)S(1)}, f32[2,64,128]{2,1,0:T(8,128)S(1)}, u32[]{:S(2)}, u32[]{:S(2)}) collective-permute-start(f32[2,64,128]{2,1,0:T(8,128)S(1)} %get-tuple-element.23), channel_id=1, source_target_pairs={{0,6},{2,8},{4,14},{6,0},{8,2},{10,12},{12,10},{14,4},{16,26},{18,... | collective-permute-start | bytes 196616 | tf_op jit(solution)/shard_map/ppermute | solution.py:219
  8.4 4.2 %collective-permute-start.3 = (f32[2,64,128]{2,1,0:T(8,128)S(1)}, f32[2,64,128]{2,1,0:T(8,128)S(1)}, u32[]{:S(2)}, u32[]{:S(2)}) collective-permute-start(f32[2,64,128]{2,1,0:T(8,128)S(1)} %get-tuple-element.22), channel_id=1, source_target_pairs={{0,6},{2,8},{4,14},{6,0},{8,2},{10,12},{12,10},{14,4},{16,26},{18,... | collective-permute-start | bytes 196616 | tf_op jit(solution)/shard_map/ppermute | solution.py:219
  10.4 4.1 %collective-permute-start.4 = (f32[2,64,128]{2,1,0:T(8,128)S(1)}, f32[2,64,128]{2,1,0:T(8,128)S(1)}, u32[]{:S(2)}, u32[]{:S(2)}) collective-permute-start(f32[2,64,128]{2,1,0:T(8,128)S(1)} %get-tuple-element.19), channel_id=1, source_target_pairs={{0,10},{2,4},{4,2},{6,12},{8,14},{10,0},{12,6},{14,8},{16,22},{18,... | collective-permute-start | bytes 196616 | tf_op jit(solution)/shard_map/ppermute | solution.py:219
  14.5 6.5 %collective-permute-start.5 = (f32[2,64,128]{2,1,0:T(8,128)S(1)}, f32[2,64,128]{2,1,0:T(8,128)S(1)}, u32[]{:S(2)}, u32[]{:S(2)}) collective-permute-start(f32[2,64,128]{2,1,0:T(8,128)S(1)} %add_add_fusion), channel_id=1, source_target_pairs={{0,18},{2,16},{4,22},{6,20},{8,26},{10,24},{12,30},{14,28},{16,2},... | collective-permute-start | bytes 196616 | tf_op jit(solution)/shard_map/ppermute | solution.py:219
  21.0 4.2 %collective-permute-start.7 = (f32[2,64,128]{2,1,0:T(8,128)S(1)}, f32[2,64,128]{2,1,0:T(8,128)S(1)}, u32[]{:S(2)}, u32[]{:S(2)}) collective-permute-start(f32[2,64,128]{2,1,0:T(8,128)S(1)} %pad_maximum_fusion.a_ref), channel_id=1, source_target_pairs={{0,3},{1,2},{2,1},{3,0},{4,7},{5,6},{6,5},{7,4},{8,11},{9,10},{10,... | collective-permute-start | bytes 196616 | tf_op jit(solution)/shard_map/ppermute | solution.py:260
  25.5 1.3 %collective-permute-start.8 = (f32[64,128]{1,0:T(8,128)S(1)}, f32[64,128]{1,0:T(8,128)S(1)}, u32[]{:S(2)}, u32[]{:S(2)}) collective-permute-start(f32[64,128]{1,0:T(8,128)S(1)} %shard_map.56), channel_id=1, source_target_pairs={{0,2},{2,0},{4,6},{6,4},{8,10},{10,8},{12,14},{14,12},{16,18},{18,... | collective-permute-start | bytes 98312 | tf_op jit(solution)/shard_map/ppermute | solution.py:219
  26.8 3.3 %collective-permute-start.9 = (f32[64,128]{1,0:T(8,128)S(1)}, f32[64,128]{1,0:T(8,128)S(1)}, u32[]{:S(2)}, u32[]{:S(2)}) collective-permute-start(f32[64,128]{1,0:T(8,128)S(1)} %add.41), channel_id=1, source_target_pairs={{0,6},{2,8},{4,14},{6,0},{8,2},{10,12},{12,10},{14,4},{16,26},{18,... | collective-permute-start | bytes 98312 | tf_op jit(solution)/shard_map/ppermute | solution.py:219
  27.7 3.2 %collective-permute-start.6 = (f32[64,128]{1,0:T(8,128)S(1)}, f32[64,128]{1,0:T(8,128)S(1)}, u32[]{:S(2)}, u32[]{:S(2)}) collective-permute-start(f32[64,128]{1,0:T(8,128)S(1)} %bitcast.3), channel_id=1, source_target_pairs={{0,2},{2,0},{4,6},{6,4},{8,10},{10,8},{12,14},{14,12},{16,18},{18,... | collective-permute-start | bytes 98312 | tf_op jit(solution)/shard_map/ppermute | solution.py:219
  30.1 3.3 %collective-permute-start.10 = (f32[64,128]{1,0:T(8,128)S(1)}, f32[64,128]{1,0:T(8,128)S(1)}, u32[]{:S(2)}, u32[]{:S(2)}) collective-permute-start(f32[64,128]{1,0:T(8,128)S(1)} %add.42), channel_id=1, source_target_pairs={{0,10},{2,4},{4,2},{6,12},{8,14},{10,0},{12,6},{14,8},{16,22},{18,... | collective-permute-start | bytes 98312 | tf_op jit(solution)/shard_map/ppermute | solution.py:219

commit v9 on v8

--- a/solution.py
+++ b/solution.py
@@ -73,7 +73,7 @@
                 t_ref[a, :] = value
         return 0
 
-    lax.fori_loop(0, WIDE // 8, butterfly, 0, unroll=4)
+    lax.fori_loop(0, WIDE // 8, butterfly, 0, unroll=16)
 
 
 def step_of(k, odd):
@@ -93,7 +93,7 @@
     odd = c0
     for k in range(bits):
         odd = odd ^ ((me >> k) & 1)
-    origin = me ^ (lax.axis_index("col") & 1) ^ c0 ^ (c1 * step_of(1, odd))
+    origin = me ^ c0 ^ (c1 * step_of(1, odd))
 
     def gather(i):
         dest = origin
@@ -205,13 +205,6 @@
         o_ref[...] = both * (1.0 / everything)
 
     return on_chip(kernel, (columns, 2 * columns), own, full, other)
-
-
-def choose(mine, traded):
-    def kernel(a_ref, b_ref, o_ref):
-        o_ref[...] = jnp.where(lax.axis_index("col") & 1 == 0, a_ref[...], b_ref[...])
-
-    return on_chip(kernel, mine.shape, mine, traded)
 
 
 def swap(value, k):
@@ -256,14 +249,13 @@
     theirs = total[1] + moved[0]
     full = jnp.concatenate([mine[None], theirs[None]], axis=0)
     size = lax.axis_size("col")
-    around = [(r * size + c, (r ^ 1) * size + (c ^ 1)) for r in range(devices) for c in range(size)]
+    around = [(r * size + c, r * size + (c ^ 1)) for r in range(devices) for c in range(size)]
     other = lax.ppermute(full, ("row", "col"), around)
-    traded = swap(mine, 0)
     own = square(full)
     gram = products(own, full, other, everything)
     for k in range(bits - 1):
-        gram = gram + swap(gram, k)
-    sketch = choose(mine, traded)
+        gram = gram + lax.ppermute(gram, "row", [(i, i ^ step_of(k, 0)) for i in range(devices)])
+    sketch = mine
     return (sketch, gram)
 
 

time: 34.2 us -> 34.4 us (level)
  waiting for transfers between devices: 15.7 us -> 18.7 us
  starting transfers between devices: 11.7 us -> 9.54 us
  local copies, waits for them, and re-layouts: 0.63 us -> 0.02 us
    ppermute x0 -> x3, waiting for transfers between devices: none -> 6.91 us  [body(): lax.ppermute(gram, 'row', [(i, i ^ step_of(k, 0)) for i in range(devices)])]
    ppermute x10 -> x6, waiting for transfers between devices: 13.1 us -> 7.76 us  [swap(): lax.ppermute(value, 'row', [(i, i ^ (step_of(k, i.bit_count() & 1) if k e...]
    ppermute x10 -> x6, starting transfers between devices: 10.4 us -> 8.43 us  [swap(): lax.ppermute(value, 'row', [(i, i ^ (step_of(k, i.bit_count() & 1) if k e...]
    ppermute x1, waiting for transfers between devices: 2.62 us -> 4.02 us  [body(): other = lax.ppermute(full, ('row', 'col'), around)]
    ppermute x1, starting transfers between devices: 1.31 us -> 0.07 us  [body(): other = lax.ppermute(full, ('row', 'col'), around)]
    ppermute x0 -> x3, starting transfers between devices: none -> 1.04 us  [body(): lax.ppermute(gram, 'row', [(i, i ^ step_of(k, 0)) for i in range(devices)])]
    unnamed x1 -> x2, local copies, waits for them, and re-layouts: 0.62 us -> 0.01 us
  transfers between devices with their start and end apart: 11 -> 10, of which waited for: 8 -> 8; matrix products, arithmetic and copies ran while one was open for 2% -> 0% of each run, Pallas kernels for 3% -> 3%
where the time goes in v9:
time: 34.4 us; the launch traced here: 34.2 us
  waiting for transfers between devices  18.7 us (54%)
  starting transfers between devices  9.54 us (28%)
  Pallas kernels  4.54 us (13%)
  between operations  0.72 us (2%)
  other arithmetic  0.71 us (2%)
    ppermute x6, starting transfers between devices, swap(): lax.ppermute(value, 'row', [(i, i ^ (step_of(k, i.bit_count() & 1) if k e...  8.43 us
    ppermute x6, waiting for transfers between devices, swap(): lax.ppermute(value, 'row', [(i, i ^ (step_of(k, i.bit_count() & 1) if k e...  7.76 us
    ppermute x3, waiting for transfers between devices, body(): lax.ppermute(gram, 'row', [(i, i ^ step_of(k, 0)) for i in range(devices)])  6.91 us
    ppermute x1, waiting for transfers between devices, body(): other = lax.ppermute(full, ('row', 'col'), around)  4.02 us
    pallas_call x1, Pallas kernels, mix(): pl.pallas_call(kernel, out_shape=(pltpu.VMEM((length // 2, LANES), jnp.fl...  2.57 us
    pallas_call x3, Pallas kernels, pick(): pl.pallas_call(kernel, out_shape=pltpu.VMEM((devices // 4, columns, per),...  1.45 us
    ppermute x3, starting transfers between devices, body(): lax.ppermute(gram, 'row', [(i, i ^ step_of(k, 0)) for i in range(devices)])  1.04 us
  transfers between devices with their start and end apart: 10, of which 8 were waited for; matrix products, arithmetic and copies ran while one was open for 0% of the time, Pallas kernels for 3%

profile of v9, /device:TPU:0, one launch (start us, length us, event | category | flops | bytes accessed | tf_op | source)
XLA Modules:
  0.0 34.2 jit_solution(15151298415939102789)
XLA Ops:
  0.6 2.6 %shard_map.50 = (f32[4096,128]{1,0:T(8,128)S(1)}, f32[4,64,128]{2,1,0:T(8,128)S(1)}, s32[16,128]{1,0:T(8,128)S(4)}, s32[16,128]{1,0:T(8,128)S(1)}) custom-call(bf16[64,8192]{1,0:T(8,128)(2,1)} %x_hbm.1, s32[64,128]{1,0:T(8,128)} %bitcast.4, s32[16,128]{1,0:T(8,128)} %bitcast.5), custom_call_target="tpu_custom_call" | custom-call | tf_op jit(solution)/shard_map/pallas_call | solution.py:138
  3.2 0.6 %collective-permute-start = (f32[4,64,128]{2,1,0:T(8,128)S(1)}, f32[4,64,128]{2,1,0:T(8,128)S(1)}, u32[]{:S(2)}, u32[]{:S(2)}) collective-permute-start(f32[4,64,128]{2,1,0:T(8,128)S(1)} %get-tuple-element.14), channel_id=1, source_target_pairs={{0,2},{2,0},{4,6},{6,4},{8,10},{10,8},{12,14},{14,12},{16,18},{18,... | collective-permute-start | bytes 393224 | tf_op jit(solution)/shard_map/ppermute | solution.py:212
  3.8 0.5 %shard_map.51 = f32[4,64,128]{2,1,0:T(8,128)S(1)} custom-call(f32[4096,128]{1,0:T(8,128)S(1)} %get-tuple-element.16.t_ref, s32[16,128]{1,0:T(8,128)S(4)} %get-tuple-element.12.flat_ref, s32[16,128]{1,0:T(8,128)S(1)} %get-tuple-element.13.rows_ref), custom_call_target="tpu_custom_call" | custom-call | tf_op jit(solution)/shard_map/pallas_call | solution.py:167
  4.2 0.5 %collective-permute-done = f32[4,64,128]{2,1,0:T(8,128)S(1)} collective-permute-done((f32[4,64,128]{2,1,0:T(8,128)S(1)}, f32[4,64,128]{2,1,0:T(8,128)S(1)}, u32[]{:S(2)}, u32[]{:S(2)}) %collective-permute-start) | collective-permute-done | bytes 131104 | tf_op jit(solution)/shard_map/ppermute | solution.py:212
  4.8 0.5 %shard_map.52 = f32[4,64,128]{2,1,0:T(8,128)S(1)} custom-call(f32[4096,128]{1,0:T(8,128)S(1)} %get-tuple-element.16.t_ref, s32[16,128]{1,0:T(8,128)S(4)} %get-tuple-element.12.flat_ref, s32[16,128]{1,0:T(8,128)S(1)} %get-tuple-element.13.rows_ref), custom_call_target="tpu_custom_call" | custom-call | tf_op jit(solution)/shard_map/pallas_call | solution.py:167
  5.3 0.4 %collective-permute-start.1 = (f32[4,64,128]{2,1,0:T(8,128)S(1)}, f32[4,64,128]{2,1,0:T(8,128)S(1)}, u32[]{:S(2)}, u32[]{:S(2)}) collective-permute-start(f32[4,64,128]{2,1,0:T(8,128)S(1)} %shard_map.52), channel_id=1, source_target_pairs={{0,2},{2,0},{4,6},{6,4},{8,10},{10,8},{12,14},{14,12},{16,18},{18,... | collective-permute-start | bytes 393224 | tf_op jit(solution)/shard_map/ppermute | solution.py:212
  5.7 2.7 %collective-permute-start.2 = (f32[2,64,128]{2,1,0:T(8,128)S(1)}, f32[2,64,128]{2,1,0:T(8,128)S(1)}, u32[]{:S(2)}, u32[]{:S(2)}) collective-permute-start(f32[2,64,128]{2,1,0:T(8,128)S(1)} %get-tuple-element.23), channel_id=1, source_target_pairs={{0,6},{2,8},{4,14},{6,0},{8,2},{10,12},{12,10},{14,4},{16,26},{18,... | collective-permute-start | bytes 196616 | tf_op jit(solution)/shard_map/ppermute | solution.py:212
  8.4 0.1 collective-permute-start.3
  8.4 0.5 %shard_map.53 = f32[4,64,128]{2,1,0:T(8,128)S(1)} custom-call(f32[4096,128]{1,0:T(8,128)S(1)} %get-tuple-element.16.t_ref, s32[16,128]{1,0:T(8,128)S(4)} %get-tuple-element.12.flat_ref, s32[16,128]{1,0:T(8,128)S(1)} %get-tuple-element.13.rows_ref), custom_call_target="tpu_custom_call" | custom-call | tf_op jit(solution)/shard_map/pallas_call | solution.py:167
  8.9 0.0 collective-permute-done.1
  9.0 1.4 %collective-permute-done.2 = f32[2,64,128]{2,1,0:T(8,128)S(1)} collective-permute-done((f32[2,64,128]{2,1,0:T(8,128)S(1)}, f32[2,64,128]{2,1,0:T(8,128)S(1)}, u32[]{:S(2)}, u32[]{:S(2)}) %collective-permute-start.2) | collective-permute-done | bytes 65568 | tf_op jit(solution)/shard_map/ppermute | solution.py:212
  10.3 2.2 %collective-permute-start.4 = (f32[2,64,128]{2,1,0:T(8,128)S(1)}, f32[2,64,128]{2,1,0:T(8,128)S(1)}, u32[]{:S(2)}, u32[]{:S(2)}) collective-permute-start(f32[2,64,128]{2,1,0:T(8,128)S(1)} %get-tuple-element.19), channel_id=1, source_target_pairs={{0,10},{2,4},{4,2},{6,12},{8,14},{10,0},{12,6},{14,8},{16,22},{18,... | collective-permute-start | bytes 196616 | tf_op jit(solution)/shard_map/ppermute | solution.py:212
  12.5 0.0 collective-permute-done.3
  12.5 1.9 %collective-permute-done.4 = f32[2,64,128]{2,1,0:T(8,128)S(1)} collective-permute-done((f32[2,64,128]{2,1,0:T(8,128)S(1)}, f32[2,64,128]{2,1,0:T(8,128)S(1)}, u32[]{:S(2)}, u32[]{:S(2)}) %collective-permute-start.4) | collective-permute-done | bytes 65568 | tf_op jit(solution)/shard_map/ppermute | solution.py:212
  14.5 2.5 %collective-permute-start.5 = (f32[2,64,128]{2,1,0:T(8,128)S(1)}, f32[2,64,128]{2,1,0:T(8,128)S(1)}, u32[]{:S(2)}, u32[]{:S(2)}) collective-permute-start(f32[2,64,128]{2,1,0:T(8,128)S(1)} %add_add_fusion), channel_id=1, source_target_pairs={{0,18},{2,16},{4,22},{6,20},{8,26},{10,24},{12,30},{14,28},{16,2},... | collective-permute-start | bytes 196616 | tf_op jit(solution)/shard_map/ppermute | solution.py:212
  17.0 3.9 %collective-permute-done.5 = f32[2,64,128]{2,1,0:T(8,128)S(1)} collective-permute-done((f32[2,64,128]{2,1,0:T(8,128)S(1)}, f32[2,64,128]{2,1,0:T(8,128)S(1)}, u32[]{:S(2)}, u32[]{:S(2)}) %collective-permute-start.5) | collective-permute-done | bytes 65568 | tf_op jit(solution)/shard_map/ppermute | solution.py:212
  21.0 0.0 copy-start
  21.0 0.1 collective-permute-start.6
  21.1 0.2 shard_map.54.own_ref
  21.3 4.0 %collective-permute-done.6.b_ref = f32[2,64,128]{2,1,0:T(8,128)S(1)} collective-permute-done((f32[2,64,128]{2,1,0:T(8,128)S(1)}, f32[2,64,128]{2,1,0:T(8,128)S(1)}, u32[]{:S(2)}, u32[]{:S(2)}) %collective-permute-start.6) | collective-permute-done | bytes 65568 | tf_op jit(solution)/shard_map/ppermute | solution.py:253
  25.3 0.3 shard_map.55
  25.6 0.1 collective-permute-start.7
  25.7 1.2 %collective-permute-done.7 = f32[64,128]{1,0:T(8,128)S(1)} collective-permute-done((f32[64,128]{1,0:T(8,128)S(1)}, f32[64,128]{1,0:T(8,128)S(1)}, u32[]{:S(2)}, u32[]{:S(2)}) %collective-permute-start.7) | collective-permute-done | bytes 32800 | tf_op jit(solution)/shard_map/ppermute | solution.py:257
  26.9 0.3 collective-permute-start.8
  27.2 3.0 %collective-permute-done.8 = f32[64,128]{1,0:T(8,128)S(1)} collective-permute-done((f32[64,128]{1,0:T(8,128)S(1)}, f32[64,128]{1,0:T(8,128)S(1)}, u32[]{:S(2)}, u32[]{:S(2)}) %collective-permute-start.8) | collective-permute-done | bytes 32800 | tf_op jit(solution)/shard_map/ppermute | solution.py:257
  30.3 0.7 %collective-permute-start.9 = (f32[64,128]{1,0:T(8,128)S(1)}, f32[64,128]{1,0:T(8,128)S(1)}, u32[]{:S(2)}, u32[]{:S(2)}) collective-permute-start(f32[64,128]{1,0:T(8,128)S(1)} %add.44), channel_id=1, source_target_pairs={{0,10},{2,8},{4,14},{6,12},{8,2},{10,0},{12,6},{14,4},{16,26},{18,... | collective-permute-start | bytes 98312 | tf_op jit(solution)/shard_map/ppermute | solution.py:257
  30.9 2.7 %collective-permute-done.9 = f32[64,128]{1,0:T(8,128)S(1)} collective-permute-done((f32[64,128]{1,0:T(8,128)S(1)}, f32[64,128]{1,0:T(8,128)S(1)}, u32[]{:S(2)}, u32[]{:S(2)}) %collective-permute-start.9) | collective-permute-done | bytes 32800 | tf_op jit(solution)/shard_map/ppermute | solution.py:257
  33.6 0.6 %add.45 = f32[64,128]{1,0:T(8,128)} add(f32[64,128]{1,0:T(8,128)S(1)} %add.44, f32[64,128]{1,0:T(8,128)S(1)} %collective-permute-done.9) | non-fusion elementwise | flops 8192 | bytes 98304 | tf_op jit(solution)/shard_map/add | solution.py:257
  34.2 0.0 copy-done
  (9 shorter events, 0.1 us)
Async XLA Ops:
  3.2 1.5 %collective-permute-start = (f32[4,64,128]{2,1,0:T(8,128)S(1)}, f32[4,64,128]{2,1,0:T(8,128)S(1)}, u32[]{:S(2)}, u32[]{:S(2)}) collective-permute-start(f32[4,64,128]{2,1,0:T(8,128)S(1)} %get-tuple-element.14), channel_id=1, source_target_pairs={{0,2},{2,0},{4,6},{6,4},{8,10},{10,8},{12,14},{14,12},{16,18},{18,... | collective-permute-start | bytes 393224 | tf_op jit(solution)/shard_map/ppermute | solution.py:212
  5.3 3.7 %collective-permute-start.1 = (f32[4,64,128]{2,1,0:T(8,128)S(1)}, f32[4,64,128]{2,1,0:T(8,128)S(1)}, u32[]{:S(2)}, u32[]{:S(2)}) collective-permute-start(f32[4,64,128]{2,1,0:T(8,128)S(1)} %shard_map.52), channel_id=1, source_target_pairs={{0,2},{2,0},{4,6},{6,4},{8,10},{10,8},{12,14},{14,12},{16,18},{18,... | collective-permute-start | bytes 393224 | tf_op jit(solution)/shard_map/ppermute | solution.py:212
  5.7 4.6 %collective-permute-start.2 = (f32[2,64,128]{2,1,0:T(8,128)S(1)}, f32[2,64,128]{2,1,0:T(8,128)S(1)}, u32[]{:S(2)}, u32[]{:S(2)}) collective-permute-start(f32[2,64,128]{2,1,0:T(8,128)S(1)} %get-tuple-element.23), channel_id=1, source_target_pairs={{0,6},{2,8},{4,14},{6,0},{8,2},{10,12},{12,10},{14,4},{16,26},{18,... | collective-permute-start | bytes 196616 | tf_op jit(solution)/shard_map/ppermute | solution.py:212
  8.4 4.2 %collective-permute-start.3 = (f32[2,64,128]{2,1,0:T(8,128)S(1)}, f32[2,64,128]{2,1,0:T(8,128)S(1)}, u32[]{:S(2)}, u32[]{:S(2)}) collective-permute-start(f32[2,64,128]{2,1,0:T(8,128)S(1)} %get-tuple-element.22), channel_id=1, source_target_pairs={{0,6},{2,8},{4,14},{6,0},{8,2},{10,12},{12,10},{14,4},{16,26},{18,... | collective-permute-start | bytes 196616 | tf_op jit(solution)/shard_map/ppermute | solution.py:212
  10.3 4.1 %collective-permute-start.4 = (f32[2,64,128]{2,1,0:T(8,128)S(1)}, f32[2,64,128]{2,1,0:T(8,128)S(1)}, u32[]{:S(2)}, u32[]{:S(2)}) collective-permute-start(f32[2,64,128]{2,1,0:T(8,128)S(1)} %get-tuple-element.19), channel_id=1, source_target_pairs={{0,10},{2,4},{4,2},{6,12},{8,14},{10,0},{12,6},{14,8},{16,22},{18,... | collective-permute-start | bytes 196616 | tf_op jit(solution)/shard_map/ppermute | solution.py:212
  14.5 6.5 %collective-permute-start.5 = (f32[2,64,128]{2,1,0:T(8,128)S(1)}, f32[2,64,128]{2,1,0:T(8,128)S(1)}, u32[]{:S(2)}, u32[]{:S(2)}) collective-permute-start(f32[2,64,128]{2,1,0:T(8,128)S(1)} %add_add_fusion), channel_id=1, source_target_pairs={{0,18},{2,16},{4,22},{6,20},{8,26},{10,24},{12,30},{14,28},{16,2},... | collective-permute-start | bytes 196616 | tf_op jit(solution)/shard_map/ppermute | solution.py:212
  21.0 13.3 %copy-start = (f32[1,64,128]{2,1,0:T(8,128)}, f32[1,64,128]{2,1,0:T(8,128)S(1)}, u32[]{:S(2)}) copy-start(f32[1,64,128]{2,1,0:T(8,128)S(1)} %get-tuple-element.21) | copy-start | bytes 98308
  21.0 4.3 %collective-permute-start.6 = (f32[2,64,128]{2,1,0:T(8,128)S(1)}, f32[2,64,128]{2,1,0:T(8,128)S(1)}, u32[]{:S(2)}, u32[]{:S(2)}) collective-permute-start(f32[2,64,128]{2,1,0:T(8,128)S(1)} %pad_maximum_fusion.a_ref), channel_id=1, source_target_pairs={{0,1},{1,0},{2,3},{3,2},{4,5},{5,4},{6,7},{7,6},{8,9},{9,8},{10,11... | collective-permute-start | bytes 196616 | tf_op jit(solution)/shard_map/ppermute | solution.py:253
  25.6 1.3 %collective-permute-start.7 = (f32[64,128]{1,0:T(8,128)S(1)}, f32[64,128]{1,0:T(8,128)S(1)}, u32[]{:S(2)}, u32[]{:S(2)}) collective-permute-start(f32[64,128]{1,0:T(8,128)S(1)} %shard_map.55), channel_id=1, source_target_pairs={{0,2},{2,0},{4,6},{6,4},{8,10},{10,8},{12,14},{14,12},{16,18},{18,... | collective-permute-start | bytes 98312 | tf_op jit(solution)/shard_map/ppermute | solution.py:257
  26.9 3.3 %collective-permute-start.8 = (f32[64,128]{1,0:T(8,128)S(1)}, f32[64,128]{1,0:T(8,128)S(1)}, u32[]{:S(2)}, u32[]{:S(2)}) collective-permute-start(f32[64,128]{1,0:T(8,128)S(1)} %add.43), channel_id=1, source_target_pairs={{0,6},{2,4},{4,2},{6,0},{8,14},{10,12},{12,10},{14,8},{16,22},{18,... | collective-permute-start | bytes 98312 | tf_op jit(solution)/shard_map/ppermute | solution.py:257
  30.3 3.3 %collective-permute-start.9 = (f32[64,128]{1,0:T(8,128)S(1)}, f32[64,128]{1,0:T(8,128)S(1)}, u32[]{:S(2)}, u32[]{:S(2)}) collective-permute-start(f32[64,128]{1,0:T(8,128)S(1)} %add.44), channel_id=1, source_target_pairs={{0,10},{2,8},{4,14},{6,12},{8,2},{10,0},{12,6},{14,4},{16,26},{18,... | collective-permute-start | bytes 98312 | tf_op jit(solution)/shard_map/ppermute | solution.py:257
